TPU v7x, 32 devices: a whole 2x2x4 slice. The times are simulated.
32 devices in a mesh: dp: 8 (over z, y), fsdp: 4 (over x, core).
Axes of the slice: x: 2, y: 2, z: 4, core: 2. Of those that a mesh axis runs over, the one named last changes fastest.
Arguments:
- tokens: bfloat16 [16, 256, 2048], P(None, ('dp', 'fsdp')), may hold values from -6 to 6
- cotangent: bfloat16 [16, 256, 2048], P(None, ('dp', 'fsdp')), may hold values from -6 to 6
- lengths: int32 [16], replicated, may hold values from 1 to 256, 3072 in all
- order: int32 [16], replicated, may hold values from 0 to 15, each once
- routes: int32 [16, 256, 4], replicated, may hold values from 0 to 7, all different within a row
- norm_attn: bfloat16 [2048], P(('dp', 'fsdp')), may hold values from 0.5 to 1.5
- q_weight: bfloat16 [2048, 2048], P(('dp', 'fsdp')), may hold values from -0.125 to 0.125
- k_weight: bfloat16 [2048, 2048], P(('dp', 'fsdp')), may hold values from -0.125 to 0.125
- v_weight: bfloat16 [2048, 2048], P(('dp', 'fsdp')), may hold values from -0.125 to 0.125
- q_bias: bfloat16 [2048], P(('dp', 'fsdp')), may hold values from -3 to 3
- k_bias: bfloat16 [2048], P(('dp', 'fsdp')), may hold values from -3 to 3
- v_bias: bfloat16 [2048], P(('dp', 'fsdp')), may hold values from -3 to 3
- o_weight: bfloat16 [2048, 2048], P(('dp', 'fsdp')), may hold values from -0.75 to 0.75
- norm_moe: bfloat16 [2048], P(('dp', 'fsdp')), may hold values from 0.5 to 1.5
- router: bfloat16 [2048, 8], P(('dp', 'fsdp')), may hold values from -0.0625 to 0.0625
- shared_gate: bfloat16 [2048], P(('dp', 'fsdp')), may hold values from -0.125 to 0.125
- shared_gate_up: bfloat16 [2048, 11264], P(('dp', 'fsdp')), may hold values from -0.125 to 0.125
- shared_down: bfloat16 [5632, 2048], P(('dp', 'fsdp')), may hold values from -0.15625 to 0.15625
- expert_gate_up: bfloat16 [8, 2048, 2816], P('dp', 'fsdp'), may hold values from -0.125 to 0.125
- expert_down: bfloat16 [8, 1408, 2048], P('dp', 'fsdp'), may hold values from -0.875 to 0.875
Outputs:
- mixed: bfloat16 [16, 256, 2048], P(None, ('dp', 'fsdp'))
- grad_tokens: bfloat16 [16, 256, 2048], P(None, ('dp', 'fsdp'))
- grad_norm_attn: float32 [2048], P(('dp', 'fsdp'))
- grad_q_weight: float32 [2048, 2048], P(('dp', 'fsdp'))
- grad_k_weight: float32 [2048, 2048], P(('dp', 'fsdp'))
- grad_v_weight: float32 [2048, 2048], P(('dp', 'fsdp'))
- grad_q_bias: float32 [2048], P(('dp', 'fsdp'))
- grad_k_bias: float32 [2048], P(('dp', 'fsdp'))
- grad_v_bias: float32 [2048], P(('dp', 'fsdp'))
- grad_o_weight: float32 [2048, 2048], P(('dp', 'fsdp'))
- grad_norm_moe: float32 [2048], P(('dp', 'fsdp'))
- grad_router: float32 [2048, 8], P(('dp', 'fsdp'))
- grad_shared_gate: float32 [2048], P(('dp', 'fsdp'))
- grad_shared_gate_up: float32 [2048, 11264], P(('dp', 'fsdp'))
- grad_shared_down: float32 [5632, 2048], P(('dp', 'fsdp'))
- grad_expert_gate_up: float32 [8, 2048, 2816], P('dp', 'fsdp')
- grad_expert_down: float32 [8, 1408, 2048], P('dp', 'fsdp')
Inputs may be any that keep to these rules, and one draw needn't show every extreme that they name: `lengths`: some sequence is exactly 256 long. `order`: each sequence number once. `routes`: the 4 experts of a token differ.
All inputs are finite; a program needn't handle non-finite values.
Results may differ from a plain program's by a relative error of at most 0.03.
Values may be sent and summed in bfloat16 or wider, within the bound.
No kernel may reach another device: no remote copies, remote signals or barrier semaphores. Data moves between devices by JAX's collectives and lax.ppermute only.
A program may use at most 448 MiB of HBM per device.

v0:
```python
import math

import jax
import jax.numpy as jnp
from jax import lax
from jax.sharding import PartitionSpec as P

HEAD = 128
EFF = 1408
SFF = 5632
TOP = 4


epsilon = 1e-06
rope_base = 1000000.0
negative = -1e30


def dense_product(matrix, operand):
    return jnp.dot(matrix, operand, preferred_element_type=jnp.float32)


def transposed_product(matrix, operand):
    return lax.dot_general(
        matrix, operand, (((0,), (0,)), ((), ())), preferred_element_type=jnp.float32
    )


def product_back(matrix, operand):
    return lax.dot_general(
        matrix, operand, (((1,), (1,)), ((), ())), preferred_element_type=jnp.float32
    )


def rotary_tables(positions):
    freq_index = jnp.arange(HEAD // 2).astype(jnp.float32)
    inverse = jnp.exp(freq_index * (-2.0 * math.log(rope_base) / HEAD))
    angles = positions.astype(jnp.float32)[:, None] * inverse[None, :]
    cosine = jnp.concatenate([jnp.cos(angles), jnp.cos(angles)], axis=-1)
    sine_table = jnp.concatenate([jnp.sin(angles), jnp.sin(angles)], axis=-1)
    return (cosine, sine_table)


def rotate(values, cosine, sine_table):
    half_width = values.shape[-1] // 2
    turned = jnp.concatenate([-values[..., half_width:], values[..., :half_width]], axis=-1)
    return values * cosine[:, None, :] + turned * sine_table[:, None, :]


def rotate_back(grads_in, cosine, sine_table):
    half_width = grads_in.shape[-1] // 2
    scaled = grads_in * sine_table[:, None, :]
    turned = jnp.concatenate([scaled[..., half_width:], -scaled[..., :half_width]], axis=-1)
    return grads_in * cosine[:, None, :] + turned


def normalize(values):
    factor = lax.rsqrt(jnp.mean(values * values, axis=-1, keepdims=True) + epsilon)
    return (values * factor, factor)


def norm_back(grad_normed, normal, factor, gain_vector):
    scaled = grad_normed * gain_vector
    grad_input = factor * (scaled - normal * jnp.mean(scaled * normal, axis=-1, keepdims=True))
    return (grad_input, jnp.sum(grad_normed * normal, axis=0))


def swiglu(joined, hidden_width):
    return jax.nn.silu(joined[:, :hidden_width]) * joined[:, hidden_width:]


def swiglu_back(joined, grad_hidden, hidden_width):
    gate_part = joined[:, :hidden_width]
    up_part = joined[:, hidden_width:]
    sigmoid_gate = jax.nn.sigmoid(gate_part)
    grad_gate = grad_hidden * up_part * sigmoid_gate * (1.0 + gate_part * (1.0 - sigmoid_gate))
    grad_up = grad_hidden * gate_part * sigmoid_gate
    return jnp.concatenate([grad_gate, grad_up], axis=1)


def on_device(
    tokens,
    cotangent,
    lengths,
    order,
    routes,
    norm_attn,
    q_weight,
    k_weight,
    v_weight,
    q_bias,
    k_bias,
    v_bias,
    o_weight,
    norm_moe,
    router,
    shared_gate,
    shared_gate_up,
    shared_down,
    expert_gate_up,
    expert_down,
):
    group_count = lax.axis_size("dp")
    column_count = lax.axis_size("fsdp")
    group_index = lax.axis_index("dp")
    column_index = lax.axis_index("fsdp")
    piece_rows = tokens.shape[1]
    model_width = tokens.shape[2]
    per_group = order.shape[0] // group_count
    local_rows = group_count * piece_rows
    token_rows = per_group * local_rows
    expert_count = router.shape[1]
    capacity = (5 * token_rows * TOP + 4 * expert_count - 1) // (4 * expert_count)
    head_count = model_width // HEAD
    score_scale = HEAD ** (-0.5)
    shape_four = (per_group, local_rows, head_count, HEAD)
    my_sequences = lax.dynamic_slice_in_dim(order, group_index * per_group, per_group)
    arrived, arrived_grad = (
        lax.all_to_all(
            jnp.take(tokens, order, axis=0), "dp", split_axis=0, concat_axis=1, tiled=True
        ),
        lax.all_to_all(
            jnp.take(cotangent, order, axis=0), "dp", split_axis=0, concat_axis=1, tiled=True
        ),
    )
    row_index = jnp.arange(local_rows, dtype=jnp.int32)
    positions = (
        row_index // piece_rows * column_count + column_index
    ) * piece_rows + row_index % piece_rows
    key_index = jnp.arange(column_count * local_rows, dtype=jnp.int32)
    key_local = key_index % local_rows
    key_positions = (
        key_local // piece_rows * column_count + key_index // local_rows
    ) * piece_rows + key_local % piece_rows
    seq_lengths = jnp.take(lengths, my_sequences)
    live_mask = (
        (positions[None, :] < seq_lengths[:, None]).astype(jnp.float32).reshape(token_rows, 1)
    )
    causal = key_positions[None, :] <= positions[:, None]
    cosine, sine_table = rotary_tables(positions)
    gathered = (
        lax.all_gather(norm_attn, ("dp", "fsdp"), axis=0, tiled=True),
        lax.all_gather(q_weight, ("dp", "fsdp"), axis=0, tiled=True),
        lax.all_gather(k_weight, ("dp", "fsdp"), axis=0, tiled=True),
        lax.all_gather(v_weight, ("dp", "fsdp"), axis=0, tiled=True),
        lax.all_gather(q_bias, ("dp", "fsdp"), axis=0, tiled=True),
        lax.all_gather(k_bias, ("dp", "fsdp"), axis=0, tiled=True),
        lax.all_gather(v_bias, ("dp", "fsdp"), axis=0, tiled=True),
        lax.all_gather(o_weight, ("dp", "fsdp"), axis=0, tiled=True),
        lax.all_gather(norm_moe, ("dp", "fsdp"), axis=0, tiled=True),
        lax.all_gather(router, ("dp", "fsdp"), axis=0, tiled=True),
        lax.all_gather(shared_gate, ("dp", "fsdp"), axis=0, tiled=True),
        lax.all_gather(shared_gate_up, ("dp", "fsdp"), axis=0, tiled=True),
        lax.all_gather(shared_down, ("dp", "fsdp"), axis=0, tiled=True),
    )
    (
        gain_attn,
        full_query,
        full_key,
        full_value,
        bias_query,
        bias_key,
        bias_value,
        full_output,
        gain_moe,
        full_router,
        full_shared_gate,
        full_shared_gu,
        full_shared_down,
    ) = gathered
    expert_full = (
        lax.all_gather(expert_gate_up, "fsdp", axis=1, tiled=True),
        lax.all_gather(expert_down, "fsdp", axis=1, tiled=True),
    )
    gate_up_full = expert_full[0][0]
    down_full = expert_full[1][0]
    inputs_f32 = arrived.astype(jnp.float32).reshape(token_rows, model_width)
    normal_one, factor_one = normalize(inputs_f32)
    normed_one = (normal_one * gain_attn.astype(jnp.float32)).astype(jnp.bfloat16)
    query_pre = dense_product(normed_one, full_query) + bias_query.astype(jnp.float32)
    key_pre = dense_product(normed_one, full_key) + bias_key.astype(jnp.float32)
    query_rot = rotate(query_pre.reshape(shape_four), cosine, sine_table).astype(jnp.bfloat16)
    key_rot = rotate(key_pre.reshape(shape_four), cosine, sine_table).astype(jnp.bfloat16)
    value_low = (
        (dense_product(normed_one, full_value) + bias_value.astype(jnp.float32))
        .astype(jnp.bfloat16)
        .reshape(shape_four)
    )
    all_keys, all_values = (
        lax.all_gather(key_rot, "fsdp", axis=1, tiled=True),
        lax.all_gather(value_low, "fsdp", axis=1, tiled=True),
    )
    raw_scores = (
        jnp.einsum("sqhd,skhd->shqk", query_rot, all_keys, preferred_element_type=jnp.float32)
        * score_scale
    )
    masked = jnp.where(causal[None, None], raw_scores, negative)
    top_score = jnp.max(masked, axis=-1, keepdims=True)
    log_total = top_score + jnp.log(jnp.sum(jnp.exp(masked - top_score), axis=-1, keepdims=True))
    probs_low = jnp.exp(masked - log_total).astype(jnp.bfloat16)
    combined = jnp.einsum(
        "shqk,skhd->sqhd", probs_low, all_values, preferred_element_type=jnp.float32
    )
    attended = combined.reshape(token_rows, model_width).astype(jnp.bfloat16)
    residual = inputs_f32 + live_mask * dense_product(attended, full_output)
    normal_two, factor_two = normalize(residual)
    normed_two = (normal_two * gain_moe.astype(jnp.float32)).astype(jnp.bfloat16)
    router_probs = jax.nn.softmax(dense_product(normed_two, full_router), axis=-1)
    my_routes = jnp.take(jnp.take(routes, my_sequences, axis=0), positions, axis=1).reshape(
        token_rows, TOP
    )
    chosen = (
        my_routes[:, :, None] == jnp.arange(expert_count, dtype=jnp.int32)[None, None, :]
    ).astype(jnp.float32)
    gates = jnp.sum(chosen * router_probs[:, None, :], axis=2)
    marks = jnp.sum(chosen, axis=1) * live_mask
    token_index = jnp.arange(token_rows, dtype=jnp.int32)
    earlier_mask = (token_index[None, :] < token_index[:, None]).astype(jnp.bfloat16)
    before = dense_product(earlier_mask, marks.astype(jnp.bfloat16))
    places = jnp.sum(chosen * before[:, None, :], axis=2)
    kept = ((places < capacity) & (live_mask > 0.0)).astype(jnp.float32)
    slot_index = jnp.where(
        kept > 0.0, my_routes * capacity + places.astype(jnp.int32), expert_count * capacity
    )
    flat_slots = slot_index.reshape(-1)
    safe_slots = jnp.minimum(flat_slots, expert_count * capacity - 1)
    pair_rows = jnp.broadcast_to(normed_two[:, None, :], (token_rows, TOP, model_width)).reshape(
        -1, model_width
    )
    send_rows = (
        jnp.zeros((expert_count * capacity, model_width), jnp.bfloat16)
        .at[flat_slots]
        .set(pair_rows, mode="drop")
    )
    received = lax.all_to_all(
        send_rows.reshape(expert_count, capacity, model_width),
        "dp",
        split_axis=0,
        concat_axis=0,
        tiled=True,
    )
    expert_rows = received.reshape(-1, model_width)
    expert_joined = dense_product(expert_rows, gate_up_full)
    expert_hidden = swiglu(expert_joined, EFF).astype(jnp.bfloat16)
    expert_out = (
        dense_product(expert_hidden, down_full)
        .astype(jnp.bfloat16)
        .reshape(group_count, capacity, model_width)
    )
    returned = lax.all_to_all(expert_out, "dp", split_axis=0, concat_axis=0, tiled=True)
    returned_rows = (
        jnp.take(returned.reshape(-1, model_width), safe_slots, axis=0)
        .astype(jnp.float32)
        .reshape(token_rows, TOP, model_width)
    )
    weighted = gates * kept
    routed = jnp.sum(weighted[:, :, None] * returned_rows, axis=1)
    shared_joined = dense_product(normed_two, full_shared_gu)
    shared_hidden = swiglu(shared_joined, SFF).astype(jnp.bfloat16)
    shared_out = dense_product(shared_hidden, full_shared_down)
    shared_weight = jax.nn.sigmoid(dense_product(normed_two, full_shared_gate))
    total = residual + live_mask * (shared_weight[:, None] * shared_out + routed)
    output_low = total.astype(jnp.bfloat16).reshape(per_group, local_rows, model_width)
    grad_out = arrived_grad.astype(jnp.float32).reshape(token_rows, model_width)
    branch_grad = live_mask * grad_out
    grad_gates = kept * jnp.sum(branch_grad[:, None, :] * returned_rows, axis=2)
    pair_grads = (
        (weighted[:, :, None] * branch_grad[:, None, :])
        .astype(jnp.bfloat16)
        .reshape(-1, model_width)
    )
    send_grads = (
        jnp.zeros((expert_count * capacity, model_width), jnp.bfloat16)
        .at[flat_slots]
        .set(pair_grads, mode="drop")
    )
    grad_received = lax.all_to_all(
        send_grads.reshape(expert_count, capacity, model_width),
        "dp",
        split_axis=0,
        concat_axis=0,
        tiled=True,
    )
    grad_rows = grad_received.reshape(-1, model_width)
    grad_expert_down = transposed_product(expert_hidden, grad_rows)
    grad_hidden = product_back(grad_rows, down_full)
    grad_joined = swiglu_back(expert_joined, grad_hidden, EFF).astype(jnp.bfloat16)
    grad_expert_gu = transposed_product(expert_rows, grad_joined)
    grad_in_rows = (
        product_back(grad_joined, gate_up_full)
        .astype(jnp.bfloat16)
        .reshape(group_count, capacity, model_width)
    )
    expert_grads = (
        lax.psum_scatter(
            grad_expert_gu[None].astype(jnp.bfloat16), "fsdp", scatter_dimension=1, tiled=True
        ).astype(jnp.float32),
        lax.psum_scatter(
            grad_expert_down[None].astype(jnp.bfloat16), "fsdp", scatter_dimension=1, tiled=True
        ).astype(jnp.float32),
    )
    grad_back = lax.all_to_all(grad_in_rows, "dp", split_axis=0, concat_axis=0, tiled=True)
    grad_pairs = (
        jnp.take(grad_back.reshape(-1, model_width), safe_slots, axis=0)
        .astype(jnp.float32)
        .reshape(token_rows, TOP, model_width)
    )
    grad_normed = jnp.sum(kept[:, :, None] * grad_pairs, axis=1)
    shared_grad = (branch_grad * shared_weight[:, None]).astype(jnp.bfloat16)
    shared_logit_grad = (
        jnp.sum(branch_grad * shared_out, axis=1) * shared_weight * (1.0 - shared_weight)
    )
    grad_shared_down = transposed_product(shared_hidden, shared_grad)
    grad_shared_hidden = product_back(shared_grad, full_shared_down)
    shared_joined_grad = swiglu_back(shared_joined, grad_shared_hidden, SFF).astype(jnp.bfloat16)
    grad_shared_gu = transposed_product(normed_two, shared_joined_grad)
    grad_shared_gate = jnp.dot(
        shared_logit_grad, normed_two.astype(jnp.float32), precision=lax.Precision.HIGHEST
    )
    moe_grads = (
        lax.psum_scatter(grad_shared_gu, ("dp", "fsdp"), scatter_dimension=0, tiled=True),
        lax.psum_scatter(grad_shared_down, ("dp", "fsdp"), scatter_dimension=0, tiled=True),
        lax.psum_scatter(grad_shared_gate, ("dp", "fsdp"), scatter_dimension=0, tiled=True),
    )
    grad_normed = (
        grad_normed
        + product_back(shared_joined_grad, full_shared_gu)
        + shared_logit_grad[:, None] * full_shared_gate.astype(jnp.float32)[None, :]
    )
    grad_probs = jnp.sum(chosen * grad_gates[:, :, None], axis=1)
    logit_grad = (
        router_probs * (grad_probs - jnp.sum(router_probs * grad_probs, axis=1, keepdims=True))
    ).astype(jnp.bfloat16)
    grad_router = transposed_product(normed_two, logit_grad)
    grad_normed = grad_normed + product_back(logit_grad, full_router)
    grad_residual_in, grad_gain_moe = norm_back(
        grad_normed, normal_two, factor_two, gain_moe.astype(jnp.float32)
    )
    grad_residual = grad_out + grad_residual_in
    back_gain_attn, back_query, back_key, back_value, back_output = (
        lax.all_gather(norm_attn, ("dp", "fsdp"), axis=0, tiled=True),
        lax.all_gather(q_weight, ("dp", "fsdp"), axis=0, tiled=True),
        lax.all_gather(k_weight, ("dp", "fsdp"), axis=0, tiled=True),
        lax.all_gather(v_weight, ("dp", "fsdp"), axis=0, tiled=True),
        lax.all_gather(o_weight, ("dp", "fsdp"), axis=0, tiled=True),
    )
    attn_grad = (live_mask * grad_residual).astype(jnp.bfloat16)
    grad_output_weight = transposed_product(attended, attn_grad)
    attended_grad = product_back(attn_grad, back_output).astype(jnp.bfloat16).reshape(shape_four)
    again_scores = (
        jnp.einsum("sqhd,skhd->shqk", query_rot, all_keys, preferred_element_type=jnp.float32)
        * score_scale
    )
    again_probs = jnp.exp(jnp.where(causal[None, None], again_scores, negative) - log_total)
    prob_grad = jnp.einsum(
        "sqhd,skhd->shqk", attended_grad, all_values, preferred_element_type=jnp.float32
    )
    inner_sum = jnp.sum(again_probs * prob_grad, axis=-1, keepdims=True)
    score_grad = (again_probs * (prob_grad - inner_sum)).astype(jnp.bfloat16)
    grad_query_rot = (
        jnp.einsum("shqk,skhd->sqhd", score_grad, all_keys, preferred_element_type=jnp.float32)
        * score_scale
    )
    grad_key_part = (
        jnp.einsum("shqk,sqhd->skhd", score_grad, query_rot, preferred_element_type=jnp.float32)
        * score_scale
    )
    grad_value_part = jnp.einsum(
        "shqk,sqhd->skhd",
        again_probs.astype(jnp.bfloat16),
        attended_grad,
        preferred_element_type=jnp.float32,
    )
    grad_keys, grad_values = (
        lax.psum_scatter(grad_key_part, "fsdp", scatter_dimension=1, tiled=True),
        lax.psum_scatter(grad_value_part, "fsdp", scatter_dimension=1, tiled=True),
    )
    grad_query = (
        rotate_back(grad_query_rot, cosine, sine_table)
        .astype(jnp.bfloat16)
        .reshape(token_rows, model_width)
    )
    grad_key = (
        rotate_back(grad_keys, cosine, sine_table)
        .astype(jnp.bfloat16)
        .reshape(token_rows, model_width)
    )
    grad_value = grad_values.astype(jnp.bfloat16).reshape(token_rows, model_width)
    grad_query_weight = transposed_product(normed_one, grad_query)
    grad_key_weight = transposed_product(normed_one, grad_key)
    grad_value_weight = transposed_product(normed_one, grad_value)
    grad_query_bias = jnp.sum(grad_query.astype(jnp.float32), axis=0)
    grad_key_bias = jnp.sum(grad_key.astype(jnp.float32), axis=0)
    grad_value_bias = jnp.sum(grad_value.astype(jnp.float32), axis=0)
    grad_normed_one = (
        product_back(grad_query, back_query)
        + product_back(grad_key, back_key)
        + product_back(grad_value, back_value)
    )
    grad_input_one, grad_gain_attn = norm_back(
        grad_normed_one, normal_one, factor_one, back_gain_attn.astype(jnp.float32)
    )
    grad_inputs = (
        (grad_residual + grad_input_one)
        .astype(jnp.bfloat16)
        .reshape(per_group, local_rows, model_width)
    )
    attn_grads = (
        lax.psum_scatter(grad_gain_attn, ("dp", "fsdp"), scatter_dimension=0, tiled=True),
        lax.psum_scatter(grad_query_weight, ("dp", "fsdp"), scatter_dimension=0, tiled=True),
        lax.psum_scatter(grad_key_weight, ("dp", "fsdp"), scatter_dimension=0, tiled=True),
        lax.psum_scatter(grad_value_weight, ("dp", "fsdp"), scatter_dimension=0, tiled=True),
        lax.psum_scatter(grad_query_bias, ("dp", "fsdp"), scatter_dimension=0, tiled=True),
        lax.psum_scatter(grad_key_bias, ("dp", "fsdp"), scatter_dimension=0, tiled=True),
        lax.psum_scatter(grad_value_bias, ("dp", "fsdp"), scatter_dimension=0, tiled=True),
        lax.psum_scatter(grad_output_weight, ("dp", "fsdp"), scatter_dimension=0, tiled=True),
        lax.psum_scatter(grad_gain_moe, ("dp", "fsdp"), scatter_dimension=0, tiled=True),
        lax.psum_scatter(grad_router, ("dp", "fsdp"), scatter_dimension=0, tiled=True),
    )
    back_rows = (
        lax.all_to_all(output_low, "dp", split_axis=1, concat_axis=0, tiled=True),
        lax.all_to_all(grad_inputs, "dp", split_axis=1, concat_axis=0, tiled=True),
    )
    mixed_given = jnp.zeros_like(tokens).at[order].set(back_rows[0])
    grad_given = jnp.zeros_like(cotangent).at[order].set(back_rows[1])
    return (
        mixed_given,
        grad_given,
        attn_grads[0],
        attn_grads[1],
        attn_grads[2],
        attn_grads[3],
        attn_grads[4],
        attn_grads[5],
        attn_grads[6],
        attn_grads[7],
        attn_grads[8],
        attn_grads[9],
        moe_grads[2],
        moe_grads[0],
        moe_grads[1],
        expert_grads[0],
        expert_grads[1],
    )


def solution(mesh):
    in_specs = (
        P(None, ("dp", "fsdp"), None),
        P(None, ("dp", "fsdp"), None),
        P(),
        P(),
        P(),
        P(("dp", "fsdp")),
        P(("dp", "fsdp"), None),
        P(("dp", "fsdp"), None),
        P(("dp", "fsdp"), None),
        P(("dp", "fsdp")),
        P(("dp", "fsdp")),
        P(("dp", "fsdp")),
        P(("dp", "fsdp"), None),
        P(("dp", "fsdp")),
        P(("dp", "fsdp"), None),
        P(("dp", "fsdp")),
        P(("dp", "fsdp"), None),
        P(("dp", "fsdp"), None),
        P("dp", "fsdp", None),
        P("dp", "fsdp", None),
    )
    out_specs = (
        P(None, ("dp", "fsdp"), None),
        P(None, ("dp", "fsdp"), None),
        P(("dp", "fsdp")),
        P(("dp", "fsdp"), None),
        P(("dp", "fsdp"), None),
        P(("dp", "fsdp"), None),
        P(("dp", "fsdp")),
        P(("dp", "fsdp")),
        P(("dp", "fsdp")),
        P(("dp", "fsdp"), None),
        P(("dp", "fsdp")),
        P(("dp", "fsdp"), None),
        P(("dp", "fsdp")),
        P(("dp", "fsdp"), None),
        P(("dp", "fsdp"), None),
        P("dp", "fsdp", None),
        P("dp", "fsdp", None),
    )
    return jax.shard_map(
        on_device, mesh=mesh, in_specs=in_specs, out_specs=out_specs, check_vma=False
    )
```

profile of v0, /device:TPU:0, one launch (start us, length us, event | category | flops | bytes accessed | tf_op | source)
XLA Modules:
  0.0 3799.1 jit_solution(8683474855407136344)
XLA Ops:
  14.1 7.3 all-to-all-start
  22.9 41.5 %all-reduce.13 = (bf16[2048]{0:T(1024)(128)(2,1)S(1)}, bf16[2048]{0:T(1024)(128)(2,1)S(1)}, bf16[2048]{0:T(1024)(128)(2,1)S(1)}, bf16[2048]{0:T(1024)(128)(2,1)S...) all-reduce(bf16[2048]{0:T(1024)(128)(2,1)S(1)} %dynamic-update-slic, ...), channel_id=1, replica_groups=mesh['dp'=8,'fsdp'=4] {'dp','fsdp'}, use_global_device_ids=true, to_apply=%add | all-reduce | flops 12288 | bytes 49152
  67.1 27.8 all-gather.18.cloned.1.call-done
  94.9 4.6 fusion.23
  99.8 74.0 %all-gather.16.cloned.1.call-done = bf16[2048,2048]{1,0:T(8,128)(2,1)} async-done(((bf16[64,2048]{1,0:T(8,128)(2,1)}), bf16[2048,2048]{1,0:T(8,128)(2,1)}) %all-gather.16.cloned.1.call-update) | async-done | bytes 8388624 | tf_op jit(solution)/shard_map/all_gather | solution.py:143
  173.8 4.6 fusion.22
  182.1 70.7 %all-gather.12.cloned.1.call-done = bf16[2048,2048]{1,0:T(8,128)(2,1)} async-done(((bf16[64,2048]{1,0:T(8,128)(2,1)}), bf16[2048,2048]{1,0:T(8,128)(2,1)}) %all-gather.12.cloned.1.call-update) | async-done | bytes 8388624 | tf_op jit(solution)/shard_map/all_gather | solution.py:145
  252.7 4.7 fusion.27
  265.8 10.1 all-gather.20.cloned.1.call-done
  279.2 21.4 all-gather.14.cloned.1.call-done
  303.1 77.7 %all-gather.22.cloned.1.call-done = bf16[2048,2048]{1,0:T(8,128)(2,1)} async-done(((bf16[64,2048]{1,0:T(8,128)(2,1)}), bf16[2048,2048]{1,0:T(8,128)(2,1)}) %all-gather.22.cloned.1.call-update) | async-done | bytes 8388624 | tf_op jit(solution)/shard_map/all_gather | solution.py:149
  380.8 5.1 multiply_reduce_fusion.9
  390.0 5.8 scatter_custom_fusion
  395.9 63.8 %all_to_all.74 = bf16[8,80,2048]{2,1,0:T(8,128)(2,1)} all-to-all(bf16[8,80,2048]{2,1,0:T(8,128)(2,1)S(1)} %bitcast.209), channel_id=1, replica_groups=mesh['dp'=8,'fsdp'=4] {'dp'}, dimensions={0} | all-to-all | bytes 5242880 | tf_op jit(solution)/shard_map/all_to_all | solution.py:235
  459.7 3.6 all-to-all-start.4
  463.4 12.8 fusion.2
  480.3 21.9 all-gather.30.cloned.1.call-done
  502.2 8.1 fusion.9
  511.1 5.5 all-to-all-start.2
  517.0 107.3 %all-gather = bf16[32,64,8]{1,2,0:T(8,128)(2,1)S(1)} all-gather(bf16[1,64,8]{1,2,0:T(8,128)(2,1)S(1)} %bitcast.247), channel_id=1, replica_groups=mesh['dp'=8,'fsdp'=4] {'dp','fsdp'}, dimensions={0}, use_global_device_ids=true | all-gather | bytes 33792 | tf_op jit(solution)/shard_map/all_gather | solution.py:151
  630.3 176.9 %all-gather.24.cloned.1.call-done = bf16[2048,11264]{1,0:T(8,128)(2,1)} async-done(((bf16[64,11264]{1,0:T(8,128)(2,1)}), bf16[2048,11264]{1,0:T(8,128)(2,1)}) %all-gather.24.cloned.1.call-update) | async-done | bytes 46137360 | tf_op jit(solution)/shard_map/all_gather | solution.py:153
  807.2 20.7 fusion.103
  831.5 121.2 %all-gather.26.cloned.1.call-done = bf16[5632,2048]{1,0:T(8,128)(2,1)} async-done(((bf16[176,2048]{1,0:T(8,128)(2,1)}), bf16[5632,2048]{1,0:T(8,128)(2,1)}) %all-gather.26.cloned.1.call-update) | async-done | bytes 23068688 | tf_op jit(solution)/shard_map/all_gather | solution.py:154
  952.7 11.8 multiply_reduce_fusion.8
  968.7 5.4 mul.564
  977.5 6.5 scatter_custom_fusion.2
  984.0 63.6 %all_to_all.75 = bf16[8,80,2048]{2,1,0:T(8,128)(2,1)S(1)} all-to-all(bf16[8,80,2048]{2,1,0:T(8,128)(2,1)S(1)} %bitcast.208), channel_id=1, replica_groups=mesh['dp'=8,'fsdp'=4] {'dp'}, dimensions={0} | all-to-all | bytes 5242880 | tf_op jit(solution)/shard_map/all_to_all | solution.py:277
  1047.6 10.1 multiply_convert_fusion.2
  1057.8 8.9 fusion.12
  1066.7 3.6 all-to-all-start.6
  1070.8 15.3 multiply_convert_fusion.5
  1086.1 43.7 %all-to-all-done.6 = bf16[8,80,2048]{2,1,0:T(8,128)(2,1)S(1)} async-done(((bf16[8,80,2048]{2,1,0:T(8,128)(2,1)}), bf16[8,80,2048]{2,1,0:T(8,128)(2,1)S(1)}, u32[]{:S(2)}, u32[]{:S(2)}) %all-to-all-start.6) | async-done | bytes 2621472 | tf_op jit(solution)/shard_map/all_to_all | solution.py:302
  1133.1 6.2 select_convert_fusion
  1139.2 5.2 reshape.663
  1144.4 6.4 multiply_reduce_fusion.1
  1150.9 22.0 fusion.16
  1175.2 5.3 reshape.646
  1180.6 5.6 multiply_reduce_fusion.2
  1187.5 6.7 fusion.29
  1197.3 5.5 copy.171
  1212.7 8.0 fusion.4
  1222.4 14.4 convert_bitcast_fusion
  1238.2 8.2 fusion.53
  1249.1 10.0 fusion.43
  1264.9 27.9 reduce-scatter.14.cloned.1.call-done
  1297.7 8.2 fusion.46
  1307.3 8.2 fusion.49
  1316.9 19.1 fusion.94
  1337.4 33.2 fusion.20
  1372.9 5.5 all-to-all-start.3
  1378.5 6.4 fusion.51
  1384.9 6.4 convolution_add_fusion.2
  1396.2 6.3 all-to-all-start.7
  1402.8 28.2 reduce-scatter.34.cloned.1.call-done
  1434.8 50.2 %reduce-scatter.32.cloned.1.call-done = bf16[1,352,2048]{2,1,0:T(8,128)(2,1)} async-done(((bf16[1,1408,2048]{2,1,0:T(8,128)(2,1)}), bf16[1,352,2048]{2,1,0:T(8,128)(2,1)}) %reduce-scatter.32.cloned.1.call-update) | async-done | bytes 1441808 | tf_op jit(solution)/shard_map/reduce_scatter | solution.py:298
  1488.3 40.3 %all-reduce.12 = (f32[2048]{0:T(1024)S(1)}, f32[2048]{0:T(1024)S(1)}, f32[2048]{0:T(1024)S(1)}, f32[2048]{0:T(1024)S(1)}, f32[2048]{0:T(1024)S(1)}, /*index=5*/f32[2048]{0:T(1024)S(1)}) all-reduce(f32[2048]{0:T(1024)S(1)} %get-tuple-element.21, f32[2048]{0:T(1024)S(1)} %bitcast.245, ...), channel_id=4, replica_groups=mesh['dp'=8,'fsdp'=4] {'dp','fsdp'}, use_global_device_ids=true, to_apply=%region_25.28.clone | all-reduce | flops 12288 | bytes 98304
  1533.5 46.8 %reduce-scatter.30.cloned.1.call-done = bf16[1,512,2816]{2,1,0:T(8,128)(2,1)} async-done(((bf16[1,2048,2816]{2,1,0:T(8,128)(2,1)}), bf16[1,512,2816]{2,1,0:T(8,128)(2,1)}) %reduce-scatter.30.cloned.1.call-update) | async-done | bytes 2883600 | tf_op jit(solution)/shard_map/reduce_scatter | solution.py:295
  1580.3 4.8 convert_element_type.302
  1585.0 180.9 %reduce-scatter.24.cloned.1.call-done = f32[64,2048]{1,0:T(8,128)} async-done(((f32[2048,2048]{1,0:T(8,128)}), f32[64,2048]{1,0:T(8,128)}) %reduce-scatter.24.cloned.1.call-update) | async-done | bytes 524304 | tf_op jit(solution)/shard_map/reduce_scatter | solution.py:416
  1765.9 187.2 %reduce-scatter.22.cloned.1.call-done = f32[64,2048]{1,0:T(8,128)} async-done(((f32[2048,2048]{1,0:T(8,128)}), f32[64,2048]{1,0:T(8,128)}) %reduce-scatter.22.cloned.1.call-update) | async-done | bytes 524304 | tf_op jit(solution)/shard_map/reduce_scatter | solution.py:412
  1953.1 187.2 %reduce-scatter.20.cloned.1.call-done = f32[64,2048]{1,0:T(8,128)} async-done(((f32[2048,2048]{1,0:T(8,128)}), f32[64,2048]{1,0:T(8,128)}) %reduce-scatter.20.cloned.1.call-update) | async-done | bytes 524304 | tf_op jit(solution)/shard_map/reduce_scatter | solution.py:411
  2140.3 187.4 %reduce-scatter.18.cloned.1.call-done = f32[64,2048]{1,0:T(8,128)} async-done(((f32[2048,2048]{1,0:T(8,128)}), f32[64,2048]{1,0:T(8,128)}) %reduce-scatter.18.cloned.1.call-update) | async-done | bytes 524304 | tf_op jit(solution)/shard_map/reduce_scatter | solution.py:410
  2327.7 489.4 %reduce-scatter.28.cloned.1.call-done = f32[176,2048]{1,0:T(8,128)} async-done(((f32[5632,2048]{1,0:T(8,128)}), f32[176,2048]{1,0:T(8,128)}) %reduce-scatter.28.cloned.1.call-update) | async-done | bytes 1441808 | tf_op jit(solution)/shard_map/reduce_scatter | solution.py:322
  2817.1 974.9 %reduce-scatter.26.cloned.1.call-done = f32[64,11264]{1,0:T(8,128)} async-done(((f32[2048,11264]{1,0:T(8,128)}), f32[64,11264]{1,0:T(8,128)}) %reduce-scatter.26.cloned.1.call-update) | async-done | bytes 2883600 | tf_op jit(solution)/shard_map/reduce_scatter | solution.py:321
  (382 shorter events, 115.2 us)
Async XLA Ops:
  7.2 87.7 %all-gather.18.cloned.1.call-start = ((), (), s32[]{:S(2)}) async-start(), calls=%async_computation.22 | async-start | bytes 8650752 | tf_op jit(solution)/shard_map/all_gather | solution.py:144
  8.0 13.4 copy-start.73
  8.0 13.7 copy-start.74
  8.0 13.9 copy-start.75
  8.0 14.2 copy-start.76
  8.0 14.4 copy-start.77
  8.0 14.7 copy-start.78
  8.0 165.8 %all-gather.16.cloned.1.call-start = ((), (), s32[]{:S(2)}) async-start(), calls=%async_computation.21 | async-start | bytes 8650752 | tf_op jit(solution)/shard_map/all_gather | solution.py:143
  8.8 244.0 %all-gather.12.cloned.1.call-start = ((), (), s32[]{:S(2)}) async-start(), calls=%async_computation.19 | async-start | bytes 8650752 | tf_op jit(solution)/shard_map/all_gather | solution.py:145
  14.1 52.0 %all-to-all-start = ((bf16[16,8,2048]{2,1,0:T(8,128)(2,1)}), bf16[16,8,2048]{2,1,0:T(8,128)(2,1)S(1)}, u32[]{:S(2)}, u32[]{:S(2)}) async-start(bf16[16,8,2048]{2,1,0:T(8,128)(2,1)} %get-tuple-element.76), calls=%async_computation | async-start | bytes 1048576 | tf_op jit(solution)/shard_map/all_to_all | solution.py:119
  21.3 254.6 %all-gather.20.cloned.1.call-start = ((), (), s32[]{:S(2)}) async-start(), calls=%async_computation.23 | async-start | bytes 2621440 | tf_op jit(solution)/shard_map/all_gather | solution.py:190
  65.3 114.8 %copy-start.47 = (f32[64,128]{1,0:T(8,128)}, f32[64,128]{1,0:T(8,128)S(1)}, u32[]{:S(2)}) copy-start(f32[64,128]{1,0:T(8,128)S(1)} %get-tuple-element.68) | copy-start | bytes 98308
  66.0 114.1 %copy-start.49 = (f32[64,128]{1,0:T(8,128)}, f32[64,128]{1,0:T(8,128)S(1)}, u32[]{:S(2)}) copy-start(f32[64,128]{1,0:T(8,128)S(1)} %get-tuple-element.70) | copy-start | bytes 98308
  66.1 33.5 copy-start.5
  66.8 28.1 copy-start.57
  66.9 32.7 copy-start.62
  182.0 94.0 %copy-start.25 = (bf16[2,64,16,128]{3,1,2,0:T(8,128)(2,1)}, bf16[2,64,16,128]{3,1,2,0:T(8,128)(2,1)S(1)}, u32[]{:S(2)}) copy-start(bf16[2,64,16,128]{3,1,2,0:T(8,128)(2,1)S(1)} %get-tuple-element.66) | copy-start | bytes 1572868
  182.0 118.5 %all-gather.14.cloned.1.call-start = ((), (), s32[]{:S(2)}) async-start(), calls=%async_computation.20 | async-start | bytes 2621440 | tf_op jit(solution)/shard_map/all_gather | solution.py:191
  258.5 122.3 %all-gather.22.cloned.1.call-start = ((), (), s32[]{:S(2)}) async-start(), calls=%async_computation.24 | async-start | bytes 8650752 | tf_op jit(solution)/shard_map/all_gather | solution.py:149
  259.1 204.3 %all-gather.28.cloned.1.call-start = ((), (), s32[]{:S(2)}) async-start(), calls=%async_computation.27 | async-start | bytes 14417920 | tf_op jit(solution)/shard_map/all_gather | solution.py:172
  259.8 242.3 %all-gather.30.cloned.1.call-start = ((), (), s32[]{:S(2)}) async-start(), calls=%async_computation.28 | async-start | bytes 7208960 | tf_op jit(solution)/shard_map/all_gather | solution.py:173
  260.6 546.6 %all-gather.24.cloned.1.call-start = ((), (), s32[]{:S(2)}) async-start(), calls=%async_computation.25 | async-start | bytes 47579136 | tf_op jit(solution)/shard_map/all_gather | solution.py:153
  261.3 691.4 %all-gather.26.cloned.1.call-start = ((), (), s32[]{:S(2)}) async-start(), calls=%async_computation.26 | async-start | bytes 23789568 | tf_op jit(solution)/shard_map/all_gather | solution.py:154
  264.6 121.3 %copy-start.54 = (f32[2048]{0:T(1024)}, f32[2048]{0:T(1024)S(1)}, u32[]{:S(2)}) copy-start(f32[2048]{0:T(1024)S(1)} %convert_element_type.266) | copy-start | bytes 24580
  278.5 24.3 copy-start.3
  279.1 21.4 copy-start.45
  303.1 82.7 %copy-start.20 = (bf16[2,64,16,128]{3,2,1,0:T(8,128)(2,1)}, bf16[2,64,16,128]{3,2,1,0:T(8,128)(2,1)S(1)}, u32[]{:S(2)}) copy-start(bf16[2,64,16,128]{3,2,1,0:T(8,128)(2,1)S(1)} %copy.147) | copy-start | bytes 1572868
  459.7 50.5 %all-to-all-start.4 = ((bf16[16,8,2048]{2,1,0:T(8,128)(2,1)}), bf16[16,8,2048]{2,1,0:T(8,128)(2,1)S(1)}, u32[]{:S(2)}, u32[]{:S(2)}) async-start(bf16[16,8,2048]{2,1,0:T(8,128)(2,1)} %get-tuple-element.75), calls=%async_computation.4 | async-start | bytes 1048576 | tf_op jit(solution)/shard_map/all_to_all | solution.py:122
  480.3 30.0 copy-start.43
  511.1 115.9 %all-to-all-start.2 = ((bf16[8,80,2048]{2,1,0:T(8,128)(2,1)}), bf16[8,80,2048]{2,1,0:T(8,128)(2,1)S(1)}, u32[]{:S(2)}, u32[]{:S(2)}) async-start(bf16[8,80,2048]{2,1,0:T(8,128)(2,1)} %bitcast.232), calls=%async_computation.2 | async-start | bytes 5242880 | tf_op jit(solution)/shard_map/all_to_all | solution.py:250
  827.9 124.8 %copy-start.15 = (f32[8,2,8,2048]{3,2,0,1:T(8,128)S(1)}, f32[8,2,8,2048]{3,2,0,1:T(8,128)}, u32[]{:S(2)}) copy-start(f32[8,2,8,2048]{3,2,0,1:T(8,128)} %copy.162) | copy-start | bytes 3145732
  831.5 133.0 %copy-start.7 = (bf16[128,5632]{1,0:T(8,128)(2,1)}, bf16[128,5632]{1,0:T(8,128)(2,1)S(1)}, u32[]{:S(2)}) copy-start(bf16[128,5632]{1,0:T(8,128)(2,1)S(1)} %multiply_convert_fusion.6) | copy-start | bytes 4325380
  984.0 73.7 %slice-start.2 = ((s8[11534336]{0:T(1024)(128)(4,1)}), s8[4194304]{0:T(1024)(128)(4,1)S(1)}, s32[]{:S(2)}) async-start(s8[11534336]{0:T(1024)(128)(4,1)} %bitcast.250), calls=%async_computation.42 | async-start | bytes 8388608
  1047.6 10.1 slice-start.4
  1066.7 63.1 %all-to-all-start.6 = ((bf16[8,80,2048]{2,1,0:T(8,128)(2,1)}), bf16[8,80,2048]{2,1,0:T(8,128)(2,1)S(1)}, u32[]{:S(2)}, u32[]{:S(2)}) async-start(bf16[8,80,2048]{2,1,0:T(8,128)(2,1)} %bitcast.233), calls=%async_computation.6 | async-start | bytes 5242880 | tf_op jit(solution)/shard_map/all_to_all | solution.py:302
  1070.3 177.3 %reduce-scatter.16.cloned.1.call-start = ((), (), s32[]{:S(2)}) async-start(), calls=%async_computation.30 | async-start | bytes 5242880 | tf_op jit(solution)/shard_map/reduce_scatter | solution.py:376
  1070.8 80.0 %copy-start.69 = (f32[128]{0:T(128)}, f32[128]{0:T(128)S(1)}, u32[]{:S(2)}) copy-start(f32[128]{0:T(128)S(1)} %get-tuple-element.84) | copy-start | bytes 1540
  1070.8 115.4 %copy-start.64 = (f32[128]{0:T(128)}, f32[128]{0:T(128)S(1)}, u32[]{:S(2)}) copy-start(f32[128]{0:T(128)S(1)} %get-tuple-element.85) | copy-start | bytes 1540
  1150.9 22.0 copy-start.11
  1150.9 22.0 copy-start.55
  1150.9 22.0 copy-start.66
  1202.9 89.9 %reduce-scatter.14.cloned.1.call-start = ((), (), s32[]{:S(2)}) async-start(), calls=%async_computation.29 | async-start | bytes 5242880 | tf_op jit(solution)/shard_map/reduce_scatter | solution.py:375
  1210.5 220.5 %reduce-scatter.34.cloned.1.call-start = ((), (), s32[]{:S(2)}) async-start(), calls=%async_computation.39 | async-start | bytes 1081344
  1211.9 273.1 %reduce-scatter.32.cloned.1.call-start = ((), (), s32[]{:S(2)}) async-start(), calls=%async_computation.38 | async-start | bytes 7208960 | tf_op jit(solution)/shard_map/reduce_scatter | solution.py:298
  1220.7 359.6 %reduce-scatter.30.cloned.1.call-start = ((), (), s32[]{:S(2)}) async-start(), calls=%async_computation.37 | async-start | bytes 14417920 | tf_op jit(solution)/shard_map/reduce_scatter | solution.py:295
  1236.9 529.0 %reduce-scatter.24.cloned.1.call-start = ((), (), s32[]{:S(2)}) async-start(), calls=%async_computation.34 | async-start | bytes 17301504 | tf_op jit(solution)/shard_map/reduce_scatter | solution.py:416
  1246.4 706.7 %reduce-scatter.22.cloned.1.call-start = ((), (), s32[]{:S(2)}) async-start(), calls=%async_computation.33 | async-start | bytes 17301504 | tf_op jit(solution)/shard_map/reduce_scatter | solution.py:412
  1259.0 881.2 %reduce-scatter.20.cloned.1.call-start = ((), (), s32[]{:S(2)}) async-start(), calls=%async_computation.32 | async-start | bytes 17301504 | tf_op jit(solution)/shard_map/reduce_scatter | solution.py:411
  1263.2 29.6 copy-start.50
  1264.9 29.8 copy-start.48
  1264.9 29.8 copy-start.56
  1305.9 1021.8 %reduce-scatter.18.cloned.1.call-start = ((), (), s32[]{:S(2)}) async-start(), calls=%async_computation.31 | async-start | bytes 17301504 | tf_op jit(solution)/shard_map/reduce_scatter | solution.py:410
  1315.6 1501.5 %reduce-scatter.28.cloned.1.call-start = ((), (), s32[]{:S(2)}) async-start(), calls=%async_computation.36 | async-start | bytes 47579136 | tf_op jit(solution)/shard_map/reduce_scatter | solution.py:322
  1336.0 2456.0 %reduce-scatter.26.cloned.1.call-start = ((), (), s32[]{:S(2)}) async-start(), calls=%async_computation.35 | async-start | bytes 95158272 | tf_op jit(solution)/shard_map/reduce_scatter | solution.py:321
  1372.9 23.3 all-to-all-start.3
  1378.4 12.9 slice-start
  1394.8 38.9 %copy-start.68 = (s32[16]{0:T(128)S(1)}, s32[16]{0:T(128)}, u32[]{:S(2)}) copy-start(s32[16]{0:T(128)} %copy-done.67) | copy-start | bytes 196
  1396.2 135.9 %all-to-all-start.7 = ((bf16[2,64,2048]{2,0,1:T(2,128)(2,1)}), bf16[2,64,2048]{2,0,1:T(2,128)(2,1)S(1)}, u32[]{:S(2)}, u32[]{:S(2)}) async-start(bf16[2,64,2048]{2,0,1:T(2,128)(2,1)} %copy.173), calls=%async_computation.9 | async-start | bytes 1048576 | tf_op jit(solution)/shard_map/all_to_all | solution.py:422
  1433.7 54.6 %copy-start.59 = (f32[2048]{0:T(1024)S(1)}, f32[2048]{0:T(1024)}, u32[]{:S(2)}) copy-start(f32[2048]{0:T(1024)} %get-tuple-element.19) | copy-start | bytes 24580
  1433.7 54.6 %copy-start.60 = (f32[16,128]{1,0:T(8,128)S(1)}, f32[16,128]{1,0:T(8,128)}, u32[]{:S(2)}) copy-start(f32[16,128]{1,0:T(8,128)} %get-tuple-element.39) | copy-start | bytes 24580
  1433.7 54.6 %copy-start.61 = (f32[16,128]{1,0:T(8,128)S(1)}, f32[16,128]{1,0:T(8,128)}, u32[]{:S(2)}) copy-start(f32[16,128]{1,0:T(8,128)} %get-tuple-element.92) | copy-start | bytes 24580
  1434.8 97.6 %copy-start.42 = (bf16[16,8,2048]{2,1,0:T(8,128)(2,1)}, bf16[16,8,2048]{2,1,0:T(8,128)(2,1)S(1)}, u32[]{:S(2)}) copy-start(bf16[16,8,2048]{2,1,0:T(8,128)(2,1)S(1)} %scatter_fusion) | copy-start | bytes 1572868
  1532.4 2259.6 %copy-start.1 = (bf16[16,8,2048]{2,1,0:T(8,128)(2,1)S(1)}, bf16[16,8,2048]{2,1,0:T(8,128)(2,1)}, u32[]{:S(2)}) copy-start(bf16[16,8,2048]{2,1,0:T(8,128)(2,1)} %param.25) | copy-start | bytes 1572868
  1533.5 51.6 %copy-start.41 = (bf16[16,8,2048]{2,1,0:T(8,128)(2,1)}, bf16[16,8,2048]{2,1,0:T(8,128)(2,1)S(1)}, u32[]{:S(2)}) copy-start(bf16[16,8,2048]{2,1,0:T(8,128)(2,1)S(1)} %scatter_fusion.1) | copy-start | bytes 1572868
  (49 other events, 202.2 us)
Sparse Core Ops, SparseCore 0:
  10.9 83.9 all-gather.17
  97.8 75.9 all-gather.15
  176.7 76.0 all-gather.11
  254.7 21.1 all-gather.19
  277.9 22.5 all-gather.13
  303.3 77.4 all-gather.21
  382.3 74.7 all-gather.27
  458.7 43.3 all-gather.29
  505.0 302.1 all-gather.23
  809.9 142.7 all-gather.25
  1203.0 42.6 reduce-scatter.15
  1248.2 44.5 reduce-scatter.13
  1295.0 135.9 reduce-scatter.33
  1434.1 50.8 reduce-scatter.31
  1487.4 92.7 reduce-scatter.29
  1583.0 182.8 reduce-scatter.23
  1768.6 184.4 reduce-scatter.21
  1955.8 184.4 reduce-scatter.19
  2143.2 184.4 reduce-scatter.17
  2330.4 486.6 reduce-scatter.27
  2820.0 971.9 reduce-scatter.25
where the time goes:
time: 3820 us; the launch traced here: 3800 us
  waiting for transfers between devices  3010 us (79%)
  blocking collectives  317 us (8%)
  matrix products  282 us (7%)
  local copies, waits for them, and re-layouts  83 us (2%)
  other arithmetic  57.7 us (2%)
    reduce_scatter x1, waiting for transfers between devices, on_device(): lax.psum_scatter(grad_shared_gu, ('dp', 'fsdp'), scatter_dimension=0, til...  975 us
    reduce_scatter x1, waiting for transfers between devices, on_device(): lax.psum_scatter(grad_shared_down, ('dp', 'fsdp'), scatter_dimension=0, t...  489 us
    reduce_scatter x1, waiting for transfers between devices, on_device(): lax.psum_scatter(grad_query_weight, ('dp', 'fsdp'), scatter_dimension=0,...  187 us
    reduce_scatter x1, waiting for transfers between devices, on_device(): lax.psum_scatter(grad_value_weight, ('dp', 'fsdp'), scatter_dimension=0,...  187 us
    reduce_scatter x1, waiting for transfers between devices, on_device(): lax.psum_scatter(grad_key_weight, ('dp', 'fsdp'), scatter_dimension=0, ti...  187 us
    reduce_scatter x1, waiting for transfers between devices, on_device(): lax.psum_scatter(grad_output_weight, ('dp', 'fsdp'), scatter_dimension=0,...  181 us
    all_gather x1, waiting for transfers between devices, on_device(): lax.all_gather(shared_gate_up, ('dp', 'fsdp'), axis=0, tiled=True)  177 us
    all_gather x1, waiting for transfers between devices, on_device(): lax.all_gather(shared_down, ('dp', 'fsdp'), axis=0, tiled=True)  121 us
  transfers between devices with their start and end apart: 27, of which 20 were waited for; matrix products, arithmetic and copies ran while one was open for 7% of the time, Pallas kernels for 0%

commit v1 on v0

v1 whole, which is shorter than its diff:
```python
import math

import jax
import jax.numpy as jnp
import numpy as np
from jax import lax
from jax.sharding import Mesh
from jax.sharding import PartitionSpec as P

HEAD = 128
TOP = 4
AXES = ("dp", "x", "core")
CHIPS = ("dp", "x")
SPLITS = (48, 40, 40)
LOW = (1, 2, 3)

epsilon = 1e-06
rope_base = 1000000.0
negative = -1e30
F32 = jnp.float32
BF16 = jnp.bfloat16


def mm(a, b):
    return lax.dot_general(a, b, (((1,), (0,)), ((), ())), preferred_element_type=F32)


def mm_tn(a, b):
    return lax.dot_general(a, b, (((0,), (0,)), ((), ())), preferred_element_type=F32)


def mm_nt(a, b):
    return lax.dot_general(a, b, (((1,), (1,)), ((), ())), preferred_element_type=F32)


def devices():
    return lax.axis_size("dp") * 4


def permute(value, pairs):
    return lax.ppermute(value, AXES, pairs)


def swap(value, bit):
    return permute(value, [(i, i ^ (1 << bit)) for i in range(devices())])


def gather_bits(value, bits):
    for bit in bits:
        value = jnp.stack([value, swap(value, bit)])
    return value


def add_low(a, b):
    return (a.astype(F32) + b.astype(F32)).astype(BF16)


def scatter_bits(value, bits):
    for bit in reversed(bits):
        value = add_low(value[0], swap(value[1], bit))
    return value


def pieces(rows):
    start = 0
    found = []
    for count in SPLITS:
        found.append(lax.slice_in_dim(rows, start, start + count, axis=-2))
        start += count
    return found


def rotations(high):
    return [high + (3, 1, 2), high + (1, 2, 3), high + (2, 3, 1)]


def to_order(value, bits, wanted):
    have = tuple(reversed(bits))
    lead = [have.index(bit) for bit in wanted]
    rest = list(range(len(bits), value.ndim))
    return value.transpose(lead + rest)


def relative(bits):
    found = np.zeros((1,), np.int64)
    for bit in bits:
        found = np.concatenate([found, found ^ (1 << bit)])
    return found


def by_bit(mine, theirs, flag, axis):
    low = jnp.where(flag == 0, mine, theirs)
    high = jnp.where(flag == 0, theirs, mine)
    return jnp.stack([low, high], axis=axis)


def xor_order(value, number):
    count = value.shape[0]
    return jnp.stack(
        [lax.dynamic_index_in_dim(value, number ^ k, 0, keepdims=False) for k in range(count)]
    )


def deal(value, part, high):
    parts = 2 << len(high)
    shape = value.shape
    value = xor_order(value.reshape((parts, shape[0] // parts) + shape[1:]), part)
    value = value.reshape((2,) * (len(high) + 1) + value.shape[1:])
    left = len(high) + 1
    for bit in tuple(reversed(high)) + (0,):
        left -= 1
        value = jnp.stack([value[0], swap(value[1], bit)], axis=left)
    return value


def undeal(value, part, high):
    done = 0
    for bit in (0,) + tuple(high):
        keep = lax.index_in_dim(value, 0, done, keepdims=False)
        give = lax.index_in_dim(value, 1, done, keepdims=False)
        value = jnp.stack([keep, swap(give, bit)])
        done += 1
    shape = value.shape[done:]
    value = xor_order(value.reshape((1 << done,) + shape), part)
    return value.reshape((value.shape[0] * shape[0],) + shape[1:])


def rotary_tables(positions):
    freq_index = jnp.arange(HEAD // 2).astype(F32)
    inverse = jnp.exp(freq_index * (-2.0 * math.log(rope_base) / HEAD))
    angles = positions.astype(F32)[:, None] * inverse[None, :]
    cosine = jnp.concatenate([jnp.cos(angles), jnp.cos(angles)], axis=-1)
    sine_table = jnp.concatenate([jnp.sin(angles), jnp.sin(angles)], axis=-1)
    return (cosine, sine_table)


def rotate(values, cosine, sine_table):
    half_width = HEAD // 2
    turned = jnp.concatenate([-values[..., half_width:], values[..., :half_width]], axis=-1)
    return values * cosine + turned * sine_table


def rotate_back(grads_in, cosine, sine_table):
    half_width = HEAD // 2
    scaled = grads_in * sine_table
    turned = jnp.concatenate([scaled[..., half_width:], -scaled[..., :half_width]], axis=-1)
    return grads_in * cosine + turned


def normalize(values):
    factor = lax.rsqrt(jnp.mean(values * values, axis=-1, keepdims=True) + epsilon)
    return (values * factor, factor)


def norm_back(grad_normed, normal, factor, gain_vector):
    scaled = grad_normed * gain_vector
    grad_input = factor * (scaled - normal * jnp.mean(scaled * normal, axis=-1, keepdims=True))
    return (grad_input, jnp.sum(grad_normed * normal, axis=0))


def on_device(
    tokens,
    cotangent,
    lengths,
    order,
    routes,
    norm_attn,
    q_weight,
    k_weight,
    v_weight,
    q_bias,
    k_bias,
    v_bias,
    o_weight,
    norm_moe,
    router,
    shared_gate,
    shared_gate_up,
    shared_down,
    expert_gate_up,
    expert_down,
):
    total = devices()
    chips = total // 2
    bit_count = total.bit_length() - 1
    high = tuple(range(4, bit_count))
    me = lax.axis_index(AXES)
    core = me & 1
    x_bit = (me >> 1) & 1
    pair = (me >> 1) & 7
    upper = me >> 4
    uppers = total // 16
    parts = 2 * uppers
    part = upper * 2 + core
    my_expert = me >> 2
    sequences, piece, width = tokens.shape
    experts = router.shape[1]
    rows = sequences * piece
    length = total * piece
    own_seq = sequences // parts
    depth = q_weight.shape[0]
    heads = width // HEAD
    shared_width = shared_down.shape[0] * total // chips
    expert_width = expert_down.shape[1] * 2
    hidden_width = shared_width + expert_width
    padded = -(-(hidden_width + experts + 1) // 128) * 128
    groups = total // 4
    per_group = sequences // groups
    group_rows = per_group * groups * piece
    capacity = (5 * group_rows * TOP + 4 * experts - 1) // (4 * experts)
    score_scale = HEAD ** (-0.5)
    low_orders = rotations(())
    full_orders = rotations(tuple(reversed(high)))

    small = jnp.concatenate(
        [
            jnp.stack([norm_attn, q_bias, k_bias, v_bias, norm_moe, shared_gate]),
            router.T,
            jnp.zeros((2, depth), BF16),
        ]
    )
    small = lax.all_gather(small, AXES, axis=0)
    small = small.transpose(1, 0, 2).reshape(small.shape[1], width)
    gain_attn = small[0].astype(F32)
    gain_moe = small[4].astype(F32)
    biases = lax.dynamic_slice_in_dim(small[1:4].reshape(3, heads // 2, 2, HEAD), pair, 1, axis=1)
    biases = biases[:, 0].transpose(1, 0, 2).astype(F32)

    token_parts = [
        gather_bits(value, bits)
        for value, bits in zip(
            pieces(deal(tokens, part, high).reshape(rows, width)), low_orders, strict=True
        )
    ]

    stacked = jnp.stack([q_weight, k_weight, v_weight], axis=1)
    by_head = stacked.reshape(depth, 3, 16, HEAD).transpose(2, 0, 1, 3).reshape(16, depth, 3 * HEAD)
    by_head = jnp.broadcast_to(by_head[None], (uppers,) + by_head.shape)
    my_head = lax.all_to_all(
        by_head.reshape(total, depth, 3 * HEAD), AXES, split_axis=0, concat_axis=0, tiled=True
    ).reshape(width, 3 * HEAD)
    qkv_weight = by_bit(my_head, swap(my_head, 0), core, 1).reshape(width, 6 * HEAD)

    o_places = []
    for k in range(uppers):
        o_places.append(
            [
                (
                    i,
                    (((i % parts >> 1) ^ k) << 4) | ((i // parts) << 1) | (i & 1),
                )
                for i in range(total)
            ]
        )
    o_rows = xor_order(jnp.stack([permute(o_weight, places) for places in o_places]), upper)
    o_rows = by_bit(o_rows, swap(o_rows, 0), core, 1).reshape(2 * HEAD, width)

    own_positions = me * piece + jnp.arange(piece, dtype=jnp.int32)
    live_own = (own_positions[None, :] < lengths[:, None]).astype(F32)[:, :, None]
    grad_out = cotangent.astype(F32)
    branch_own = (live_own * grad_out).astype(BF16).reshape(rows, width)
    branch_parts = [
        gather_bits(value, bits)
        for value, bits in zip(pieces(branch_own), full_orders, strict=True)
    ]

    shared_pieces = (
        shared_gate_up.reshape(depth, 2, chips, shared_width)
        .transpose(2, 0, 1, 3)
        .reshape(chips, depth, 2 * shared_width)
    )
    shared_in = lax.all_to_all(shared_pieces, CHIPS, split_axis=0, concat_axis=0, tiled=True)
    shared_in = by_bit(shared_in, swap(shared_in, 0), core, 1).reshape(width, 2, shared_width)
    expert_rows = expert_gate_up.shape[1]
    expert_halves = expert_gate_up[0].reshape(expert_rows, 2, 2, expert_width)
    keep_half = jnp.where(x_bit == 0, expert_halves[:, :, 0], expert_halves[:, :, 1])
    give_half = jnp.where(x_bit == 0, expert_halves[:, :, 1], expert_halves[:, :, 0])
    expert_in = by_bit(keep_half, swap(give_half, 1), x_bit, 0)
    expert_in = by_bit(expert_in, swap(expert_in, 0), core, 1).reshape(width, 2, expert_width)
    spare = padded - hidden_width
    extra = jnp.concatenate(
        [small[6 : 6 + experts], small[5:6], jnp.zeros((spare - experts - 1, width), BF16)]
    ).T
    gate_weight = jnp.concatenate([shared_in[:, 0], expert_in[:, 0], extra], axis=1)
    up_weight = jnp.concatenate(
        [shared_in[:, 1], expert_in[:, 1], jnp.zeros((width, spare), BF16)], axis=1
    )
    shared_out_rows = by_bit(shared_down, swap(shared_down, 0), core, 0).reshape(-1, width)
    expert_out_rows = by_bit(expert_down[0], swap(expert_down[0], 0), core, 0).reshape(-1, width)
    down_weight = jnp.concatenate(
        [shared_out_rows, expert_out_rows, jnp.zeros((spare, width), BF16)]
    )

    all_positions = jnp.arange(length, dtype=jnp.int32)
    named = jnp.any(routes == my_expert, axis=-1) & (all_positions[None, :] < lengths[:, None])
    dealt = (
        jnp.take(named, order, axis=0)
        .reshape(groups, per_group, length // (4 * piece), 4, piece)
        .transpose(0, 3, 1, 2, 4)
        .reshape(groups * 4, group_rows)
        .astype(BF16)
    )
    index = jnp.arange(group_rows, dtype=jnp.int32)
    before = mm(dealt, (index[:, None] < index[None, :]).astype(BF16))
    kept = (
        jnp.where(before < capacity, dealt.astype(F32), 0.0)
        .reshape(groups, 4, per_group, length // (4 * piece), piece)
        .transpose(0, 2, 3, 1, 4)
        .reshape(sequences, length)
    )
    seq_index = jnp.arange(sequences, dtype=jnp.int32)
    place_of = jnp.sum(
        jnp.where(order[None, :] == seq_index[:, None], seq_index[None, :], 0), axis=1
    )
    kept = (
        jnp.take(kept, place_of, axis=0)
        .reshape(sequences, total, piece)
        .transpose(1, 0, 2)
        .reshape(total, rows)
    )

    wanted = (3, 2, 1)
    normed_parts = []
    projected = []
    for value, bits in zip(token_parts, low_orders, strict=True):
        flat = value.reshape(-1, width).astype(F32)
        normed = (normalize(flat)[0] * gain_attn).astype(BF16)
        normed_parts.append(normed)
        out = mm(normed, qkv_weight).reshape(value.shape[:-1] + (6 * HEAD,))
        projected.append(to_order(out, bits, wanted))
    shape_rows = (8, parts, own_seq, piece, 2, 3, HEAD)
    joined = jnp.concatenate(projected, axis=-2).reshape(shape_rows)
    joined = joined + biases
    joined = joined.transpose(5, 2, 4, 0, 1, 3, 6).reshape(3, own_seq, 2, length, HEAD)
    source = relative(tuple(reversed(high)) + (0,))
    low_relative = relative(LOW)
    rel = (low_relative[:, None] ^ source[None, :]).reshape(-1)
    positions = (
        (me ^ jnp.asarray(rel, jnp.int32))[:, None] * piece
        + jnp.arange(piece, dtype=jnp.int32)[None, :]
    ).reshape(-1)
    causal = positions[None, :] <= positions[:, None]
    cosine, sine_table = rotary_tables(positions)
    queries = rotate(joined[0], cosine, sine_table).astype(BF16)
    keys = rotate(joined[1], cosine, sine_table).astype(BF16)
    values = joined[2].astype(BF16)
    scores = (
        jnp.einsum("shqd,shkd->shqk", queries, keys, preferred_element_type=F32) * score_scale
    )
    masked = jnp.where(causal[None, None], scores, negative)
    top_score = jnp.max(masked, axis=-1, keepdims=True)
    log_total = top_score + jnp.log(jnp.sum(jnp.exp(masked - top_score), axis=-1, keepdims=True))
    probs = jnp.exp(masked - log_total).astype(BF16)
    attended = jnp.einsum("shqk,shkd->shqd", probs, values, preferred_element_type=F32)

    def to_parts(value):
        columns = value.shape[0]
        value = value.reshape(columns, own_seq, 2, 8, parts, piece, HEAD)
        value = value.transpose(3, 4, 1, 5, 2, 0, 6).reshape(2, 2, 2, rows, 2 * columns * HEAD)
        return [
            to_order(part_rows, (1, 2, 3), tuple(reversed(bits))).reshape(
                8 * part_rows.shape[-2], -1
            )
            for part_rows, bits in zip(pieces(value), low_orders, strict=True)
        ]

    def reduce_low(parts_in):
        found = [
            scatter_bits(value.astype(BF16).reshape(2, 2, 2, -1, width), bits)
            for value, bits in zip(parts_in, low_orders, strict=True)
        ]
        found = jnp.concatenate(found).reshape(
            (2,) * (1 + len(high)) + (own_seq, piece, width)
        )
        return undeal(found, part, high)

    attended_parts = to_parts(attended.astype(BF16)[None])
    attn_out = reduce_low([mm(value, o_rows) for value in attended_parts])
    inputs = tokens.astype(F32)
    residual = (inputs + live_own * attn_out.astype(F32)).reshape(rows, width)
    normal_two, factor_two = normalize(residual)
    normed_own = (normal_two * gain_moe).astype(BF16)

    column = jnp.arange(padded, dtype=jnp.int32)[None, :]
    is_shared = column < shared_width
    expert_column = jnp.arange(experts, dtype=jnp.int32)[None, :]
    one_expert = (expert_column == my_expert).astype(F32)
    out_parts = []
    grad_parts = []
    grad_gate = grad_up = grad_down = 0.0
    for normed, branch, bits, start in zip(
        pieces(normed_own), branch_parts, full_orders, (0, 48, 88), strict=True
    ):
        count = normed.shape[0]
        everyone = gather_bits(normed, bits)
        lead = everyone.shape[:-1]
        everyone = everyone.reshape(-1, width)
        branch = branch.reshape(-1, width)
        mask = jnp.take(
            kept[:, start : start + count], me ^ jnp.asarray(relative(bits), jnp.int32), axis=0
        ).reshape(-1, 1)
        gate = mm(everyone, gate_weight)
        up = mm(everyone, up_weight)
        back = mm_nt(branch, down_weight)
        logits = gate[:, hidden_width : hidden_width + experts]
        router_probs = jax.nn.softmax(logits, axis=-1)
        shared_weight = jax.nn.sigmoid(
            gate[:, hidden_width + experts : hidden_width + experts + 1]
        )
        my_prob = jnp.sum(router_probs * one_expert, axis=1, keepdims=True)
        weight = jnp.where(is_shared, shared_weight, my_prob * mask)
        sigmoid_gate = jax.nn.sigmoid(gate)
        hidden = gate * sigmoid_gate * up
        hidden_low = (hidden * weight).astype(BF16)
        grad_hidden = back * weight
        along = hidden * back
        shared_along = jnp.sum(jnp.where(is_shared, along, 0.0), axis=1, keepdims=True)
        expert_along = jnp.sum(jnp.where(is_shared, 0.0, along), axis=1, keepdims=True) * mask
        logit_grad = router_probs * expert_along * (one_expert - my_prob)
        shared_logit_grad = shared_along * shared_weight * (1.0 - shared_weight)
        tail = jnp.concatenate([logit_grad, shared_logit_grad], axis=1)
        gate_grad = grad_hidden * up * sigmoid_gate * (1.0 + gate * (1.0 - sigmoid_gate))
        gate_grad = (
            gate_grad + jnp.pad(tail, ((0, 0), (hidden_width, spare - experts - 1)))
        ).astype(BF16)
        up_grad = (grad_hidden * gate * sigmoid_gate).astype(BF16)
        grad_down = grad_down + mm_tn(hidden_low, branch)
        grad_gate = grad_gate + mm_tn(everyone, gate_grad)
        grad_up = grad_up + mm_tn(everyone, up_grad)
        back_rows = mm_nt(gate_grad, gate_weight) + mm_nt(up_grad, up_weight)
        grad_parts.append(scatter_bits(back_rows.astype(BF16).reshape(lead + (width,)), bits))
        out_parts.append(
            scatter_bits(mm(hidden_low, down_weight).astype(BF16).reshape(lead + (width,)), bits)
        )
    live_rows = jnp.broadcast_to(live_own, (sequences, piece, 1)).reshape(rows, 1)
    moe_out = jnp.concatenate(out_parts).astype(F32)
    mixed = (residual + live_rows * moe_out).astype(BF16).reshape(tokens.shape)
    grad_normed = jnp.concatenate(grad_parts).astype(F32)
    grad_residual_in, grad_gain_moe = norm_back(grad_normed, normal_two, factor_two, gain_moe)
    grad_residual = grad_out.reshape(rows, width) + grad_residual_in

    attn_grad = (live_rows * grad_residual).astype(BF16).reshape(tokens.shape)
    attn_grad_parts = [
        gather_bits(value, bits)
        for value, bits in zip(
            pieces(deal(attn_grad, part, high).reshape(rows, width)), low_orders, strict=True
        )
    ]
    attended_grads = []
    grad_o = 0.0
    for value, ahead, bits in zip(attn_grad_parts, attended_parts, low_orders, strict=True):
        flat = value.reshape(-1, width)
        back = mm_nt(flat, o_rows).astype(BF16).reshape(value.shape[:-1] + (2 * HEAD,))
        attended_grads.append(to_order(back, bits, wanted))
        grad_o = grad_o + mm_tn(ahead, flat)
    attended_grad = jnp.concatenate(attended_grads, axis=-2)
    attended_grad = (
        attended_grad.reshape(8, parts, own_seq, piece, 2, HEAD)
        .transpose(2, 4, 0, 1, 3, 5)
        .reshape(own_seq, 2, length, HEAD)
    )
    again = jnp.exp(masked - log_total)
    prob_grad = jnp.einsum("shqd,shkd->shqk", attended_grad, values, preferred_element_type=F32)
    inner_sum = jnp.sum(again * prob_grad, axis=-1, keepdims=True)
    score_grad = (again * (prob_grad - inner_sum)).astype(BF16)
    grad_query = (
        jnp.einsum("shqk,shkd->shqd", score_grad, keys, preferred_element_type=F32) * score_scale
    )
    grad_key = (
        jnp.einsum("shqk,shqd->shkd", score_grad, queries, preferred_element_type=F32)
        * score_scale
    )
    grad_value = jnp.einsum("shqk,shqd->shkd", probs, attended_grad, preferred_element_type=F32)
    grads = jnp.stack(
        [
            rotate_back(grad_query, cosine, sine_table).astype(BF16),
            rotate_back(grad_key, cosine, sine_table).astype(BF16),
            grad_value.astype(BF16),
        ]
    )
    bias_grads = jnp.sum(grads.astype(F32), axis=(1, 3))
    grads_parts = to_parts(grads)
    grad_qkv = 0.0
    normed_grads = []
    for value, normed in zip(grads_parts, normed_parts, strict=True):
        normed_grads.append(mm_nt(value, qkv_weight))
        grad_qkv = grad_qkv + mm_tn(normed, value)
    grad_normed_one = reduce_low(normed_grads).astype(F32).reshape(rows, width)
    normal_one, factor_one = normalize(inputs.reshape(rows, width))
    grad_input, grad_gain_attn = norm_back(grad_normed_one, normal_one, factor_one, gain_attn)
    grad_tokens = (grad_residual + grad_input).astype(BF16).reshape(tokens.shape)

    grad_down = grad_down[:hidden_width].astype(BF16)

    def to_core(value, axis):
        low = lax.index_in_dim(value, 0, axis, keepdims=False)
        top = lax.index_in_dim(value, 1, axis, keepdims=False)
        keep = jnp.where(core == 0, low, top)
        give = jnp.where(core == 0, top, low)
        return keep.astype(F32) + swap(give, 0).astype(F32)

    grad_shared_down = to_core(grad_down[:shared_width].reshape(2, -1, width), 0)
    grad_expert_down = to_core(grad_down[shared_width:].reshape(2, -1, width), 0)
    tail_grads = grad_gate[:, hidden_width : hidden_width + experts + 1]
    grad_gu = jnp.stack(
        [grad_gate[:, :hidden_width].astype(BF16), grad_up[:, :hidden_width].astype(BF16)], axis=1
    )
    grad_shared_gu = to_core(
        grad_gu[:, :, :shared_width].reshape(chips, 2, depth, 2 * shared_width), 1
    ).astype(BF16)
    grad_shared_gu = lax.all_to_all(
        grad_shared_gu, CHIPS, split_axis=0, concat_axis=0, tiled=True
    )
    grad_shared_gu = (
        grad_shared_gu.reshape(chips, depth, 2, shared_width)
        .transpose(1, 2, 0, 3)
        .reshape(depth, -1)
        .astype(F32)
    )
    grad_expert_gu = to_core(
        grad_gu[:, :, shared_width:].reshape(2, 2, expert_rows, 2, expert_width), 1
    ).astype(BF16)
    keep_rows = jnp.where(x_bit == 0, grad_expert_gu[0], grad_expert_gu[1])
    give_rows = jnp.where(x_bit == 0, grad_expert_gu[1], grad_expert_gu[0])
    grad_expert_gu = by_bit(keep_rows, swap(give_rows, 1), x_bit, 2)
    grad_expert_gu = grad_expert_gu.reshape(1, expert_rows, -1).astype(F32)

    grad_qkv = to_core(grad_qkv.astype(BF16).reshape(width, 2, 3 * HEAD), 1).astype(BF16)
    grad_qkv = lax.all_to_all(
        grad_qkv.reshape(total, depth, 3 * HEAD), AXES, split_axis=0, concat_axis=0, tiled=True
    )
    grad_qkv = jnp.sum(grad_qkv.reshape(uppers, 16, depth, 3, HEAD).astype(F32), axis=0)
    grad_qkv = grad_qkv.transpose(2, 1, 0, 3).reshape(3, depth, width)
    grad_o = to_core(grad_o.astype(BF16).reshape(uppers, 2, depth, width), 1).astype(BF16)
    grad_o = xor_order(grad_o, upper)
    grad_o = sum(
        permute(grad_o[k], [(b, a) for a, b in places]).astype(F32)
        for k, places in enumerate(o_places)
    )

    bias_rows = lax.dynamic_update_slice_in_dim(
        jnp.zeros((3, heads // 2, 2 * HEAD), F32),
        bias_grads.reshape(3, 1, 2 * HEAD),
        pair,
        axis=1,
    ).reshape(3, width)
    vectors = jnp.concatenate(
        [grad_gain_attn[None], bias_rows, grad_gain_moe[None], tail_grads.T], axis=0
    )
    vectors = vectors.reshape(-1, total, depth).transpose(1, 0, 2)
    vectors = lax.psum_scatter(vectors, AXES, scatter_dimension=0, tiled=True)[0]
    return (
        mixed,
        grad_tokens,
        vectors[0],
        grad_qkv[0],
        grad_qkv[1],
        grad_qkv[2],
        vectors[1],
        vectors[2],
        vectors[3],
        grad_o,
        vectors[4],
        vectors[5 : 5 + experts].T,
        vectors[5 + experts],
        grad_shared_gu,
        grad_shared_down,
        grad_expert_gu,
        grad_expert_down[None],
    )


def solution(mesh):
    fine = Mesh(mesh.devices.reshape(mesh.devices.size // 4, 2, 2), AXES)
    given = P(None, AXES, None)
    rows = P(AXES, None)
    vector = P(AXES)
    expert = P("dp", ("x", "core"), None)
    in_specs = (
        given,
        given,
        P(),
        P(),
        P(),
        vector,
        rows,
        rows,
        rows,
        vector,
        vector,
        vector,
        rows,
        vector,
        rows,
        vector,
        rows,
        rows,
        expert,
        expert,
    )
    out_specs = (
        given,
        given,
        vector,
        rows,
        rows,
        rows,
        vector,
        vector,
        vector,
        rows,
        vector,
        rows,
        vector,
        rows,
        rows,
        expert,
        expert,
    )
    return jax.shard_map(
        on_device, mesh=fine, in_specs=in_specs, out_specs=out_specs, check_vma=False
    )
```

time: 3820 us -> 1420 us (0.37)
  waiting for transfers between devices: 3010 us -> 565 us
  blocking collectives: 317 us -> 62.1 us
  local copies, waits for them, and re-layouts: 83 us -> 268 us
  other arithmetic: 57.7 us -> 179 us
  starting transfers between devices: 33.3 us -> 123 us
  matrix products: 282 us -> 199 us
    reduce_scatter x10 -> x1, waiting for transfers between devices: 2330 us -> 130 us  [on_device(): lax.psum_scatter(vectors, AXES, scatter_dimension=0, tiled=True)[0]]
    all_gather x10 -> x0, waiting for transfers between devices: 602 us -> none  [the longest x1 177 us: on_device(): lax.all_gather(shared_gate_up, ('dp', 'fsdp'), axis=0, tiled=True)]
    ppermute x0 -> x110, waiting for transfers between devices: none -> 435 us  [permute(): return lax.ppermute(value, AXES, pairs)]
    all_to_all x2 -> x0, blocking collectives: 127 us -> none  [the longest x1 63.8 us: on_device(): lax.all_to_all(send_rows.reshape(expert_count, capacity, model_width), 'd...]
    ppermute x0 -> x110, starting transfers between devices: none -> 105 us  [permute(): return lax.ppermute(value, AXES, pairs)]
    unnamed x2 -> x0, blocking collectives: 81.8 us -> none
    dot_general x35 -> x52, matrix products: 280 us -> 199 us  [the longest x15 78.4 us: mm_tn(): lax.dot_general(a, b, (((0,), (0,)), ((), ())), preferred_element_type=F32)]
    slice x0 -> x37, local copies, waits for them, and re-layouts: none -> 61.6 us  [the longest x12 14.7 us: scatter_bits(): value = add_low(value[0], swap(value[1], bit))]
  transfers between devices with their start and end apart: 27 -> 115, of which waited for: 20 -> 52; matrix products, arithmetic and copies ran while one was open for 7% -> 42% of each run, Pallas kernels for 0% -> 0%
where the time goes in v1:
time: 1420 us; the launch traced here: 1410 us
  waiting for transfers between devices  565 us (40%)
  local copies, waits for them, and re-layouts  268 us (19%)
  matrix products  199 us (14%)
  other arithmetic  179 us (13%)
  starting transfers between devices  123 us (9%)
  blocking collectives  62.1 us (4%)
  between operations  18.4 us (1%)
    ppermute x110, waiting for transfers between devices, permute(): return lax.ppermute(value, AXES, pairs)  435 us
    reduce_scatter x1, waiting for transfers between devices, on_device(): lax.psum_scatter(vectors, AXES, scatter_dimension=0, tiled=True)[0]  130 us
    ppermute x110, starting transfers between devices, permute(): return lax.ppermute(value, AXES, pairs)  105 us
    dot_general x15, matrix products, mm_tn(): lax.dot_general(a, b, (((0,), (0,)), ((), ())), preferred_element_type=F32)  78.4 us
    dot_general x15, matrix products, mm_nt(): lax.dot_general(a, b, (((1,), (1,)), ((), ())), preferred_element_type=F32)  67.6 us
    all_gather x1, blocking collectives, on_device(): small = lax.all_gather(small, AXES, axis=0)  62.1 us
    dot_general x16, matrix products, mm(): lax.dot_general(a, b, (((1,), (0,)), ((), ())), preferred_element_type=F32)  48.1 us
    another operation x3, local copies, waits for them, and re-layouts, by_bit(): return jnp.stack([low, high], axis=axis)  47.7 us
  transfers between devices with their start and end apart: 115, of which 52 were waited for; matrix products, arithmetic and copies ran while one was open for 42% of the time, Pallas kernels for 0%

profile of v1, /device:TPU:0, one launch (start us, length us, event | category | flops | bytes accessed | tf_op | source)
XLA Modules:
  0.0 1414.5 jit_solution(6822125868337956184)
XLA Ops:
  37.0 5.9 all-to-all-start.1
  43.2 62.1 %all-gather = bf16[512,64]{1,0:T(8,128)(2,1)S(1)} all-gather(bf16[16,64]{1,0:T(8,128)(2,1)S(1)} %concatenate.98), channel_id=2, replica_groups=mesh['dp'=8,'x'=2,'core'=2] {'dp','x','core'}, dimensions={0}, use_global_device_ids=true | all-gather | bytes 67584 | tf_op jit(solution)/shard_map/all_gather | solution.py:222
  153.4 6.2 collective-permute-done.6
  159.7 5.4 collective-permute-done.9
  201.0 15.6 %collective-permute-done.11 = bf16[2,2,40,2048]{3,2,1,0:T(8,128)(2,1)S(1)} collective-permute-done((bf16[2,2,40,2048]{3,2,1,0:T(8,128)(2,1)S(1)}, bf16[2,2,40,2048]{3,2,1,0:T(8,128)(2,1)S(1)}, u32[]{:S(2)}, u32[]{:S(2)}) %collective-permute-start.11) | collective-permute-done | bytes 655392 | tf_op jit(solution)/shard_map/ppermute | solution.py:41
  225.5 6.9 reshape.1155
  232.5 6.0 fusion.226
  238.4 8.3 copy.519
  246.8 6.2 copy.528
  257.5 30.0 %copy.501 = bf16[2048,2,384]{2,1,0:T(2,128)(2,1)S(1)} copy(bf16[2048,2,384]{2,0,1:T(8,128)(2,1)S(1)} %get-tuple-element.169) | data formatting | bytes 6291456 | tf_op jit(solution)/shard_map/stack | solution.py:94
  309.9 12.1 collective-permute-done.18
  349.5 15.7 %copy.525 = bf16[2,2,512,2,704]{2,1,0,4,3:T(2,128)(2,1)} copy(bf16[2,2,512,2,704]{2,4,3,0,1:T(8,128)(2,1)S(1)} %pad_maximum_fusion.1) | data formatting | bytes 11534336 | tf_op jit(solution)/shard_map/stack | solution.py:94
  365.2 10.6 reshape.1156
  379.3 6.2 slice_bitcast_fusion.1
  399.3 19.5 %collective-permute-done.39 = bf16[40,2048]{1,0:T(8,128)(2,1)S(1)} collective-permute-done((bf16[40,2048]{1,0:T(8,128)(2,1)S(1)}, bf16[40,2048]{1,0:T(8,128)(2,1)S(1)}, u32[]{:S(2)}, u32[]{:S(2)}) %collective-permute-start.39) | collective-permute-done | bytes 163872 | tf_op jit(solution)/shard_map/ppermute | solution.py:41
  418.8 7.7 collective-permute-done.71
  448.6 4.9 collective-permute-done.27
  455.2 6.4 collective-permute-done.41
  462.7 27.3 %collective-permute-done.49 = bf16[2,2,40,2048]{3,2,1,0:T(8,128)(2,1)S(1)} collective-permute-done((bf16[2,2,40,2048]{3,2,1,0:T(8,128)(2,1)S(1)}, bf16[2,2,40,2048]{3,2,1,0:T(8,128)(2,1)S(1)}, u32[]{:S(2)}, u32[]{:S(2)}) %collective-permute-start.49) | collective-permute-done | bytes 655392 | tf_op jit(solution)/shard_map/ppermute | solution.py:41
  495.0 15.6 %collective-permute-done.57 = bf16[2,2,48,2048]{3,2,1,0:T(8,128)(2,1)S(1)} collective-permute-done((bf16[2,2,48,2048]{3,2,1,0:T(8,128)(2,1)S(1)}, bf16[2,2,48,2048]{3,2,1,0:T(8,128)(2,1)S(1)}, u32[]{:S(2)}, u32[]{:S(2)}) %collective-permute-start.57) | collective-permute-done | bytes 786464 | tf_op jit(solution)/shard_map/ppermute | solution.py:41
  519.9 18.7 %collective-permute-done.50 = bf16[2,2,2,40,2048]{4,3,2,1,0:T(8,128)(2,1)S(1)} collective-permute-done((bf16[2,2,2,40,2048]{4,3,2,1,0:T(8,128)(2,1)S(1)}, bf16[2,2,2,40,2048]{4,3,2,1,0:T(8,128)(2,1)S(1)}, u32[]{:S(2)}, u32[]{:S(2)}) %collective-permute-start.50) | collective-permute-done | bytes 1310752 | tf_op jit(solution)/shard_map/ppermute | solution.py:41
  547.1 16.1 %collective-permute-done.74 = bf16[2,2,2,40,2048]{4,3,2,1,0:T(8,128)(2,1)S(1)} collective-permute-done((bf16[2,2,2,40,2048]{4,3,2,1,0:T(8,128)(2,1)S(1)}, bf16[2,2,2,40,2048]{4,3,2,1,0:T(8,128)(2,1)S(1)}, u32[]{:S(2)}, u32[]{:S(2)}) %collective-permute-start.74) | collective-permute-done | bytes 1310752 | tf_op jit(solution)/shard_map/ppermute | solution.py:41
  575.6 5.6 fusion.216
  581.2 12.1 select_reduce_fusion.5
  595.1 9.3 multiply_convert_fusion.2
  604.4 5.4 fusion.208
  609.8 6.3 fusion.251
  616.1 5.3 fusion.207
  621.4 6.3 fusion.254
  627.7 5.9 add_convert_fusion.2
  636.8 6.0 add_convert_fusion.3
  658.5 6.5 fusion.253
  665.0 6.5 fusion.193
  684.8 8.7 select_reduce_fusion.1
  694.3 7.0 multiply_convert_fusion
  701.4 6.4 fusion.209
  707.8 6.3 fusion.250
  714.1 8.6 add_add_fusion
  724.9 8.5 convolution_convert_fusion
  733.4 6.8 fusion.196
  740.3 6.3 fusion.252
  746.6 7.2 fusion.4
  758.9 8.7 add_convert_fusion
  772.8 6.6 add_convert_fusion.1
  782.2 5.9 copy.591
  788.1 6.4 reshape.1190
  794.6 10.5 reshape.1191
  805.1 11.8 fusion.222
  858.3 11.4 collective-permute-done.76
  871.1 56.4 %collective-permute-done.68 = bf16[2,2,40,2048]{3,2,1,0:T(8,128)(2,1)S(1)} collective-permute-done((bf16[2,2,40,2048]{3,2,1,0:T(8,128)(2,1)S(1)}, bf16[2,2,40,2048]{3,2,1,0:T(8,128)(2,1)S(1)}, u32[]{:S(2)}, u32[]{:S(2)}) %collective-permute-start.68) | collective-permute-done | bytes 655392 | tf_op jit(solution)/shard_map/ppermute | solution.py:41
  930.1 15.1 %collective-permute-done.44 = bf16[2,2,40,2048]{3,2,1,0:T(8,128)(2,1)S(1)} collective-permute-done((bf16[2,2,40,2048]{3,2,1,0:T(8,128)(2,1)S(1)}, bf16[2,2,40,2048]{3,2,1,0:T(8,128)(2,1)S(1)}, u32[]{:S(2)}, u32[]{:S(2)}) %collective-permute-start.44) | collective-permute-done | bytes 655392 | tf_op jit(solution)/shard_map/ppermute | solution.py:41
  962.8 8.9 collective-permute-done.78
  972.5 8.1 collective-permute-done.70
  994.8 6.6 collective-permute-done.61
  1002.4 8.9 collective-permute-done.37
  1025.4 7.7 collective-permute-done.79
  1043.6 15.8 %collective-permute-done.84 = bf16[40,2048]{1,0:T(8,128)(2,1)S(1)} collective-permute-done((bf16[40,2048]{1,0:T(8,128)(2,1)S(1)}, bf16[40,2048]{1,0:T(8,128)(2,1)S(1)}, u32[]{:S(2)}, u32[]{:S(2)}) %collective-permute-start.84) | collective-permute-done | bytes 163872 | tf_op jit(solution)/shard_map/ppermute | solution.py:41
  1074.9 5.4 reshape.1249
  1080.4 5.3 copy.592
  1095.7 6.5 copy.596
  1167.6 11.1 collective-permute-done.94
  1181.1 12.2 collective-permute-done.95
  1214.5 41.8 %collective-permute-done.100 = bf16[2,4,8,2048]{3,2,1,0:T(8,128)(2,1)S(1)} collective-permute-done((bf16[2,4,8,2048]{3,2,1,0:T(8,128)(2,1)S(1)}, bf16[2,4,8,2048]{3,2,1,0:T(8,128)(2,1)S(1)}, u32[]{:S(2)}, u32[]{:S(2)}) %collective-permute-start.100) | collective-permute-done | bytes 262176 | tf_op jit(solution)/shard_map/ppermute | solution.py:41
  1262.1 129.7 %reduce-scatter.2.cloned.1.call-done = f32[1,14,64]{2,1,0:T(8,128)} async-done(((f32[32,14,64]{2,1,0:T(8,128)}), f32[1,14,64]{2,1,0:T(8,128)}) %reduce-scatter.2.cloned.1.call-update) | async-done | bytes 3600 | tf_op jit(solution)/shard_map/reduce_scatter | solution.py:551
  (965 shorter events, 540.8 us)
Async XLA Ops:
  7.2 144.0 %collective-permute-start.12 = (bf16[64,2048]{1,0:T(8,128)(2,1)}, bf16[64,2048]{1,0:T(8,128)(2,1)}, u32[]{:S(2)}, u32[]{:S(2)}) collective-permute-start(bf16[64,2048]{1,0:T(8,128)(2,1)} %param.38), channel_id=1, source_target_pairs={{0,0},{1,1},{2,16},{3,17},{4,2},{5,3},{6,18},{7,19},{8,4},{9,5},{1... | collective-permute-start | bytes 786440 | tf_op jit(solution)/shard_map/ppermute | solution.py:41
  10.8 140.6 %collective-permute-start.13 = (bf16[64,2048]{1,0:T(8,128)(2,1)}, bf16[64,2048]{1,0:T(8,128)(2,1)}, u32[]{:S(2)}, u32[]{:S(2)}) collective-permute-start(bf16[64,2048]{1,0:T(8,128)(2,1)} %param.38), channel_id=1, source_target_pairs={{0,16},{1,17},{2,0},{3,1},{4,18},{5,19},{6,2},{7,3},{8,20},{9,21},... | collective-permute-start | bytes 786440 | tf_op jit(solution)/shard_map/ppermute | solution.py:41
  16.2 133.7 %collective-permute-start = (bf16[2,4,8,2048]{3,2,1,0:T(8,128)(2,1)}, bf16[2,4,8,2048]{3,2,1,0:T(8,128)(2,1)}, u32[]{:S(2)}, u32[]{:S(2)}) collective-permute-start(bf16[2,4,8,2048]{3,2,1,0:T(8,128)(2,1)} %pad_maximum_fusion.72), channel_id=1, source_target_pairs={{0,16},{1,17},{2,18},{3,19},{4,20},{5,21},{6,22},{7,23},{8,24},{9,... | collective-permute-start | bytes 786440 | tf_op jit(solution)/shard_map/ppermute | solution.py:41
  23.0 166.6 %collective-permute-start.31 = (bf16[512,2,704]{0,2,1:T(8,128)(2,1)}, bf16[512,2,704]{0,2,1:T(8,128)(2,1)}, u32[]{:S(2)}, u32[]{:S(2)}) collective-permute-start(bf16[512,2,704]{0,2,1:T(8,128)(2,1)} %fusion.50), channel_id=1, source_target_pairs={{0,2},{1,3},{2,0},{3,1},{4,6},{5,7},{6,4},{7,5},{8,10},{9,11},{10,... | collective-permute-start | bytes 4325384 | tf_op jit(solution)/shard_map/ppermute | solution.py:41
  37.0 140.7 %all-to-all-start.1 = ((bf16[16,64,704]{2,1,0:T(8,128)(2,1)}), bf16[16,64,704]{2,1,0:T(8,128)(2,1)}, u32[]{:S(2)}, u32[]{:S(2)}) async-start(bf16[16,64,704]{2,1,0:T(8,128)(2,1)} %reshape.1154), calls=%async_computation.1 | async-start | bytes 3145728 | tf_op jit(solution)/shard_map/all_to_all | solution.py:272
  42.9 150.8 %collective-permute-start.34 = (bf16[352,2048]{1,0:T(8,128)(2,1)}, bf16[352,2048]{1,0:T(8,128)(2,1)}, u32[]{:S(2)}, u32[]{:S(2)}) collective-permute-start(bf16[352,2048]{1,0:T(8,128)(2,1)} %bitcast.991), channel_id=1, source_target_pairs={{0,1},{1,0},{2,3},{3,2},{4,5},{5,4},{6,7},{7,6},{8,9},{9,8},{10,11... | collective-permute-start | bytes 4325384 | tf_op jit(solution)/shard_map/ppermute | solution.py:41
  152.8 20.1 %collective-permute-start.14 = (bf16[2,64,2048]{2,1,0:T(8,128)(2,1)S(1)}, bf16[2,64,2048]{2,1,0:T(8,128)(2,1)S(1)}, u32[]{:S(2)}, u32[]{:S(2)}) collective-permute-start(bf16[2,64,2048]{2,1,0:T(8,128)(2,1)S(1)} %pad_maximum_fusion.42), channel_id=1, source_target_pairs={{0,1},{1,0},{2,3},{3,2},{4,5},{5,4},{6,7},{7,6},{8,9},{9,8},{10,11... | collective-permute-start | bytes 1572872 | tf_op jit(solution)/shard_map/ppermute | solution.py:41
  175.8 23.8 %collective-permute-start.8 = (bf16[2,2,40,2048]{3,2,1,0:T(8,128)(2,1)}, bf16[2,2,40,2048]{3,2,1,0:T(8,128)(2,1)}, u32[]{:S(2)}, u32[]{:S(2)}) collective-permute-start(bf16[2,2,40,2048]{3,2,1,0:T(8,128)(2,1)} %get-tuple-element.253), channel_id=1, source_target_pairs={{0,8},{1,9},{2,10},{3,11},{4,12},{5,13},{6,14},{7,15},{8,0},{9,1},... | collective-permute-start | bytes 1966088 | tf_op jit(solution)/shard_map/ppermute | solution.py:41
  180.1 41.4 %all-to-all-start = ((bf16[32,64,384]{2,1,0:T(8,128)(2,1)}), bf16[32,64,384]{2,1,0:T(8,128)(2,1)}, u32[]{:S(2)}, u32[]{:S(2)}) async-start(bf16[32,64,384]{2,1,0:T(8,128)(2,1)} %bitcast.913), calls=%async_computation | async-start | bytes 3145728 | tf_op jit(solution)/shard_map/all_to_all | solution.py:239
  184.9 31.7 %collective-permute-start.11 = (bf16[2,2,40,2048]{3,2,1,0:T(8,128)(2,1)S(1)}, bf16[2,2,40,2048]{3,2,1,0:T(8,128)(2,1)S(1)}, u32[]{:S(2)}, u32[]{:S(2)}) collective-permute-start(bf16[2,2,40,2048]{3,2,1,0:T(8,128)(2,1)S(1)} %get-tuple-element.255), channel_id=1, source_target_pairs={{0,2},{1,3},{2,0},{3,1},{4,6},{5,7},{6,4},{7,5},{8,10},{9,11},{10,... | collective-permute-start | bytes 1966088 | tf_op jit(solution)/shard_map/ppermute | solution.py:41
  188.0 32.2 %collective-permute-start.4 = (bf16[2,2,48,2048]{3,2,1,0:T(8,128)(2,1)S(1)}, bf16[2,2,48,2048]{3,2,1,0:T(8,128)(2,1)S(1)}, u32[]{:S(2)}, u32[]{:S(2)}) collective-permute-start(bf16[2,2,48,2048]{3,2,1,0:T(8,128)(2,1)S(1)} %get-tuple-element.243), channel_id=1, source_target_pairs={{0,4},{1,5},{2,6},{3,7},{4,0},{5,1},{6,2},{7,3},{8,12},{9,13},{10,... | collective-permute-start | bytes 2359304 | tf_op jit(solution)/shard_map/ppermute | solution.py:41
  193.7 153.2 %collective-permute-start.32 = (bf16[2,512,2,704]{1,3,2,0:T(8,128)(2,1)}, bf16[2,512,2,704]{1,3,2,0:T(8,128)(2,1)}, u32[]{:S(2)}, u32[]{:S(2)}) collective-permute-start(bf16[2,512,2,704]{1,3,2,0:T(8,128)(2,1)} %pad_maximum_fusion.9), channel_id=1, source_target_pairs={{0,1},{1,0},{2,3},{3,2},{4,5},{5,4},{6,7},{7,6},{8,9},{9,8},{10,11... | collective-permute-start | bytes 8650760 | tf_op jit(solution)/shard_map/ppermute | solution.py:41
  195.3 26.4 %collective-permute-start.30 = (bf16[16,64,704]{2,1,0:T(8,128)(2,1)}, bf16[16,64,704]{2,1,0:T(8,128)(2,1)S(1)}, u32[]{:S(2)}, u32[]{:S(2)}) collective-permute-start(bf16[16,64,704]{2,1,0:T(8,128)(2,1)} %all-to-all-done.1), channel_id=1, source_target_pairs={{0,1},{1,0},{2,3},{3,2},{4,5},{5,4},{6,7},{7,6},{8,9},{9,8},{10,11... | collective-permute-start | bytes 4325384 | tf_op jit(solution)/shard_map/ppermute | solution.py:41
  221.5 31.5 %collective-permute-start.5 = (bf16[2048,384]{1,0:T(8,128)(2,1)}, bf16[2048,384]{1,0:T(8,128)(2,1)}, u32[]{:S(2)}, u32[]{:S(2)}) collective-permute-start(bf16[2048,384]{1,0:T(8,128)(2,1)} %bitcast.23), channel_id=1, source_target_pairs={{0,1},{1,0},{2,3},{3,2},{4,5},{5,4},{6,7},{7,6},{8,9},{9,8},{10,11... | collective-permute-start | bytes 4718600 | tf_op jit(solution)/shard_map/ppermute | solution.py:41
  306.8 20.4 %collective-permute-start.15 = (bf16[2,2,48,2048]{3,2,1,0:T(8,128)(2,1)S(1)}, bf16[2,2,48,2048]{3,2,1,0:T(8,128)(2,1)S(1)}, u32[]{:S(2)}, u32[]{:S(2)}) collective-permute-start(bf16[2,2,48,2048]{3,2,1,0:T(8,128)(2,1)S(1)} %bitcast.1019), channel_id=1, source_target_pairs={{0,4},{1,5},{2,6},{3,7},{4,0},{5,1},{6,2},{7,3},{8,12},{9,13},{10,... | collective-permute-start | bytes 2359304 | tf_op jit(solution)/shard_map/ppermute | solution.py:41
  346.8 29.0 %collective-permute-start.24 = (bf16[2,4,8,2048]{3,2,1,0:T(8,128)(2,1)S(1)}, bf16[2,4,8,2048]{3,2,1,0:T(8,128)(2,1)S(1)}, u32[]{:S(2)}, u32[]{:S(2)}) collective-permute-start(bf16[2,4,8,2048]{3,2,1,0:T(8,128)(2,1)S(1)} %bitcast.1055), channel_id=1, source_target_pairs={{0,1},{1,0},{2,3},{3,2},{4,5},{5,4},{6,7},{7,6},{8,9},{9,8},{10,11... | collective-permute-start | bytes 786440 | tf_op jit(solution)/shard_map/ppermute | solution.py:41
  393.1 25.7 %collective-permute-start.39 = (bf16[40,2048]{1,0:T(8,128)(2,1)S(1)}, bf16[40,2048]{1,0:T(8,128)(2,1)S(1)}, u32[]{:S(2)}, u32[]{:S(2)}) collective-permute-start(bf16[40,2048]{1,0:T(8,128)(2,1)S(1)} %get-tuple-element.287), channel_id=1, source_target_pairs={{0,16},{1,17},{2,18},{3,19},{4,20},{5,21},{6,22},{7,23},{8,24},{9,... | collective-permute-start | bytes 491528 | tf_op jit(solution)/shard_map/ppermute | solution.py:41
  393.3 33.2 %collective-permute-start.71 = (bf16[40,2048]{1,0:T(8,128)(2,1)S(1)}, bf16[40,2048]{1,0:T(8,128)(2,1)S(1)}, u32[]{:S(2)}, u32[]{:S(2)}) collective-permute-start(bf16[40,2048]{1,0:T(8,128)(2,1)S(1)} %get-tuple-element.312), channel_id=1, source_target_pairs={{0,16},{1,17},{2,18},{3,19},{4,20},{5,21},{6,22},{7,23},{8,24},{9,... | collective-permute-start | bytes 491528 | tf_op jit(solution)/shard_map/ppermute | solution.py:41
  396.3 33.7 %collective-permute-start.47 = (bf16[40,2048]{1,0:T(8,128)(2,1)S(1)}, bf16[40,2048]{1,0:T(8,128)(2,1)S(1)}, u32[]{:S(2)}, u32[]{:S(2)}) collective-permute-start(bf16[40,2048]{1,0:T(8,128)(2,1)S(1)} %get-tuple-element.286), channel_id=1, source_target_pairs={{0,16},{1,17},{2,18},{3,19},{4,20},{5,21},{6,22},{7,23},{8,24},{9,... | collective-permute-start | bytes 491528 | tf_op jit(solution)/shard_map/ppermute | solution.py:41
  396.4 37.2 %collective-permute-start.63 = (bf16[40,2048]{1,0:T(8,128)(2,1)S(1)}, bf16[40,2048]{1,0:T(8,128)(2,1)S(1)}, u32[]{:S(2)}, u32[]{:S(2)}) collective-permute-start(bf16[40,2048]{1,0:T(8,128)(2,1)S(1)} %get-tuple-element.311), channel_id=1, source_target_pairs={{0,16},{1,17},{2,18},{3,19},{4,20},{5,21},{6,22},{7,23},{8,24},{9,... | collective-permute-start | bytes 491528 | tf_op jit(solution)/shard_map/ppermute | solution.py:41
  399.2 38.5 %collective-permute-start.26 = (bf16[48,2048]{1,0:T(8,128)(2,1)S(1)}, bf16[48,2048]{1,0:T(8,128)(2,1)S(1)}, u32[]{:S(2)}, u32[]{:S(2)}) collective-permute-start(bf16[48,2048]{1,0:T(8,128)(2,1)S(1)} %get-tuple-element.281), channel_id=1, source_target_pairs={{0,16},{1,17},{2,18},{3,19},{4,20},{5,21},{6,22},{7,23},{8,24},{9,... | collective-permute-start | bytes 589832 | tf_op jit(solution)/shard_map/ppermute | solution.py:41
  418.8 22.7 %collective-permute-start.55 = (bf16[48,2048]{1,0:T(8,128)(2,1)S(1)}, bf16[48,2048]{1,0:T(8,128)(2,1)S(1)}, u32[]{:S(2)}, u32[]{:S(2)}) collective-permute-start(bf16[48,2048]{1,0:T(8,128)(2,1)S(1)} %get-tuple-element.283), channel_id=1, source_target_pairs={{0,16},{1,17},{2,18},{3,19},{4,20},{5,21},{6,22},{7,23},{8,24},{9,... | collective-permute-start | bytes 589832 | tf_op jit(solution)/shard_map/ppermute | solution.py:41
  441.6 20.9 %collective-permute-start.56 = (bf16[2,48,2048]{2,1,0:T(8,128)(2,1)S(1)}, bf16[2,48,2048]{2,1,0:T(8,128)(2,1)S(1)}, u32[]{:S(2)}, u32[]{:S(2)}) collective-permute-start(bf16[2,48,2048]{2,1,0:T(8,128)(2,1)S(1)} %get-tuple-element.319), channel_id=1, source_target_pairs={{0,8},{1,9},{2,10},{3,11},{4,12},{5,13},{6,14},{7,15},{8,0},{9,1},... | collective-permute-start | bytes 1179656 | tf_op jit(solution)/shard_map/ppermute | solution.py:41
  446.3 44.7 %collective-permute-start.73 = (bf16[2,2,40,2048]{3,2,1,0:T(8,128)(2,1)S(1)}, bf16[2,2,40,2048]{3,2,1,0:T(8,128)(2,1)S(1)}, u32[]{:S(2)}, u32[]{:S(2)}) collective-permute-start(bf16[2,2,40,2048]{3,2,1,0:T(8,128)(2,1)S(1)} %get-tuple-element.257), channel_id=1, source_target_pairs={{0,8},{1,9},{2,10},{3,11},{4,12},{5,13},{6,14},{7,15},{8,0},{9,1},... | collective-permute-start | bytes 1966088 | tf_op jit(solution)/shard_map/ppermute | solution.py:41
  446.6 43.5 %collective-permute-start.49 = (bf16[2,2,40,2048]{3,2,1,0:T(8,128)(2,1)S(1)}, bf16[2,2,40,2048]{3,2,1,0:T(8,128)(2,1)S(1)}, u32[]{:S(2)}, u32[]{:S(2)}) collective-permute-start(bf16[2,2,40,2048]{3,2,1,0:T(8,128)(2,1)S(1)} %get-tuple-element.249), channel_id=1, source_target_pairs={{0,8},{1,9},{2,10},{3,11},{4,12},{5,13},{6,14},{7,15},{8,0},{9,1},... | collective-permute-start | bytes 1966088 | tf_op jit(solution)/shard_map/ppermute | solution.py:41
  453.5 39.0 %collective-permute-start.65 = (bf16[2,2,40,2048]{3,2,1,0:T(8,128)(2,1)S(1)}, bf16[2,2,40,2048]{3,2,1,0:T(8,128)(2,1)S(1)}, u32[]{:S(2)}, u32[]{:S(2)}) collective-permute-start(bf16[2,2,40,2048]{3,2,1,0:T(8,128)(2,1)S(1)} %get-tuple-element.259), channel_id=1, source_target_pairs={{0,4},{1,5},{2,6},{3,7},{4,0},{5,1},{6,2},{7,3},{8,12},{9,13},{10,... | collective-permute-start | bytes 1966088 | tf_op jit(solution)/shard_map/ppermute | solution.py:41
  461.5 32.0 %collective-permute-start.28 = (bf16[2,2,48,2048]{3,2,1,0:T(8,128)(2,1)S(1)}, bf16[2,2,48,2048]{3,2,1,0:T(8,128)(2,1)S(1)}, u32[]{:S(2)}, u32[]{:S(2)}) collective-permute-start(bf16[2,2,48,2048]{3,2,1,0:T(8,128)(2,1)S(1)} %get-tuple-element.239), channel_id=1, source_target_pairs={{0,2},{1,3},{2,0},{3,1},{4,6},{5,7},{6,4},{7,5},{8,10},{9,11},{10,... | collective-permute-start | bytes 2359304 | tf_op jit(solution)/shard_map/ppermute | solution.py:41
  462.5 55.6 %collective-permute-start.42 = (bf16[2,2,2,40,2048]{4,3,2,1,0:T(8,128)(2,1)S(1)}, bf16[2,2,2,40,2048]{4,3,2,1,0:T(8,128)(2,1)S(1)}, u32[]{:S(2)}, u32[]{:S(2)}) collective-permute-start(bf16[2,2,2,40,2048]{4,3,2,1,0:T(8,128)(2,1)S(1)} %get-tuple-element.214), channel_id=1, source_target_pairs={{0,8},{1,9},{2,10},{3,11},{4,12},{5,13},{6,14},{7,15},{8,0},{9,1},... | collective-permute-start | bytes 3932168 | tf_op jit(solution)/shard_map/ppermute | solution.py:41
  490.1 20.5 %collective-permute-start.57 = (bf16[2,2,48,2048]{3,2,1,0:T(8,128)(2,1)S(1)}, bf16[2,2,48,2048]{3,2,1,0:T(8,128)(2,1)S(1)}, u32[]{:S(2)}, u32[]{:S(2)}) collective-permute-start(bf16[2,2,48,2048]{3,2,1,0:T(8,128)(2,1)S(1)} %get-tuple-element.241), channel_id=1, source_target_pairs={{0,2},{1,3},{2,0},{3,1},{4,6},{5,7},{6,4},{7,5},{8,10},{9,11},{10,... | collective-permute-start | bytes 2359304 | tf_op jit(solution)/shard_map/ppermute | solution.py:41
  491.0 47.6 %collective-permute-start.50 = (bf16[2,2,2,40,2048]{4,3,2,1,0:T(8,128)(2,1)S(1)}, bf16[2,2,2,40,2048]{4,3,2,1,0:T(8,128)(2,1)S(1)}, u32[]{:S(2)}, u32[]{:S(2)}) collective-permute-start(bf16[2,2,2,40,2048]{4,3,2,1,0:T(8,128)(2,1)S(1)} %get-tuple-element.212), channel_id=1, source_target_pairs={{0,2},{1,3},{2,0},{3,1},{4,6},{5,7},{6,4},{7,5},{8,10},{9,11},{10,... | collective-permute-start | bytes 3932168 | tf_op jit(solution)/shard_map/ppermute | solution.py:41
  492.5 70.6 %collective-permute-start.74 = (bf16[2,2,2,40,2048]{4,3,2,1,0:T(8,128)(2,1)S(1)}, bf16[2,2,2,40,2048]{4,3,2,1,0:T(8,128)(2,1)S(1)}, u32[]{:S(2)}, u32[]{:S(2)}) collective-permute-start(bf16[2,2,2,40,2048]{4,3,2,1,0:T(8,128)(2,1)S(1)} %get-tuple-element.220), channel_id=1, source_target_pairs={{0,2},{1,3},{2,0},{3,1},{4,6},{5,7},{6,4},{7,5},{8,10},{9,11},{10,... | collective-permute-start | bytes 3932168 | tf_op jit(solution)/shard_map/ppermute | solution.py:41
  493.5 77.8 %collective-permute-start.66 = (bf16[2,2,2,40,2048]{4,3,2,1,0:T(8,128)(2,1)S(1)}, bf16[2,2,2,40,2048]{4,3,2,1,0:T(8,128)(2,1)S(1)}, u32[]{:S(2)}, u32[]{:S(2)}) collective-permute-start(bf16[2,2,2,40,2048]{4,3,2,1,0:T(8,128)(2,1)S(1)} %get-tuple-element.222), channel_id=1, source_target_pairs={{0,8},{1,9},{2,10},{3,11},{4,12},{5,13},{6,14},{7,15},{8,0},{9,1},... | collective-permute-start | bytes 3932168 | tf_op jit(solution)/shard_map/ppermute | solution.py:41
  510.5 161.0 %collective-permute-start.29 = (bf16[2,2,2,48,2048]{4,3,2,1,0:T(8,128)(2,1)}, bf16[2,2,2,48,2048]{4,3,2,1,0:T(8,128)(2,1)}, u32[]{:S(2)}, u32[]{:S(2)}) collective-permute-start(bf16[2,2,2,48,2048]{4,3,2,1,0:T(8,128)(2,1)} %get-tuple-element.200), channel_id=1, source_target_pairs={{0,4},{1,5},{2,6},{3,7},{4,0},{5,1},{6,2},{7,3},{8,12},{9,13},{10,... | collective-permute-start | bytes 4718600 | tf_op jit(solution)/shard_map/ppermute | solution.py:41
  518.1 163.7 %collective-permute-start.58 = (bf16[2,2,2,48,2048]{4,3,2,1,0:T(8,128)(2,1)}, bf16[2,2,2,48,2048]{4,3,2,1,0:T(8,128)(2,1)}, u32[]{:S(2)}, u32[]{:S(2)}) collective-permute-start(bf16[2,2,2,48,2048]{4,3,2,1,0:T(8,128)(2,1)} %get-tuple-element.202), channel_id=1, source_target_pairs={{0,4},{1,5},{2,6},{3,7},{4,0},{5,1},{6,2},{7,3},{8,12},{9,13},{10,... | collective-permute-start | bytes 4718600 | tf_op jit(solution)/shard_map/ppermute | solution.py:41
  635.3 195.3 %collective-permute-start.75 = (bf16[2,2,2,40,2048]{4,3,2,1,0:T(8,128)(2,1)}, bf16[2,2,2,40,2048]{4,3,2,1,0:T(8,128)(2,1)}, u32[]{:S(2)}, u32[]{:S(2)}) collective-permute-start(bf16[2,2,2,40,2048]{4,3,2,1,0:T(8,128)(2,1)} %bitcast.223), channel_id=1, source_target_pairs={{0,2},{1,3},{2,0},{3,1},{4,6},{5,7},{6,4},{7,5},{8,10},{9,11},{10,... | collective-permute-start | bytes 3932168 | tf_op jit(solution)/shard_map/ppermute | solution.py:41
  644.5 189.3 %collective-permute-start.67 = (bf16[2,2,2,40,2048]{4,3,2,1,0:T(8,128)(2,1)}, bf16[2,2,2,40,2048]{4,3,2,1,0:T(8,128)(2,1)}, u32[]{:S(2)}, u32[]{:S(2)}) collective-permute-start(bf16[2,2,2,40,2048]{4,3,2,1,0:T(8,128)(2,1)} %bitcast.205), channel_id=1, source_target_pairs={{0,8},{1,9},{2,10},{3,11},{4,12},{5,13},{6,14},{7,15},{8,0},{9,1},... | collective-permute-start | bytes 3932168 | tf_op jit(solution)/shard_map/ppermute | solution.py:41
  651.7 185.1 %collective-permute-start.51 = (bf16[2,2,2,40,2048]{4,3,2,1,0:T(8,128)(2,1)}, bf16[2,2,2,40,2048]{4,3,2,1,0:T(8,128)(2,1)}, u32[]{:S(2)}, u32[]{:S(2)}) collective-permute-start(bf16[2,2,2,40,2048]{4,3,2,1,0:T(8,128)(2,1)} %bitcast.168), channel_id=1, source_target_pairs={{0,2},{1,3},{2,0},{3,1},{4,6},{5,7},{6,4},{7,5},{8,10},{9,11},{10,... | collective-permute-start | bytes 3932168 | tf_op jit(solution)/shard_map/ppermute | solution.py:41
  671.5 168.4 %collective-permute-start.43 = (bf16[2,2,2,40,2048]{4,3,2,1,0:T(8,128)(2,1)}, bf16[2,2,2,40,2048]{4,3,2,1,0:T(8,128)(2,1)}, u32[]{:S(2)}, u32[]{:S(2)}) collective-permute-start(bf16[2,2,2,40,2048]{4,3,2,1,0:T(8,128)(2,1)} %bitcast.151), channel_id=1, source_target_pairs={{0,8},{1,9},{2,10},{3,11},{4,12},{5,13},{6,14},{7,15},{8,0},{9,1},... | collective-permute-start | bytes 3932168 | tf_op jit(solution)/shard_map/ppermute | solution.py:41
  794.5 31.4 %collective-permute-start.106 = (bf16[176,2048]{1,0:T(8,128)(2,1)}, bf16[176,2048]{1,0:T(8,128)(2,1)}, u32[]{:S(2)}, u32[]{:S(2)}) collective-permute-start(bf16[176,2048]{1,0:T(8,128)(2,1)} %broadcast_select_fusion.2), channel_id=1, source_target_pairs={{0,1},{1,0},{2,3},{3,2},{4,5},{5,4},{6,7},{7,6},{8,9},{9,8},{10,11... | collective-permute-start | bytes 2162696 | tf_op jit(solution)/shard_map/ppermute | solution.py:41
  825.9 120.5 %collective-permute-start.59 = (bf16[2,2,2,48,2048]{4,3,2,1,0:T(8,128)(2,1)}, bf16[2,2,2,48,2048]{4,3,2,1,0:T(8,128)(2,1)}, u32[]{:S(2)}, u32[]{:S(2)}) collective-permute-start(bf16[2,2,2,48,2048]{4,3,2,1,0:T(8,128)(2,1)} %bitcast.187), channel_id=1, source_target_pairs={{0,4},{1,5},{2,6},{3,7},{4,0},{5,1},{6,2},{7,3},{8,12},{9,13},{10,... | collective-permute-start | bytes 4718600 | tf_op jit(solution)/shard_map/ppermute | solution.py:41
  830.6 119.9 %collective-permute-start.35 = (bf16[2,2,2,48,2048]{4,3,2,1,0:T(8,128)(2,1)}, bf16[2,2,2,48,2048]{4,3,2,1,0:T(8,128)(2,1)}, u32[]{:S(2)}, u32[]{:S(2)}) collective-permute-start(bf16[2,2,2,48,2048]{4,3,2,1,0:T(8,128)(2,1)} %bitcast.134), channel_id=1, source_target_pairs={{0,4},{1,5},{2,6},{3,7},{4,0},{5,1},{6,2},{7,3},{8,12},{9,13},{10,... | collective-permute-start | bytes 4718600 | tf_op jit(solution)/shard_map/ppermute | solution.py:41
  839.9 172.3 %collective-permute-start.107 = (bf16[2,512,2,704]{1,3,2,0:T(8,128)(2,1)}, bf16[2,512,2,704]{1,3,2,0:T(8,128)(2,1)}, u32[]{:S(2)}, u32[]{:S(2)}) collective-permute-start(bf16[2,512,2,704]{1,3,2,0:T(8,128)(2,1)} %select_bitcast_fusion), channel_id=1, source_target_pairs={{0,1},{1,0},{2,3},{3,2},{4,5},{5,4},{6,7},{7,6},{8,9},{9,8},{10,11... | collective-permute-start | bytes 8650760 | tf_op jit(solution)/shard_map/ppermute | solution.py:41
  843.4 26.3 %collective-permute-start.76 = (bf16[2,2,40,2048]{3,2,1,0:T(8,128)(2,1)}, bf16[2,2,40,2048]{3,2,1,0:T(8,128)(2,1)}, u32[]{:S(2)}, u32[]{:S(2)}) collective-permute-start(bf16[2,2,40,2048]{3,2,1,0:T(8,128)(2,1)} %slice_bitcast_fusion.6), channel_id=1, source_target_pairs={{0,8},{1,9},{2,10},{3,11},{4,12},{5,13},{6,14},{7,15},{8,0},{9,1},... | collective-permute-start | bytes 1966088 | tf_op jit(solution)/shard_map/ppermute | solution.py:41
  846.7 228.2 %all-to-all-start.3 = ((bf16[16,64,704]{2,1,0:T(8,128)(2,1)}), bf16[16,64,704]{2,1,0:T(8,128)(2,1)}, u32[]{:S(2)}, u32[]{:S(2)}) async-start(bf16[16,64,704]{2,1,0:T(8,128)(2,1)} %fusion.12), calls=%async_computation.4 | async-start | bytes 3145728 | tf_op jit(solution)/shard_map/all_to_all | solution.py:511
  851.7 75.8 %collective-permute-start.68 = (bf16[2,2,40,2048]{3,2,1,0:T(8,128)(2,1)S(1)}, bf16[2,2,40,2048]{3,2,1,0:T(8,128)(2,1)S(1)}, u32[]{:S(2)}, u32[]{:S(2)}) collective-permute-start(bf16[2,2,40,2048]{3,2,1,0:T(8,128)(2,1)S(1)} %copy-done.119), channel_id=1, source_target_pairs={{0,4},{1,5},{2,6},{3,7},{4,0},{5,1},{6,2},{7,3},{8,12},{9,13},{10,... | collective-permute-start | bytes 1966088 | tf_op jit(solution)/shard_map/ppermute | solution.py:41
  869.7 59.7 %collective-permute-start.52 = (bf16[2,2,40,2048]{3,2,1,0:T(8,128)(2,1)S(1)}, bf16[2,2,40,2048]{3,2,1,0:T(8,128)(2,1)S(1)}, u32[]{:S(2)}, u32[]{:S(2)}) collective-permute-start(bf16[2,2,40,2048]{3,2,1,0:T(8,128)(2,1)S(1)} %copy-done.120), channel_id=1, source_target_pairs={{0,8},{1,9},{2,10},{3,11},{4,12},{5,13},{6,14},{7,15},{8,0},{9,1},... | collective-permute-start | bytes 1966088 | tf_op jit(solution)/shard_map/ppermute | solution.py:41
  929.4 24.2 %collective-permute-start.77 = (bf16[2,40,2048]{2,1,0:T(8,128)(2,1)S(1)}, bf16[2,40,2048]{2,1,0:T(8,128)(2,1)S(1)}, u32[]{:S(2)}, u32[]{:S(2)}) collective-permute-start(bf16[2,40,2048]{2,1,0:T(8,128)(2,1)S(1)} %slice_bitcast_fusion.26), channel_id=1, source_target_pairs={{0,4},{1,5},{2,6},{3,7},{4,0},{5,1},{6,2},{7,3},{8,12},{9,13},{10,... | collective-permute-start | bytes 983048 | tf_op jit(solution)/shard_map/ppermute | solution.py:41
  953.6 35.4 %collective-permute-start.60 = (bf16[2,2,48,2048]{3,2,1,0:T(8,128)(2,1)S(1)}, bf16[2,2,48,2048]{3,2,1,0:T(8,128)(2,1)S(1)}, u32[]{:S(2)}, u32[]{:S(2)}) collective-permute-start(bf16[2,2,48,2048]{3,2,1,0:T(8,128)(2,1)S(1)} %slice_bitcast_fusion.2), channel_id=1, source_target_pairs={{0,2},{1,3},{2,0},{3,1},{4,6},{5,7},{6,4},{7,5},{8,10},{9,11},{10,... | collective-permute-start | bytes 2359304 | tf_op jit(solution)/shard_map/ppermute | solution.py:41
  954.9 38.2 %collective-permute-start.36 = (bf16[2,2,48,2048]{3,2,1,0:T(8,128)(2,1)S(1)}, bf16[2,2,48,2048]{3,2,1,0:T(8,128)(2,1)S(1)}, u32[]{:S(2)}, u32[]{:S(2)}) collective-permute-start(bf16[2,2,48,2048]{3,2,1,0:T(8,128)(2,1)S(1)} %slice_bitcast_fusion.4), channel_id=1, source_target_pairs={{0,2},{1,3},{2,0},{3,1},{4,6},{5,7},{6,4},{7,5},{8,10},{9,11},{10,... | collective-permute-start | bytes 2359304 | tf_op jit(solution)/shard_map/ppermute | solution.py:41
  1012.1 21.7 %collective-permute-start.38 = (bf16[48,2048]{1,0:T(8,128)(2,1)}, bf16[48,2048]{1,0:T(8,128)(2,1)}, u32[]{:S(2)}, u32[]{:S(2)}) collective-permute-start(bf16[48,2048]{1,0:T(8,128)(2,1)} %slice_bitcast_fusion.42), channel_id=1, source_target_pairs={{0,16},{1,17},{2,18},{3,19},{4,20},{5,21},{6,22},{7,23},{8,24},{9,... | collective-permute-start | bytes 589832 | tf_op jit(solution)/shard_map/ppermute | solution.py:41
  1024.2 66.3 %collective-permute-start.108 = (bf16[512,2,704]{0,2,1:T(8,128)(2,1)}, bf16[512,2,704]{0,2,1:T(8,128)(2,1)}, u32[]{:S(2)}, u32[]{:S(2)}) collective-permute-start(bf16[512,2,704]{0,2,1:T(8,128)(2,1)} %select_bitcast_fusion.9), channel_id=1, source_target_pairs={{0,2},{1,3},{2,0},{3,1},{4,6},{5,7},{6,4},{7,5},{8,10},{9,11},{10,... | collective-permute-start | bytes 4325384 | tf_op jit(solution)/shard_map/ppermute | solution.py:41
  1038.3 21.1 %collective-permute-start.84 = (bf16[40,2048]{1,0:T(8,128)(2,1)S(1)}, bf16[40,2048]{1,0:T(8,128)(2,1)S(1)}, u32[]{:S(2)}, u32[]{:S(2)}) collective-permute-start(bf16[40,2048]{1,0:T(8,128)(2,1)S(1)} %get-tuple-element.273), channel_id=1, source_target_pairs={{0,2},{1,3},{2,0},{3,1},{4,6},{5,7},{6,4},{7,5},{8,10},{9,11},{10,... | collective-permute-start | bytes 491528 | tf_op jit(solution)/shard_map/ppermute | solution.py:41
  1061.9 40.4 %collective-permute-start.89 = (bf16[2,2,40,2048]{3,2,1,0:T(8,128)(2,1)}, bf16[2,2,40,2048]{3,2,1,0:T(8,128)(2,1)}, u32[]{:S(2)}, u32[]{:S(2)}) collective-permute-start(bf16[2,2,40,2048]{3,2,1,0:T(8,128)(2,1)} %get-tuple-element.247), channel_id=1, source_target_pairs={{0,2},{1,3},{2,0},{3,1},{4,6},{5,7},{6,4},{7,5},{8,10},{9,11},{10,... | collective-permute-start | bytes 1966088 | tf_op jit(solution)/shard_map/ppermute | solution.py:41
  1067.7 36.4 %collective-permute-start.86 = (bf16[2,2,40,2048]{3,2,1,0:T(8,128)(2,1)}, bf16[2,2,40,2048]{3,2,1,0:T(8,128)(2,1)}, u32[]{:S(2)}, u32[]{:S(2)}) collective-permute-start(bf16[2,2,40,2048]{3,2,1,0:T(8,128)(2,1)} %get-tuple-element.245), channel_id=1, source_target_pairs={{0,8},{1,9},{2,10},{3,11},{4,12},{5,13},{6,14},{7,15},{8,0},{9,1},... | collective-permute-start | bytes 1966088 | tf_op jit(solution)/shard_map/ppermute | solution.py:41
  1072.9 39.5 %collective-permute-start.83 = (bf16[2,2,48,2048]{3,2,1,0:T(8,128)(2,1)}, bf16[2,2,48,2048]{3,2,1,0:T(8,128)(2,1)}, u32[]{:S(2)}, u32[]{:S(2)}) collective-permute-start(bf16[2,2,48,2048]{3,2,1,0:T(8,128)(2,1)} %get-tuple-element.237), channel_id=1, source_target_pairs={{0,4},{1,5},{2,6},{3,7},{4,0},{5,1},{6,2},{7,3},{8,12},{9,13},{10,... | collective-permute-start | bytes 2359304 | tf_op jit(solution)/shard_map/ppermute | solution.py:41
  1133.4 22.9 %collective-permute-start.93 = (bf16[2,2,40,2048]{3,2,1,0:T(8,128)(2,1)}, bf16[2,2,40,2048]{3,2,1,0:T(8,128)(2,1)}, u32[]{:S(2)}, u32[]{:S(2)}) collective-permute-start(bf16[2,2,40,2048]{3,2,1,0:T(8,128)(2,1)} %bitcast.286), channel_id=1, source_target_pairs={{0,8},{1,9},{2,10},{3,11},{4,12},{5,13},{6,14},{7,15},{8,0},{9,1},... | collective-permute-start | bytes 1966088 | tf_op jit(solution)/shard_map/ppermute | solution.py:41
  1136.4 28.5 %collective-permute-start.90 = (bf16[2,2,48,2048]{3,2,1,0:T(8,128)(2,1)}, bf16[2,2,48,2048]{3,2,1,0:T(8,128)(2,1)}, u32[]{:S(2)}, u32[]{:S(2)}) collective-permute-start(bf16[2,2,48,2048]{3,2,1,0:T(8,128)(2,1)} %bitcast.279), channel_id=1, source_target_pairs={{0,4},{1,5},{2,6},{3,7},{4,0},{5,1},{6,2},{7,3},{8,12},{9,13},{10,... | collective-permute-start | bytes 2359304 | tf_op jit(solution)/shard_map/ppermute | solution.py:41
  1138.9 22.3 %collective-permute-start.96 = (bf16[2,2,40,2048]{3,2,1,0:T(8,128)(2,1)}, bf16[2,2,40,2048]{3,2,1,0:T(8,128)(2,1)}, u32[]{:S(2)}, u32[]{:S(2)}) collective-permute-start(bf16[2,2,40,2048]{3,2,1,0:T(8,128)(2,1)} %bitcast.295), channel_id=1, source_target_pairs={{0,2},{1,3},{2,0},{3,1},{4,6},{5,7},{6,4},{7,5},{8,10},{9,11},{10,... | collective-permute-start | bytes 1966088 | tf_op jit(solution)/shard_map/ppermute | solution.py:41
  1152.6 49.9 %collective-permute-start.101 = (bf16[2048,384]{1,0:T(8,128)(2,1)S(1)}, bf16[2048,384]{1,0:T(8,128)(2,1)S(1)}, u32[]{:S(2)}, u32[]{:S(2)}) collective-permute-start(bf16[2048,384]{1,0:T(8,128)(2,1)S(1)} %select_bitcast_fusion.4), channel_id=1, source_target_pairs={{0,1},{1,0},{2,3},{3,2},{4,5},{5,4},{6,7},{7,6},{8,9},{9,8},{10,11... | collective-permute-start | bytes 4718600 | tf_op jit(solution)/shard_map/ppermute | solution.py:41
  1155.3 57.3 %collective-permute-start.104 = (bf16[64,2048]{1,0:T(8,128)(2,1)}, bf16[64,2048]{1,0:T(8,128)(2,1)}, u32[]{:S(2)}, u32[]{:S(2)}) collective-permute-start(bf16[64,2048]{1,0:T(8,128)(2,1)} %get-tuple-element.261), channel_id=1, source_target_pairs={{16,0},{17,1},{0,2},{1,3},{18,4},{19,5},{2,6},{3,7},{20,8},{21,9},... | collective-permute-start | bytes 786440 | tf_op jit(solution)/shard_map/ppermute | solution.py:41
  1156.3 56.4 %collective-permute-start.103 = (bf16[64,2048]{1,0:T(8,128)(2,1)}, bf16[64,2048]{1,0:T(8,128)(2,1)}, u32[]{:S(2)}, u32[]{:S(2)}) collective-permute-start(bf16[64,2048]{1,0:T(8,128)(2,1)} %get-tuple-element.260), channel_id=1, source_target_pairs={{0,0},{1,1},{16,2},{17,3},{2,4},{3,5},{18,6},{19,7},{4,8},{5,9},{2... | collective-permute-start | bytes 786440 | tf_op jit(solution)/shard_map/ppermute | solution.py:41
  1204.5 190.0 %all-to-all-start.2 = ((bf16[32,64,384]{2,1,0:T(8,128)(2,1)}), bf16[32,64,384]{2,1,0:T(8,128)(2,1)S(1)}, u32[]{:S(2)}, u32[]{:S(2)}) async-start(bf16[32,64,384]{2,1,0:T(8,128)(2,1)} %bitcast.915), calls=%async_computation.3 | async-start | bytes 3145728 | tf_op jit(solution)/shard_map/all_to_all | solution.py:529
  1207.3 184.5 %reduce-scatter.2.cloned.1.call-start = ((), (), s32[]{:S(2)}) async-start(), calls=%async_computation.5 | async-start | bytes 270336 | tf_op jit(solution)/shard_map/reduce_scatter | solution.py:551
  1209.9 46.5 %collective-permute-start.100 = (bf16[2,4,8,2048]{3,2,1,0:T(8,128)(2,1)S(1)}, bf16[2,4,8,2048]{3,2,1,0:T(8,128)(2,1)S(1)}, u32[]{:S(2)}, u32[]{:S(2)}) collective-permute-start(bf16[2,4,8,2048]{3,2,1,0:T(8,128)(2,1)S(1)} %get-tuple-element.267), channel_id=1, source_target_pairs={{0,16},{1,17},{2,18},{3,19},{4,20},{5,21},{6,22},{7,23},{8,24},{9,... | collective-permute-start | bytes 786440 | tf_op jit(solution)/shard_map/ppermute | solution.py:41
  (225 other events, 3160.1 us)
Sparse Core Ops, SparseCore 0:
  1259.0 132.7 reduce-scatter.1

commit v2 on v1

--- a/solution.py
+++ b/solution.py
@@ -4,6 +4,8 @@
 import jax.numpy as jnp
 import numpy as np
 from jax import lax
+from jax.experimental import pallas as pl
+from jax.experimental.pallas import tpu as pltpu
 from jax.sharding import Mesh
 from jax.sharding import PartitionSpec as P
 
@@ -123,6 +125,157 @@
     shape = value.shape[done:]
     value = xor_order(value.reshape((1 << done,) + shape), part)
     return value.reshape((value.shape[0] * shape[0],) + shape[1:])
+
+
+def whole_kernel(body, outs, *operands):
+    specs = [
+        pl.BlockSpec(memory_space=pltpu.SMEM if value.dtype == jnp.int32 else pltpu.VMEM)
+        for value in operands
+    ]
+    moved = sum(math.prod(value.shape) * value.dtype.itemsize for value in operands)
+    moved += sum(math.prod(value.shape) * value.dtype.itemsize for value in outs)
+    return pl.pallas_call(
+        body,
+        out_shape=outs,
+        in_specs=specs,
+        out_specs=[pl.BlockSpec(memory_space=pltpu.VMEM) for _ in outs],
+        cost_estimate=pl.CostEstimate(flops=0, bytes_accessed=moved, transcendentals=0),
+        compiler_params=pltpu.CompilerParams(vmem_limit_bytes=40 * 1024 * 1024),
+    )(*operands)
+
+
+def shape_of(dims, dtype=BF16):
+    return jax.ShapeDtypeStruct(tuple(dims), dtype)
+
+
+def split_heads(q_ref, k_ref, v_ref, out_ref):
+    for place in range(out_ref.shape[0]):
+        columns = pl.ds(place % 16 * HEAD, HEAD)
+        for number, ref in enumerate((q_ref, k_ref, v_ref)):
+            out_ref[place, :, number * HEAD : (number + 1) * HEAD] = ref[:, columns]
+
+
+def join_heads(in_ref, q_ref, k_ref, v_ref):
+    for head in range(16):
+        for number, ref in enumerate((q_ref, k_ref, v_ref)):
+            columns = slice(number * HEAD, (number + 1) * HEAD)
+            total = in_ref[head, :, columns].astype(F32)
+            for upper in range(1, in_ref.shape[0] // 16):
+                total = total + in_ref[upper * 16 + head, :, columns].astype(F32)
+            ref[:, head * HEAD : (head + 1) * HEAD] = total
+
+
+def split_columns(in_ref, out_ref):
+    count, rows, wide = out_ref.shape
+    width = in_ref.shape[1] // (2 * count)
+    tail = jnp.zeros((rows, wide // 2 - width), in_ref.dtype)
+    for place in range(count):
+        for side in range(2):
+            start = (side * count + place) * width
+            out_ref[place, :, side * wide // 2 : (side + 1) * wide // 2] = jnp.concatenate(
+                [in_ref[:, start : start + width], tail], axis=1
+            )
+
+
+def join_columns(in_ref, out_ref):
+    count, rows, wide = in_ref.shape
+    width = out_ref.shape[1] // (2 * count)
+    out_ref[...] = jnp.concatenate(
+        [
+            in_ref[place, :, side * wide // 2 : side * wide // 2 + width].astype(F32)
+            for side in range(2)
+            for place in range(count)
+        ],
+        axis=1,
+    )
+
+
+def join_halves(bit_ref, mine_ref, theirs_ref, out_ref):
+    wide = mine_ref.shape[1]
+    width = out_ref.shape[1] // 4
+    mine = mine_ref[...].astype(F32)
+    theirs = theirs_ref[...].astype(F32)
+    first = jnp.where(bit_ref[0] == 0, mine, theirs)
+    second = jnp.where(bit_ref[0] == 0, theirs, mine)
+    out_ref[...] = jnp.concatenate(
+        [
+            half[:, side * wide // 2 : side * wide // 2 + width]
+            for side in range(2)
+            for half in (first, second)
+        ],
+        axis=1,
+    )
+
+
+def join_down(core_ref, shared_ref, shared_other, expert_ref, expert_other, out_ref):
+    start = 0
+    for ref, other, room in (
+        (shared_ref, shared_other, -(-2 * shared_ref.shape[0] // 128) * 128),
+        (expert_ref, expert_other, -(-2 * expert_ref.shape[0] // 128) * 128),
+    ):
+        count = ref.shape[0]
+        mine = ref[...]
+        theirs = other[...]
+        out_ref[start : start + count, :] = jnp.where(core_ref[0] == 0, mine, theirs)
+        out_ref[start + count : start + 2 * count, :] = jnp.where(core_ref[0] == 0, theirs, mine)
+        out_ref[start + 2 * count : start + room, :] = jnp.zeros(
+            (room - 2 * count, out_ref.shape[1]), out_ref.dtype
+        )
+        start += room
+
+
+def join_gate_up(flags_ref, shared_ref, shared_other, expert_ref, expert_other, extra_ref, out_ref):
+    chips, rows, shared_wide = shared_ref.shape
+    core = flags_ref[0]
+    for chip in range(chips):
+        mine = shared_ref[chip]
+        theirs = shared_other[chip]
+        start = 2 * rows * chip
+        out_ref[start : start + rows, :shared_wide] = jnp.where(core == 0, mine, theirs)
+        out_ref[start + rows : start + 2 * rows, :shared_wide] = jnp.where(core == 0, theirs, mine)
+    blocks = 512 // out_ref.shape[0]
+    row_core = (pl.program_id(0) // blocks) & 1
+    expert = jnp.where(row_core == core, expert_ref[0], expert_other[0])
+    half = expert.shape[1] // 2
+    out_ref[:, shared_wide:] = expert
+    last = expert[:, half - 128 : half]
+    out_ref[:, shared_wide + half - 128 : shared_wide + half] = last + extra_ref[...]
+
+
+def assemble(flags, shared, shared_other, expert, expert_other, extra):
+    chips, depth, shared_wide = shared.shape
+    expert_wide = expert.shape[2]
+    width = 2 * chips * depth
+    block = 256
+    per = block // (2 * depth)
+    blocks = expert.shape[1] // block
+
+    def expert_block(b, flags):
+        return ((b // (2 * blocks)) ^ flags[1], b % blocks, 0)
+
+    shared_spec = pl.BlockSpec((per, depth, shared_wide), lambda b, flags: (b, 0, 0))
+    expert_spec = pl.BlockSpec((1, block, expert_wide), expert_block)
+    wide = shared_wide + expert_wide
+    return pl.pallas_call(
+        join_gate_up,
+        grid_spec=pltpu.PrefetchScalarGridSpec(
+            num_scalar_prefetch=1,
+            grid=(width // block,),
+            in_specs=[
+                shared_spec,
+                shared_spec,
+                expert_spec,
+                expert_spec,
+                pl.BlockSpec((block, 128), lambda b, flags: (b, 0)),
+            ],
+            out_specs=pl.BlockSpec((block, wide), lambda b, flags: (b, 0)),
+        ),
+        out_shape=shape_of((width, wide)),
+        cost_estimate=pl.CostEstimate(
+            flops=0, bytes_accessed=6 * width * wide, transcendentals=0
+        ),
+        compiler_params=pltpu.CompilerParams(vmem_limit_bytes=40 * 1024 * 1024),
+    )(flags, shared, shared_other, expert, expert_other, extra)
 
 
 def rotary_tables(positions):
@@ -202,8 +355,10 @@
     heads = width // HEAD
     shared_width = shared_down.shape[0] * total // chips
     expert_width = expert_down.shape[1] * 2
-    hidden_width = shared_width + expert_width
-    padded = -(-(hidden_width + experts + 1) // 128) * 128
+    shared_wide = -(-shared_width // 128) * 128
+    expert_wide = -(-(expert_width + experts + 1) // 128) * 128
+    padded = shared_wide + expert_wide
+    tail_at = 2 * shared_wide + expert_width
     groups = total // 4
     per_group = sequences // groups
     group_rows = per_group * groups * piece
@@ -219,7 +374,8 @@
             jnp.zeros((2, depth), BF16),
         ]
     )
-    small = lax.all_gather(small, AXES, axis=0)
+    small = jnp.broadcast_to(small[None], (total,) + small.shape)
+    small = lax.all_to_all(small, AXES, split_axis=0, concat_axis=0, tiled=True)
     small = small.transpose(1, 0, 2).reshape(small.shape[1], width)
     gain_attn = small[0].astype(F32)
     gain_moe = small[4].astype(F32)
@@ -233,13 +389,20 @@
         )
     ]
 
-    stacked = jnp.stack([q_weight, k_weight, v_weight], axis=1)
-    by_head = stacked.reshape(depth, 3, 16, HEAD).transpose(2, 0, 1, 3).reshape(16, depth, 3 * HEAD)
-    by_head = jnp.broadcast_to(by_head[None], (uppers,) + by_head.shape)
+    by_head = whole_kernel(
+        split_heads, [shape_of((total, depth, 3 * HEAD))], q_weight, k_weight, v_weight
+    )[0]
     my_head = lax.all_to_all(
-        by_head.reshape(total, depth, 3 * HEAD), AXES, split_axis=0, concat_axis=0, tiled=True
+        by_head, AXES, split_axis=0, concat_axis=0, tiled=True
     ).reshape(width, 3 * HEAD)
-    qkv_weight = by_bit(my_head, swap(my_head, 0), core, 1).reshape(width, 6 * HEAD)
+    other_head = swap(my_head, 0)
+    qkv_weight = jnp.concatenate(
+        [
+            jnp.where(core == 0, my_head, other_head),
+            jnp.where(core == 0, other_head, my_head),
+        ],
+        axis=1,
+    )
 
     o_places = []
     for k in range(uppers):
@@ -264,32 +427,39 @@
         for value, bits in zip(pieces(branch_own), full_orders, strict=True)
     ]
 
-    shared_pieces = (
-        shared_gate_up.reshape(depth, 2, chips, shared_width)
-        .transpose(2, 0, 1, 3)
-        .reshape(chips, depth, 2 * shared_width)
-    )
+    shared_pieces = whole_kernel(
+        split_columns, [shape_of((chips, depth, 2 * shared_wide))], shared_gate_up
+    )[0]
     shared_in = lax.all_to_all(shared_pieces, CHIPS, split_axis=0, concat_axis=0, tiled=True)
-    shared_in = by_bit(shared_in, swap(shared_in, 0), core, 1).reshape(width, 2, shared_width)
+    shared_other = swap(shared_in, 0)
     expert_rows = expert_gate_up.shape[1]
-    expert_halves = expert_gate_up[0].reshape(expert_rows, 2, 2, expert_width)
-    keep_half = jnp.where(x_bit == 0, expert_halves[:, :, 0], expert_halves[:, :, 1])
-    give_half = jnp.where(x_bit == 0, expert_halves[:, :, 1], expert_halves[:, :, 0])
-    expert_in = by_bit(keep_half, swap(give_half, 1), x_bit, 0)
-    expert_in = by_bit(expert_in, swap(expert_in, 0), core, 1).reshape(width, 2, expert_width)
-    spare = padded - hidden_width
+    expert_halves = whole_kernel(
+        split_columns, [shape_of((2, expert_rows, 2 * expert_wide))], expert_gate_up[0]
+    )[0]
+    keep_half = lax.dynamic_index_in_dim(expert_halves, x_bit, 0, keepdims=False)
+    give_half = lax.dynamic_index_in_dim(expert_halves, 1 - x_bit, 0, keepdims=False)
+    expert_in = jnp.stack([keep_half, swap(give_half, 1)])
+    expert_other = swap(expert_in, 0)
     extra = jnp.concatenate(
-        [small[6 : 6 + experts], small[5:6], jnp.zeros((spare - experts - 1, width), BF16)]
+        [
+            jnp.zeros((expert_width - expert_wide + 128, width), BF16),
+            small[6 : 6 + experts],
+            small[5:6],
+            jnp.zeros((expert_wide - expert_width - experts - 1, width), BF16),
+        ]
     ).T
-    gate_weight = jnp.concatenate([shared_in[:, 0], expert_in[:, 0], extra], axis=1)
-    up_weight = jnp.concatenate(
-        [shared_in[:, 1], expert_in[:, 1], jnp.zeros((width, spare), BF16)], axis=1
-    )
-    shared_out_rows = by_bit(shared_down, swap(shared_down, 0), core, 0).reshape(-1, width)
-    expert_out_rows = by_bit(expert_down[0], swap(expert_down[0], 0), core, 0).reshape(-1, width)
-    down_weight = jnp.concatenate(
-        [shared_out_rows, expert_out_rows, jnp.zeros((spare, width), BF16)]
-    )
+    gate_up_weight = assemble(
+        jnp.stack([core, x_bit]), shared_in, shared_other, expert_in, expert_other, extra
+    )
+    down_weight = whole_kernel(
+        join_down,
+        [shape_of((padded, width))],
+        core.reshape(1),
+        shared_down,
+        swap(shared_down, 0),
+        expert_down[0],
+        swap(expert_down[0], 0),
+    )[0]
 
     all_positions = jnp.arange(length, dtype=jnp.int32)
     named = jnp.any(routes == my_expert, axis=-1) & (all_positions[None, :] < lengths[:, None])
@@ -381,13 +551,11 @@
     normal_two, factor_two = normalize(residual)
     normed_own = (normal_two * gain_moe).astype(BF16)
 
-    column = jnp.arange(padded, dtype=jnp.int32)[None, :]
-    is_shared = column < shared_width
     expert_column = jnp.arange(experts, dtype=jnp.int32)[None, :]
     one_expert = (expert_column == my_expert).astype(F32)
     out_parts = []
     grad_parts = []
-    grad_gate = grad_up = grad_down = 0.0
+    grad_gate_up = grad_down = 0.0
     for normed, branch, bits, start in zip(
         pieces(normed_own), branch_parts, full_orders, (0, 48, 88), strict=True
     ):
@@ -399,35 +567,40 @@
         mask = jnp.take(
             kept[:, start : start + count], me ^ jnp.asarray(relative(bits), jnp.int32), axis=0
         ).reshape(-1, 1)
-        gate = mm(everyone, gate_weight)
-        up = mm(everyone, up_weight)
+        joined_gu = mm(everyone, gate_up_weight)
         back = mm_nt(branch, down_weight)
-        logits = gate[:, hidden_width : hidden_width + experts]
-        router_probs = jax.nn.softmax(logits, axis=-1)
-        shared_weight = jax.nn.sigmoid(
-            gate[:, hidden_width + experts : hidden_width + experts + 1]
+        router_probs = jax.nn.softmax(joined_gu[:, tail_at : tail_at + experts], axis=-1)
+        shared_weight = jax.nn.sigmoid(joined_gu[:, tail_at + experts : tail_at + experts + 1])
+        my_prob = jnp.sum(router_probs * one_expert, axis=1, keepdims=True)
+        hidden_low = []
+        joined_grad = []
+        alongs = []
+        at = 0
+        for wide, weight in ((shared_wide, shared_weight), (expert_wide, my_prob * mask)):
+            gate = joined_gu[:, 2 * at : 2 * at + wide]
+            up = joined_gu[:, 2 * at + wide : 2 * at + 2 * wide]
+            back_part = back[:, at : at + wide]
+            sigmoid_gate = jax.nn.sigmoid(gate)
+            hidden = gate * sigmoid_gate * up
+            hidden_low.append((hidden * weight).astype(BF16))
+            alongs.append(jnp.sum(hidden * back_part, axis=1, keepdims=True))
+            grad_hidden = back_part * weight
+            joined_grad.append(
+                grad_hidden * up * sigmoid_gate * (1.0 + gate * (1.0 - sigmoid_gate))
+            )
+            joined_grad.append(grad_hidden * gate * sigmoid_gate)
+            at += wide
+        logit_grad = router_probs * (alongs[1] * mask) * (one_expert - my_prob)
+        shared_logit_grad = alongs[0] * shared_weight * (1.0 - shared_weight)
+        tail = jnp.concatenate([logit_grad, shared_logit_grad], axis=1)
+        joined_grad[2] = joined_grad[2] + jnp.pad(
+            tail, ((0, 0), (expert_width, expert_wide - expert_width - experts - 1))
         )
-        my_prob = jnp.sum(router_probs * one_expert, axis=1, keepdims=True)
-        weight = jnp.where(is_shared, shared_weight, my_prob * mask)
-        sigmoid_gate = jax.nn.sigmoid(gate)
-        hidden = gate * sigmoid_gate * up
-        hidden_low = (hidden * weight).astype(BF16)
-        grad_hidden = back * weight
-        along = hidden * back
-        shared_along = jnp.sum(jnp.where(is_shared, along, 0.0), axis=1, keepdims=True)
-        expert_along = jnp.sum(jnp.where(is_shared, 0.0, along), axis=1, keepdims=True) * mask
-        logit_grad = router_probs * expert_along * (one_expert - my_prob)
-        shared_logit_grad = shared_along * shared_weight * (1.0 - shared_weight)
-        tail = jnp.concatenate([logit_grad, shared_logit_grad], axis=1)
-        gate_grad = grad_hidden * up * sigmoid_gate * (1.0 + gate * (1.0 - sigmoid_gate))
-        gate_grad = (
-            gate_grad + jnp.pad(tail, ((0, 0), (hidden_width, spare - experts - 1)))
-        ).astype(BF16)
-        up_grad = (grad_hidden * gate * sigmoid_gate).astype(BF16)
+        joined_grad = jnp.concatenate([value.astype(BF16) for value in joined_grad], axis=1)
+        hidden_low = jnp.concatenate(hidden_low, axis=1)
         grad_down = grad_down + mm_tn(hidden_low, branch)
-        grad_gate = grad_gate + mm_tn(everyone, gate_grad)
-        grad_up = grad_up + mm_tn(everyone, up_grad)
-        back_rows = mm_nt(gate_grad, gate_weight) + mm_nt(up_grad, up_weight)
+        grad_gate_up = grad_gate_up + mm_tn(everyone, joined_grad)
+        back_rows = mm_nt(joined_grad, gate_up_weight)
         grad_parts.append(scatter_bits(back_rows.astype(BF16).reshape(lead + (width,)), bits))
         out_parts.append(
             scatter_bits(mm(hidden_low, down_weight).astype(BF16).reshape(lead + (width,)), bits)
@@ -490,47 +663,49 @@
     grad_input, grad_gain_attn = norm_back(grad_normed_one, normal_one, factor_one, gain_attn)
     grad_tokens = (grad_residual + grad_input).astype(BF16).reshape(tokens.shape)
 
-    grad_down = grad_down[:hidden_width].astype(BF16)
+    def pick(value, axis, number):
+        return lax.dynamic_index_in_dim(value, number, axis, keepdims=False)
 
     def to_core(value, axis):
-        low = lax.index_in_dim(value, 0, axis, keepdims=False)
-        top = lax.index_in_dim(value, 1, axis, keepdims=False)
-        keep = jnp.where(core == 0, low, top)
-        give = jnp.where(core == 0, top, low)
-        return keep.astype(F32) + swap(give, 0).astype(F32)
-
+        given_rows = swap(pick(value, axis, 1 - core), 0)
+        return pick(value, axis, core).astype(F32) + given_rows.astype(F32)
+
+    grad_down = grad_down.astype(BF16)
     grad_shared_down = to_core(grad_down[:shared_width].reshape(2, -1, width), 0)
-    grad_expert_down = to_core(grad_down[shared_width:].reshape(2, -1, width), 0)
-    tail_grads = grad_gate[:, hidden_width : hidden_width + experts + 1]
-    grad_gu = jnp.stack(
-        [grad_gate[:, :hidden_width].astype(BF16), grad_up[:, :hidden_width].astype(BF16)], axis=1
-    )
+    grad_expert_down = to_core(
+        grad_down[shared_wide : shared_wide + expert_width].reshape(2, -1, width), 0
+    )
+    tail_grads = grad_gate_up[:, tail_at : tail_at + experts + 1]
+    grad_gate_up = grad_gate_up.astype(BF16)
     grad_shared_gu = to_core(
-        grad_gu[:, :, :shared_width].reshape(chips, 2, depth, 2 * shared_width), 1
+        grad_gate_up[:, : 2 * shared_wide].reshape(chips, 2, depth, 2 * shared_wide), 1
     ).astype(BF16)
     grad_shared_gu = lax.all_to_all(
         grad_shared_gu, CHIPS, split_axis=0, concat_axis=0, tiled=True
     )
-    grad_shared_gu = (
-        grad_shared_gu.reshape(chips, depth, 2, shared_width)
-        .transpose(1, 2, 0, 3)
-        .reshape(depth, -1)
-        .astype(F32)
-    )
+    grad_shared_gu = whole_kernel(
+        join_columns, [shape_of((depth, 2 * chips * shared_width), F32)], grad_shared_gu
+    )[0]
     grad_expert_gu = to_core(
-        grad_gu[:, :, shared_width:].reshape(2, 2, expert_rows, 2, expert_width), 1
+        grad_gate_up[:, 2 * shared_wide :].reshape(2, 2, expert_rows, 2 * expert_wide), 1
     ).astype(BF16)
-    keep_rows = jnp.where(x_bit == 0, grad_expert_gu[0], grad_expert_gu[1])
-    give_rows = jnp.where(x_bit == 0, grad_expert_gu[1], grad_expert_gu[0])
-    grad_expert_gu = by_bit(keep_rows, swap(give_rows, 1), x_bit, 2)
-    grad_expert_gu = grad_expert_gu.reshape(1, expert_rows, -1).astype(F32)
-
-    grad_qkv = to_core(grad_qkv.astype(BF16).reshape(width, 2, 3 * HEAD), 1).astype(BF16)
+    grad_expert_gu = whole_kernel(
+        join_halves,
+        [shape_of((expert_rows, 4 * expert_width), F32)],
+        x_bit.reshape(1),
+        pick(grad_expert_gu, 0, x_bit),
+        swap(pick(grad_expert_gu, 0, 1 - x_bit), 1),
+    )[0][None]
+
+    grad_qkv = grad_qkv.astype(BF16)
+    low_head = grad_qkv[:, : 3 * HEAD]
+    high_head = grad_qkv[:, 3 * HEAD :]
+    given_head = swap(jnp.where(core == 0, high_head, low_head), 0)
+    grad_qkv = add_low(jnp.where(core == 0, low_head, high_head), given_head)
     grad_qkv = lax.all_to_all(
         grad_qkv.reshape(total, depth, 3 * HEAD), AXES, split_axis=0, concat_axis=0, tiled=True
     )
-    grad_qkv = jnp.sum(grad_qkv.reshape(uppers, 16, depth, 3, HEAD).astype(F32), axis=0)
-    grad_qkv = grad_qkv.transpose(2, 1, 0, 3).reshape(3, depth, width)
+    grad_qkv = whole_kernel(join_heads, [shape_of((depth, width), F32)] * 3, grad_qkv)
     grad_o = to_core(grad_o.astype(BF16).reshape(uppers, 2, depth, width), 1).astype(BF16)
     grad_o = xor_order(grad_o, upper)
     grad_o = sum(
@@ -544,25 +719,28 @@
         pair,
         axis=1,
     ).reshape(3, width)
-    vectors = jnp.concatenate(
-        [grad_gain_attn[None], bias_rows, grad_gain_moe[None], tail_grads.T], axis=0
-    )
-    vectors = vectors.reshape(-1, total, depth).transpose(1, 0, 2)
-    vectors = lax.psum_scatter(vectors, AXES, scatter_dimension=0, tiled=True)[0]
+
+    def to_owners(vectors):
+        vectors = vectors.reshape(-1, total, depth).transpose(1, 0, 2)
+        vectors = lax.all_to_all(vectors, AXES, split_axis=0, concat_axis=0, tiled=True)
+        return jnp.sum(vectors, axis=0)
+
+    vectors = to_owners(jnp.concatenate([bias_rows, grad_gain_moe[None], tail_grads.T], axis=0))
+    grad_gain_attn = to_owners(grad_gain_attn[None])[0]
     return (
         mixed,
         grad_tokens,
-        vectors[0],
+        grad_gain_attn,
         grad_qkv[0],
         grad_qkv[1],
         grad_qkv[2],
+        vectors[0],
         vectors[1],
         vectors[2],
+        grad_o,
         vectors[3],
-        grad_o,
-        vectors[4],
-        vectors[5 : 5 + experts].T,
-        vectors[5 + experts],
+        vectors[4 : 4 + experts].T,
+        vectors[4 + experts],
         grad_shared_gu,
         grad_shared_down,
         grad_expert_gu,

time: 1420 us -> 1140 us (0.80)
  local copies, waits for them, and re-layouts: 268 us -> 96.4 us
  blocking collectives: 62.1 us -> 0 us
  other arithmetic: 179 us -> 136 us
  waiting for transfers between devices: 565 us -> 531 us
  starting transfers between devices: 123 us -> 148 us
  Pallas kernels: 0 us -> 24.3 us
    reduce_scatter x1 -> x0, waiting for transfers between devices: 130 us -> none  [on_device(): lax.psum_scatter(vectors, AXES, scatter_dimension=0, tiled=True)[0]]
    ppermute x110, waiting for transfers between devices: 435 us -> 521 us  [permute(): return lax.ppermute(value, AXES, pairs)]
    all_gather x1 -> x0, blocking collectives: 62.1 us -> none  [on_device(): small = lax.all_gather(small, AXES, axis=0)]
    reshape x9 -> x0, local copies, waits for them, and re-layouts: 53.6 us -> none  [the longest x1 10.6 us: on_device(): by_bit(expert_in, swap(expert_in, 0), core, 1)]
    another operation x7 -> x1, local copies, waits for them, and re-layouts: 49.9 us -> 0.69 us  [to_owners(): vectors = vectors.reshape(-1, total, depth).transpose(1, 0, 2)]
    slice x10 -> x6, local copies, waits for them, and re-layouts: 42.6 us -> 10.5 us  [the longest x1 3.19 us: on_device(): grad_gate_up[:, 2 * shared_wide:]]
    pallas_call x0 -> x8, Pallas kernels: none -> 24.3 us  [the longest x7 14 us: whole_kernel(): pl.pallas_call(body, out_shape=outs, in_specs=specs, out_specs=[pl.BlockS...]
    convert_element_type x5 -> x0, local copies, waits for them, and re-layouts: 22 us -> none  [the longest x3 15.6 us: on_device(): grad_shared_gu = grad_shared_gu.reshape(chips, depth, 2, shared_width).tr...]
  transfers between devices with their start and end apart: 115 -> 117, of which waited for: 52 -> 60; matrix products, arithmetic and copies ran while one was open for 42% -> 35% of each run, Pallas kernels for 0% -> 2%
where the time goes in v2:
time: 1140 us; the launch traced here: 1130 us
  waiting for transfers between devices  531 us (47%)
  matrix products  189 us (17%)
  starting transfers between devices  148 us (13%)
  other arithmetic  136 us (12%)
  local copies, waits for them, and re-layouts  96.4 us (8%)
  Pallas kernels  24.3 us (2%)
    ppermute x110, waiting for transfers between devices, permute(): return lax.ppermute(value, AXES, pairs)  521 us
    ppermute x110, starting transfers between devices, permute(): return lax.ppermute(value, AXES, pairs)  119 us
    dot_general x12, matrix products, mm_tn(): lax.dot_general(a, b, (((0,), (0,)), ((), ())), preferred_element_type=F32)  86 us
    dot_general x13, matrix products, mm(): lax.dot_general(a, b, (((1,), (0,)), ((), ())), preferred_element_type=F32)  50.4 us
    dot_general x12, matrix products, mm_nt(): lax.dot_general(a, b, (((1,), (1,)), ((), ())), preferred_element_type=F32)  48.2 us
    convert_element_type x43, other arithmetic, add_low(): return (a.astype(F32) + b.astype(F32)).astype(BF16)  28.8 us
    unnamed x341, local copies, waits for them, and re-layouts  25.5 us
  transfers between devices with their start and end apart: 117, of which 60 were waited for; matrix products, arithmetic and copies ran while one was open for 35% of the time, Pallas kernels for 2%

profile of v2, /device:TPU:0, one launch (start us, length us, event | category | flops | bytes accessed | tf_op | source)
XLA Modules:
  0.0 1128.9 jit_solution(16526625665849213396)
XLA Ops:
  9.5 5.0 all-to-all-start
  49.8 30.4 %collective-permute-done.6 = bf16[40,2048]{1,0:T(8,128)(2,1)S(1)} collective-permute-done((bf16[40,2048]{1,0:T(8,128)(2,1)S(1)}, bf16[40,2048]{1,0:T(8,128)(2,1)S(1)}, u32[]{:S(2)}, u32[]{:S(2)}) %collective-permute-start.6) | collective-permute-done | bytes 163872 | tf_op jit(solution)/shard_map/ppermute | solution.py:43
  85.6 4.2 collective-permute-start.2
  105.4 5.8 collective-permute-done.3
  112.4 6.9 all-to-all-start.2
  121.8 7.3 collective-permute-done.8
  134.1 16.6 %collective-permute-done.4 = bf16[2,2,48,2048]{3,2,1,0:T(8,128)(2,1)S(1)} collective-permute-done((bf16[2,2,48,2048]{3,2,1,0:T(8,128)(2,1)S(1)}, bf16[2,2,48,2048]{3,2,1,0:T(8,128)(2,1)S(1)}, u32[]{:S(2)}, u32[]{:S(2)}) %collective-permute-start.4) | collective-permute-done | bytes 786464 | tf_op jit(solution)/shard_map/ppermute | solution.py:43
  172.8 8.5 collective-permute-done.18
  189.1 15.8 %collective-permute-done.15 = bf16[2,2,48,2048]{3,2,1,0:T(8,128)(2,1)S(1)} collective-permute-done((bf16[2,2,48,2048]{3,2,1,0:T(8,128)(2,1)}, bf16[2,2,48,2048]{3,2,1,0:T(8,128)(2,1)S(1)}, u32[]{:S(2)}, u32[]{:S(2)}) %collective-permute-start.15) | collective-permute-done | bytes 786464 | tf_op jit(solution)/shard_map/ppermute | solution.py:43
  207.4 5.9 collective-permute-done.19
  213.3 7.0 collective-permute-done.22
  222.3 4.7 collective-permute-done.20
  229.0 5.8 collective-permute-done.16
  268.8 10.3 shard_map.362
  287.8 18.8 %collective-permute-done.71 = bf16[40,2048]{1,0:T(8,128)(2,1)S(1)} collective-permute-done((bf16[40,2048]{1,0:T(8,128)(2,1)S(1)}, bf16[40,2048]{1,0:T(8,128)(2,1)S(1)}, u32[]{:S(2)}, u32[]{:S(2)}) %collective-permute-start.71) | collective-permute-done | bytes 163872 | tf_op jit(solution)/shard_map/ppermute | solution.py:43
  306.6 7.7 collective-permute-done.47
  333.7 4.2 collective-permute-done.64
  342.7 7.2 collective-permute-done.41
  353.8 10.3 collective-permute-done.73
  366.9 11.2 collective-permute-done.49
  387.8 18.4 %collective-permute-done.42 = bf16[2,2,2,40,2048]{4,3,2,1,0:T(8,128)(2,1)S(1)} collective-permute-done((bf16[2,2,2,40,2048]{4,3,2,1,0:T(8,128)(2,1)S(1)}, bf16[2,2,2,40,2048]{4,3,2,1,0:T(8,128)(2,1)S(1)}, u32[]{:S(2)}, u32[]{:S(2)}) %collective-permute-start.42) | collective-permute-done | bytes 1310752 | tf_op jit(solution)/shard_map/ppermute | solution.py:43
  407.5 8.4 fusion.231
  415.9 23.6 %collective-permute-done.50 = bf16[2,2,2,40,2048]{4,3,2,1,0:T(8,128)(2,1)} collective-permute-done((bf16[2,2,2,40,2048]{4,3,2,1,0:T(8,128)(2,1)}, bf16[2,2,2,40,2048]{4,3,2,1,0:T(8,128)(2,1)}, u32[]{:S(2)}, u32[]{:S(2)}) %collective-permute-start.50) | collective-permute-done | bytes 1310752 | tf_op jit(solution)/shard_map/ppermute | solution.py:43
  441.2 11.7 %fusion.232 = f32[640,2304]{0,1:T(8,128)S(1)} fusion(bf16[640,2048]{1,0:T(8,128)(2,1)S(1)} %bitcast.774, bf16[2048,2304]{1,0:T(8,128)(2,1)} %shard_map.362), kind=kOutput, calls=%fused_computation.659 | convolution fusion | flops 6039797760 | bytes 17956864 | tf_op jit(solution)/shard_map/dot_general | solution.py:27
  470.7 4.3 fusion.34
  475.0 10.3 convolution_convert_fusion.3
  485.3 13.7 %fusion.99 = f32[2048,2304]{1,0:T(8,128)} fusion(bf16[640,2048]{1,0:T(8,128)(2,1)S(1)} %bitcast.827, bf16[640,768]{0,1:T(8,128)(2,1)S(1)} %get-tuple-element.154, bf16[640,768]{0,1:T(8,128)(2,1)S(1)} %get-tuple-element.153, bf16[640,384]{0,1:T(8,128)(2,1)S(1)} %get-tuple-element.152, bf16[640,384]{0,1:T(8,128)(2,1)S(1)} %get-tuple-element.151), kind=kOutput, calls=%fused_computation.332 | convolution fusion | flops 6051594240 | bytes 24444928 | tf_op jit(solution)/shard_map/dot_general | solution.py:31
  501.9 4.1 fusion.32
  506.1 10.1 convolution_convert_fusion.2
  529.5 6.6 fusion.84
  536.1 4.0 convolution_convert_fusion.5
  551.5 11.0 fusion.230
  572.1 10.6 convolution_convert_fusion
  582.7 12.5 %fusion.97 = f32[2048,2304]{1,0:T(8,128)} fusion(bf16[768,2048]{1,0:T(8,128)(2,1)S(1)} %bitcast.813, bf16[768,768]{0,1:T(8,128)(2,1)S(1)} %get-tuple-element.150, bf16[768,768]{0,1:T(8,128)(2,1)S(1)} %get-tuple-element.149, bf16[768,384]{0,1:T(8,128)(2,1)} %copy-done.116, bf16[768,384]{0,1:T(8,128)(2,1)S(1)} %get-tuple-element.147), kind=kOutput, calls=%fused_computation.299 | convolution fusion | flops 7261913088 | bytes 25559040 | tf_op jit(solution)/shard_map/dot_general | solution.py:31
  595.2 5.9 convolution_convert_fusion.1
  601.1 7.9 fusion.64
  609.1 8.9 add_convert_fusion
  623.2 22.7 %fusion.229 = (bf16[2048,2304]{1,0:T(8,128)(2,1)}, f32[2048,2304]{1,0:T(8,128)}) fusion(bf16[640,2048]{1,0:T(8,128)(2,1)S(1)} %bitcast.775, bf16[640,768]{0,1:T(8,128)(2,1)} %copy-done.56, bf16[640,768]{0,1:T(8,128)(2,1)} %copy-done.55, bf16[640,384]{0,1:T(8,128)(2,1)} %copy-done.89, bf16[640,384]{0,1:T(8,128)(2,1)S(1)} %copy-done.88, ...), kind=kOutput, calls=%fused_computation.656 | convolution fusion | flops 6065750016 | bytes 71630848 | tf_op jit(solution)/shard_map/dot_general | solution.py:31
  682.7 10.4 collective-permute-done.76
  694.8 55.3 %collective-permute-done.68 = bf16[2,2,40,2048]{3,2,1,0:T(8,128)(2,1)S(1)} collective-permute-done((bf16[2,2,40,2048]{3,2,1,0:T(8,128)(2,1)S(1)}, bf16[2,2,40,2048]{3,2,1,0:T(8,128)(2,1)S(1)}, u32[]{:S(2)}, u32[]{:S(2)}) %collective-permute-start.68) | collective-permute-done | bytes 655392 | tf_op jit(solution)/shard_map/ppermute | solution.py:43
  752.7 14.8 %collective-permute-done.44 = bf16[2,2,40,2048]{3,2,1,0:T(8,128)(2,1)S(1)} collective-permute-done((bf16[2,2,40,2048]{3,2,1,0:T(8,128)(2,1)S(1)}, bf16[2,2,40,2048]{3,2,1,0:T(8,128)(2,1)S(1)}, u32[]{:S(2)}, u32[]{:S(2)}) %collective-permute-start.44) | collective-permute-done | bytes 655392 | tf_op jit(solution)/shard_map/ppermute | solution.py:43
  771.9 5.0 all-to-all-start.6
  789.2 8.6 collective-permute-done.53
  801.7 24.5 %collective-permute-done.78 = bf16[40,2048]{1,0:T(8,128)(2,1)S(1)} collective-permute-done((bf16[40,2048]{1,0:T(8,128)(2,1)S(1)}, bf16[40,2048]{1,0:T(8,128)(2,1)S(1)}, u32[]{:S(2)}, u32[]{:S(2)}) %collective-permute-start.78) | collective-permute-done | bytes 163872 | tf_op jit(solution)/shard_map/ppermute | solution.py:43
  826.2 7.0 collective-permute-done.70
  833.2 4.8 collective-permute-done.54
  841.6 9.6 collective-permute-done.61
  852.4 9.6 collective-permute-done.37
  868.2 13.7 %collective-permute-done.79 = bf16[2,4,8,2048]{3,2,1,0:T(8,128)(2,1)S(1)} collective-permute-done((bf16[2,4,8,2048]{3,2,1,0:T(8,128)(2,1)S(1)}, bf16[2,4,8,2048]{3,2,1,0:T(8,128)(2,1)S(1)}, u32[]{:S(2)}, u32[]{:S(2)}) %collective-permute-start.79) | collective-permute-done | bytes 262176 | tf_op jit(solution)/shard_map/ppermute | solution.py:43
  889.6 4.7 collective-permute-done.87
  899.5 4.4 collective-permute-done.88
  910.6 12.0 %collective-permute-done.89 = bf16[2,2,40,2048]{3,2,1,0:T(8,128)(2,1)S(1)} collective-permute-done((bf16[2,2,40,2048]{3,2,1,0:T(8,128)(2,1)S(1)}, bf16[2,2,40,2048]{3,2,1,0:T(8,128)(2,1)S(1)}, u32[]{:S(2)}, u32[]{:S(2)}) %collective-permute-start.89) | collective-permute-done | bytes 655392 | tf_op jit(solution)/shard_map/ppermute | solution.py:43
  930.2 9.2 collective-permute-done.83
  979.0 15.2 %collective-permute-done.90 = bf16[2,2,48,2048]{3,2,1,0:T(8,128)(2,1)S(1)} collective-permute-done((bf16[2,2,48,2048]{3,2,1,0:T(8,128)(2,1)S(1)}, bf16[2,2,48,2048]{3,2,1,0:T(8,128)(2,1)S(1)}, u32[]{:S(2)}, u32[]{:S(2)}) %collective-permute-start.90) | collective-permute-done | bytes 786464 | tf_op jit(solution)/shard_map/ppermute | solution.py:43
  996.2 5.0 collective-permute-done.94
  1001.6 6.7 collective-permute-done.97
  1010.0 4.3 collective-permute-done.95
  1015.9 6.3 collective-permute-done.91
  1027.9 5.3 collective-permute-done.92
  1044.1 11.4 %collective-permute-done.100 = bf16[2,4,8,2048]{3,2,1,0:T(8,128)(2,1)S(1)} collective-permute-done((bf16[2,4,8,2048]{3,2,1,0:T(8,128)(2,1)}, bf16[2,4,8,2048]{3,2,1,0:T(8,128)(2,1)S(1)}, u32[]{:S(2)}, u32[]{:S(2)}) %collective-permute-start.100) | collective-permute-done | bytes 262176 | tf_op jit(solution)/shard_map/ppermute | solution.py:43
  1060.1 6.3 all-to-all-done.5
  1069.0 4.1 add_convert_fusion.1
  1085.0 4.7 shard_map.366
  1100.3 23.1 %collective-permute-done.104 = bf16[64,2048]{1,0:T(8,128)(2,1)S(1)} collective-permute-done((bf16[64,2048]{1,0:T(8,128)(2,1)S(1)}, bf16[64,2048]{1,0:T(8,128)(2,1)S(1)}, u32[]{:S(2)}, u32[]{:S(2)}) %collective-permute-start.104) | collective-permute-done | bytes 262176 | tf_op jit(solution)/shard_map/ppermute | solution.py:43
  (912 shorter events, 450.7 us)
Async XLA Ops:
  0.7 45.1 %collective-permute-start.12 = (bf16[64,2048]{1,0:T(8,128)(2,1)}, bf16[64,2048]{1,0:T(8,128)(2,1)}, u32[]{:S(2)}, u32[]{:S(2)}) collective-permute-start(bf16[64,2048]{1,0:T(8,128)(2,1)} %param.38), channel_id=1, source_target_pairs={{0,0},{1,1},{2,16},{3,17},{4,2},{5,3},{6,18},{7,19},{8,4},{9,5},{1... | collective-permute-start | bytes 786440 | tf_op jit(solution)/shard_map/ppermute | solution.py:43
  4.3 41.8 %collective-permute-start.13 = (bf16[64,2048]{1,0:T(8,128)(2,1)}, bf16[64,2048]{1,0:T(8,128)(2,1)}, u32[]{:S(2)}, u32[]{:S(2)}) collective-permute-start(bf16[64,2048]{1,0:T(8,128)(2,1)} %param.38), channel_id=1, source_target_pairs={{0,16},{1,17},{2,0},{3,1},{4,18},{5,19},{6,2},{7,3},{8,20},{9,21},... | collective-permute-start | bytes 786440 | tf_op jit(solution)/shard_map/ppermute | solution.py:43
  9.5 28.4 %all-to-all-start = ((bf16[32,2,512]{2,1,0:T(2,128)(2,1)}), bf16[32,2,512]{2,1,0:T(2,128)(2,1)S(1)}, u32[]{:S(2)}, u32[]{:S(2)}) async-start(bf16[32,2,512]{2,1,0:T(2,128)(2,1)} %reshape.1148), calls=%async_computation | async-start | bytes 131072 | tf_op jit(solution)/shard_map/all_to_all | solution.py:378
  16.4 28.0 %collective-permute-start = (bf16[2,4,8,2048]{3,2,1,0:T(8,128)(2,1)}, bf16[2,4,8,2048]{3,2,1,0:T(8,128)(2,1)}, u32[]{:S(2)}, u32[]{:S(2)}) collective-permute-start(bf16[2,4,8,2048]{3,2,1,0:T(8,128)(2,1)} %pad_maximum_fusion.83), channel_id=1, source_target_pairs={{0,16},{1,17},{2,18},{3,19},{4,20},{5,21},{6,22},{7,23},{8,24},{9,... | collective-permute-start | bytes 786440 | tf_op jit(solution)/shard_map/ppermute | solution.py:43
  23.4 96.0 %collective-permute-start.31 = (bf16[512,1536]{1,0:T(8,128)(2,1)}, bf16[512,1536]{1,0:T(8,128)(2,1)}, u32[]{:S(2)}, u32[]{:S(2)}) collective-permute-start(bf16[512,1536]{1,0:T(8,128)(2,1)} %get-tuple-element.172), channel_id=1, source_target_pairs={{0,2},{1,3},{2,0},{3,1},{4,6},{5,7},{6,4},{7,5},{8,10},{9,11},{10,... | collective-permute-start | bytes 4718600 | tf_op jit(solution)/shard_map/ppermute | solution.py:43
  24.8 239.2 %collective-permute-start.33 = (bf16[176,2048]{1,0:T(8,128)(2,1)}, bf16[176,2048]{1,0:T(8,128)(2,1)}, u32[]{:S(2)}, u32[]{:S(2)}) collective-permute-start(bf16[176,2048]{1,0:T(8,128)(2,1)} %shared_ref.1), channel_id=1, source_target_pairs={{0,1},{1,0},{2,3},{3,2},{4,5},{5,4},{6,7},{7,6},{8,9},{9,8},{10,11... | collective-permute-start | bytes 2162696 | tf_op jit(solution)/shard_map/ppermute | solution.py:43
  38.5 73.9 %all-to-all-start.1 = ((bf16[32,64,384]{2,1,0:T(8,128)(2,1)}), bf16[32,64,384]{2,1,0:T(8,128)(2,1)}, u32[]{:S(2)}, u32[]{:S(2)}) async-start(bf16[32,64,384]{2,1,0:T(8,128)(2,1)} %shard_map.359), calls=%async_computation.1 | async-start | bytes 3145728 | tf_op jit(solution)/shard_map/all_to_all | solution.py:395
  44.4 219.5 %collective-permute-start.34 = (bf16[352,2048]{1,0:T(8,128)(2,1)}, bf16[352,2048]{1,0:T(8,128)(2,1)}, u32[]{:S(2)}, u32[]{:S(2)}) collective-permute-start(bf16[352,2048]{1,0:T(8,128)(2,1)} %bitcast.111.expert_ref), channel_id=1, source_target_pairs={{0,1},{1,0},{2,3},{3,2},{4,5},{5,4},{6,7},{7,6},{8,9},{9,8},{10,11... | collective-permute-start | bytes 4325384 | tf_op jit(solution)/shard_map/ppermute | solution.py:43
  47.3 46.3 %collective-permute-start.14 = (bf16[2,64,2048]{2,1,0:T(8,128)(2,1)S(1)}, bf16[2,64,2048]{2,1,0:T(8,128)(2,1)S(1)}, u32[]{:S(2)}, u32[]{:S(2)}) collective-permute-start(bf16[2,64,2048]{2,1,0:T(8,128)(2,1)S(1)} %pad_maximum_fusion.49), channel_id=1, source_target_pairs={{0,1},{1,0},{2,3},{3,2},{4,5},{5,4},{6,7},{7,6},{8,9},{9,8},{10,11... | collective-permute-start | bytes 1572872 | tf_op jit(solution)/shard_map/ppermute | solution.py:43
  48.2 32.1 %collective-permute-start.6 = (bf16[40,2048]{1,0:T(8,128)(2,1)S(1)}, bf16[40,2048]{1,0:T(8,128)(2,1)S(1)}, u32[]{:S(2)}, u32[]{:S(2)}) collective-permute-start(bf16[40,2048]{1,0:T(8,128)(2,1)S(1)} %get-tuple-element.295), channel_id=1, source_target_pairs={{0,2},{1,3},{2,0},{3,1},{4,6},{5,7},{6,4},{7,5},{8,10},{9,11},{10,... | collective-permute-start | bytes 491528 | tf_op jit(solution)/shard_map/ppermute | solution.py:43
  101.9 27.2 %collective-permute-start.8 = (bf16[2,2,40,2048]{3,2,1,0:T(8,128)(2,1)}, bf16[2,2,40,2048]{3,2,1,0:T(8,128)(2,1)}, u32[]{:S(2)}, u32[]{:S(2)}) collective-permute-start(bf16[2,2,40,2048]{3,2,1,0:T(8,128)(2,1)} %get-tuple-element.245), channel_id=1, source_target_pairs={{0,8},{1,9},{2,10},{3,11},{4,12},{5,13},{6,14},{7,15},{8,0},{9,1},... | collective-permute-start | bytes 1966088 | tf_op jit(solution)/shard_map/ppermute | solution.py:43
  111.1 19.4 %collective-permute-start.11 = (bf16[2,2,40,2048]{3,2,1,0:T(8,128)(2,1)}, bf16[2,2,40,2048]{3,2,1,0:T(8,128)(2,1)}, u32[]{:S(2)}, u32[]{:S(2)}) collective-permute-start(bf16[2,2,40,2048]{3,2,1,0:T(8,128)(2,1)} %get-tuple-element.247), channel_id=1, source_target_pairs={{0,2},{1,3},{2,0},{3,1},{4,6},{5,7},{6,4},{7,5},{8,10},{9,11},{10,... | collective-permute-start | bytes 1966088 | tf_op jit(solution)/shard_map/ppermute | solution.py:43
  112.4 60.4 %all-to-all-start.2 = ((bf16[16,64,768]{2,1,0:T(8,128)(2,1)}), bf16[16,64,768]{2,1,0:T(8,128)(2,1)}, u32[]{:S(2)}, u32[]{:S(2)}) async-start(bf16[16,64,768]{2,1,0:T(8,128)(2,1)} %shard_map.360), calls=%async_computation.2 | async-start | bytes 3145728 | tf_op jit(solution)/shard_map/all_to_all | solution.py:433
  119.4 31.7 %collective-permute-start.5 = (bf16[2048,384]{1,0:T(8,128)(2,1)}, bf16[2048,384]{1,0:T(8,128)(2,1)S(1)}, u32[]{:S(2)}, u32[]{:S(2)}) collective-permute-start(bf16[2048,384]{1,0:T(8,128)(2,1)} %bitcast.20), channel_id=1, source_target_pairs={{0,1},{1,0},{2,3},{3,2},{4,5},{5,4},{6,7},{7,6},{8,9},{9,8},{10,11... | collective-permute-start | bytes 4718600 | tf_op jit(solution)/shard_map/ppermute | solution.py:43
  129.0 21.6 %collective-permute-start.4 = (bf16[2,2,48,2048]{3,2,1,0:T(8,128)(2,1)S(1)}, bf16[2,2,48,2048]{3,2,1,0:T(8,128)(2,1)S(1)}, u32[]{:S(2)}, u32[]{:S(2)}) collective-permute-start(bf16[2,2,48,2048]{3,2,1,0:T(8,128)(2,1)S(1)} %copy-done.112), channel_id=1, source_target_pairs={{0,4},{1,5},{2,6},{3,7},{4,0},{5,1},{6,2},{7,3},{8,12},{9,13},{10,... | collective-permute-start | bytes 2359304 | tf_op jit(solution)/shard_map/ppermute | solution.py:43
  130.5 138.3 %collective-permute-start.32 = (bf16[2,512,1536]{2,1,0:T(8,128)(2,1)S(1)}, bf16[2,512,1536]{2,1,0:T(8,128)(2,1)}, u32[]{:S(2)}, u32[]{:S(2)}) collective-permute-start(bf16[2,512,1536]{2,1,0:T(8,128)(2,1)S(1)} %pad_maximum_fusion.4.expert_ref), channel_id=1, source_target_pairs={{0,1},{1,0},{2,3},{3,2},{4,5},{5,4},{6,7},{7,6},{8,9},{9,8},{10,11... | collective-permute-start | bytes 9437192 | tf_op jit(solution)/shard_map/ppermute | solution.py:43
  181.3 87.5 %collective-permute-start.30 = (bf16[16,64,768]{2,1,0:T(8,128)(2,1)}, bf16[16,64,768]{2,1,0:T(8,128)(2,1)}, u32[]{:S(2)}, u32[]{:S(2)}) collective-permute-start(bf16[16,64,768]{2,1,0:T(8,128)(2,1)} %all-to-all-done.2.shared_ref), channel_id=1, source_target_pairs={{0,1},{1,0},{2,3},{3,2},{4,5},{5,4},{6,7},{7,6},{8,9},{9,8},{10,11... | collective-permute-start | bytes 4718600 | tf_op jit(solution)/shard_map/ppermute | solution.py:43
  186.4 18.5 %collective-permute-start.15 = (bf16[2,2,48,2048]{3,2,1,0:T(8,128)(2,1)}, bf16[2,2,48,2048]{3,2,1,0:T(8,128)(2,1)S(1)}, u32[]{:S(2)}, u32[]{:S(2)}) collective-permute-start(bf16[2,2,48,2048]{3,2,1,0:T(8,128)(2,1)} %bitcast.862), channel_id=1, source_target_pairs={{0,4},{1,5},{2,6},{3,7},{4,0},{5,1},{6,2},{7,3},{8,12},{9,13},{10,... | collective-permute-start | bytes 2359304 | tf_op jit(solution)/shard_map/ppermute | solution.py:43
  259.5 19.6 %collective-permute-start.25 = (bf16[2,4,8,2048]{3,2,1,0:T(8,128)(2,1)S(1)}, bf16[2,4,8,2048]{3,2,1,0:T(8,128)(2,1)S(1)}, u32[]{:S(2)}, u32[]{:S(2)}) collective-permute-start(bf16[2,4,8,2048]{3,2,1,0:T(8,128)(2,1)S(1)} %get-tuple-element.285), channel_id=1, source_target_pairs={{0,16},{1,17},{2,18},{3,19},{4,20},{5,21},{6,22},{7,23},{8,24},{9,... | collective-permute-start | bytes 786440 | tf_op jit(solution)/shard_map/ppermute | solution.py:43
  281.0 25.6 %collective-permute-start.71 = (bf16[40,2048]{1,0:T(8,128)(2,1)S(1)}, bf16[40,2048]{1,0:T(8,128)(2,1)S(1)}, u32[]{:S(2)}, u32[]{:S(2)}) collective-permute-start(bf16[40,2048]{1,0:T(8,128)(2,1)S(1)} %get-tuple-element.274), channel_id=1, source_target_pairs={{0,16},{1,17},{2,18},{3,19},{4,20},{5,21},{6,22},{7,23},{8,24},{9,... | collective-permute-start | bytes 491528 | tf_op jit(solution)/shard_map/ppermute | solution.py:43
  281.9 32.4 %collective-permute-start.47 = (bf16[40,2048]{1,0:T(8,128)(2,1)S(1)}, bf16[40,2048]{1,0:T(8,128)(2,1)S(1)}, u32[]{:S(2)}, u32[]{:S(2)}) collective-permute-start(bf16[40,2048]{1,0:T(8,128)(2,1)S(1)} %get-tuple-element.278), channel_id=1, source_target_pairs={{0,16},{1,17},{2,18},{3,19},{4,20},{5,21},{6,22},{7,23},{8,24},{9,... | collective-permute-start | bytes 491528 | tf_op jit(solution)/shard_map/ppermute | solution.py:43
  284.7 33.1 %collective-permute-start.39 = (bf16[40,2048]{1,0:T(8,128)(2,1)S(1)}, bf16[40,2048]{1,0:T(8,128)(2,1)S(1)}, u32[]{:S(2)}, u32[]{:S(2)}) collective-permute-start(bf16[40,2048]{1,0:T(8,128)(2,1)S(1)} %get-tuple-element.279), channel_id=1, source_target_pairs={{0,16},{1,17},{2,18},{3,19},{4,20},{5,21},{6,22},{7,23},{8,24},{9,... | collective-permute-start | bytes 491528 | tf_op jit(solution)/shard_map/ppermute | solution.py:43
  284.9 36.5 %collective-permute-start.63 = (bf16[40,2048]{1,0:T(8,128)(2,1)S(1)}, bf16[40,2048]{1,0:T(8,128)(2,1)S(1)}, u32[]{:S(2)}, u32[]{:S(2)}) collective-permute-start(bf16[40,2048]{1,0:T(8,128)(2,1)S(1)} %get-tuple-element.273), channel_id=1, source_target_pairs={{0,16},{1,17},{2,18},{3,19},{4,20},{5,21},{6,22},{7,23},{8,24},{9,... | collective-permute-start | bytes 491528 | tf_op jit(solution)/shard_map/ppermute | solution.py:43
  287.6 37.9 %collective-permute-start.55 = (bf16[48,2048]{1,0:T(8,128)(2,1)S(1)}, bf16[48,2048]{1,0:T(8,128)(2,1)S(1)}, u32[]{:S(2)}, u32[]{:S(2)}) collective-permute-start(bf16[48,2048]{1,0:T(8,128)(2,1)S(1)} %get-tuple-element.269), channel_id=1, source_target_pairs={{0,16},{1,17},{2,18},{3,19},{4,20},{5,21},{6,22},{7,23},{8,24},{9,... | collective-permute-start | bytes 589832 | tf_op jit(solution)/shard_map/ppermute | solution.py:43
  306.6 23.1 %collective-permute-start.26 = (bf16[48,2048]{1,0:T(8,128)(2,1)S(1)}, bf16[48,2048]{1,0:T(8,128)(2,1)S(1)}, u32[]{:S(2)}, u32[]{:S(2)}) collective-permute-start(bf16[48,2048]{1,0:T(8,128)(2,1)S(1)} %get-tuple-element.271), channel_id=1, source_target_pairs={{0,16},{1,17},{2,18},{3,19},{4,20},{5,21},{6,22},{7,23},{8,24},{9,... | collective-permute-start | bytes 589832 | tf_op jit(solution)/shard_map/ppermute | solution.py:43
  329.7 21.9 %collective-permute-start.27 = (bf16[2,48,2048]{2,1,0:T(8,128)(2,1)S(1)}, bf16[2,48,2048]{2,1,0:T(8,128)(2,1)S(1)}, u32[]{:S(2)}, u32[]{:S(2)}) collective-permute-start(bf16[2,48,2048]{2,1,0:T(8,128)(2,1)S(1)} %get-tuple-element.307), channel_id=1, source_target_pairs={{0,8},{1,9},{2,10},{3,11},{4,12},{5,13},{6,14},{7,15},{8,0},{9,1},... | collective-permute-start | bytes 1179656 | tf_op jit(solution)/shard_map/ppermute | solution.py:43
  331.9 32.2 %collective-permute-start.73 = (bf16[2,2,40,2048]{3,2,1,0:T(8,128)(2,1)S(1)}, bf16[2,2,40,2048]{3,2,1,0:T(8,128)(2,1)S(1)}, u32[]{:S(2)}, u32[]{:S(2)}) collective-permute-start(bf16[2,2,40,2048]{3,2,1,0:T(8,128)(2,1)S(1)} %get-tuple-element.239), channel_id=1, source_target_pairs={{0,8},{1,9},{2,10},{3,11},{4,12},{5,13},{6,14},{7,15},{8,0},{9,1},... | collective-permute-start | bytes 1966088 | tf_op jit(solution)/shard_map/ppermute | solution.py:43
  337.9 40.2 %collective-permute-start.49 = (bf16[2,2,40,2048]{3,2,1,0:T(8,128)(2,1)S(1)}, bf16[2,2,40,2048]{3,2,1,0:T(8,128)(2,1)S(1)}, u32[]{:S(2)}, u32[]{:S(2)}) collective-permute-start(bf16[2,2,40,2048]{3,2,1,0:T(8,128)(2,1)S(1)} %get-tuple-element.241), channel_id=1, source_target_pairs={{0,8},{1,9},{2,10},{3,11},{4,12},{5,13},{6,14},{7,15},{8,0},{9,1},... | collective-permute-start | bytes 1966088 | tf_op jit(solution)/shard_map/ppermute | solution.py:43
  341.6 39.4 %collective-permute-start.65 = (bf16[2,2,40,2048]{3,2,1,0:T(8,128)(2,1)S(1)}, bf16[2,2,40,2048]{3,2,1,0:T(8,128)(2,1)S(1)}, u32[]{:S(2)}, u32[]{:S(2)}) collective-permute-start(bf16[2,2,40,2048]{3,2,1,0:T(8,128)(2,1)S(1)} %get-tuple-element.237), channel_id=1, source_target_pairs={{0,4},{1,5},{2,6},{3,7},{4,0},{5,1},{6,2},{7,3},{8,12},{9,13},{10,... | collective-permute-start | bytes 1966088 | tf_op jit(solution)/shard_map/ppermute | solution.py:43
  349.8 33.3 %collective-permute-start.57 = (bf16[2,2,48,2048]{3,2,1,0:T(8,128)(2,1)S(1)}, bf16[2,2,48,2048]{3,2,1,0:T(8,128)(2,1)S(1)}, u32[]{:S(2)}, u32[]{:S(2)}) collective-permute-start(bf16[2,2,48,2048]{3,2,1,0:T(8,128)(2,1)S(1)} %get-tuple-element.227), channel_id=1, source_target_pairs={{0,2},{1,3},{2,0},{3,1},{4,6},{5,7},{6,4},{7,5},{8,10},{9,11},{10,... | collective-permute-start | bytes 2359304 | tf_op jit(solution)/shard_map/ppermute | solution.py:43
  351.6 54.6 %collective-permute-start.42 = (bf16[2,2,2,40,2048]{4,3,2,1,0:T(8,128)(2,1)S(1)}, bf16[2,2,2,40,2048]{4,3,2,1,0:T(8,128)(2,1)S(1)}, u32[]{:S(2)}, u32[]{:S(2)}) collective-permute-start(bf16[2,2,2,40,2048]{4,3,2,1,0:T(8,128)(2,1)S(1)} %get-tuple-element.206), channel_id=1, source_target_pairs={{0,8},{1,9},{2,10},{3,11},{4,12},{5,13},{6,14},{7,15},{8,0},{9,1},... | collective-permute-start | bytes 3932168 | tf_op jit(solution)/shard_map/ppermute | solution.py:43
  364.1 20.8 %collective-permute-start.28 = (bf16[2,2,48,2048]{3,2,1,0:T(8,128)(2,1)S(1)}, bf16[2,2,48,2048]{3,2,1,0:T(8,128)(2,1)S(1)}, u32[]{:S(2)}, u32[]{:S(2)}) collective-permute-start(bf16[2,2,48,2048]{3,2,1,0:T(8,128)(2,1)S(1)} %get-tuple-element.229), channel_id=1, source_target_pairs={{0,2},{1,3},{2,0},{3,1},{4,6},{5,7},{6,4},{7,5},{8,10},{9,11},{10,... | collective-permute-start | bytes 2359304 | tf_op jit(solution)/shard_map/ppermute | solution.py:43
  378.2 74.7 %collective-permute-start.74 = (bf16[2,2,2,40,2048]{4,3,2,1,0:T(8,128)(2,1)}, bf16[2,2,2,40,2048]{4,3,2,1,0:T(8,128)(2,1)S(1)}, u32[]{:S(2)}, u32[]{:S(2)}) collective-permute-start(bf16[2,2,2,40,2048]{4,3,2,1,0:T(8,128)(2,1)} %get-tuple-element.202), channel_id=1, source_target_pairs={{0,2},{1,3},{2,0},{3,1},{4,6},{5,7},{6,4},{7,5},{8,10},{9,11},{10,... | collective-permute-start | bytes 3932168 | tf_op jit(solution)/shard_map/ppermute | solution.py:43
  381.0 58.4 %collective-permute-start.50 = (bf16[2,2,2,40,2048]{4,3,2,1,0:T(8,128)(2,1)}, bf16[2,2,2,40,2048]{4,3,2,1,0:T(8,128)(2,1)}, u32[]{:S(2)}, u32[]{:S(2)}) collective-permute-start(bf16[2,2,2,40,2048]{4,3,2,1,0:T(8,128)(2,1)} %get-tuple-element.204), channel_id=1, source_target_pairs={{0,2},{1,3},{2,0},{3,1},{4,6},{5,7},{6,4},{7,5},{8,10},{9,11},{10,... | collective-permute-start | bytes 3932168 | tf_op jit(solution)/shard_map/ppermute | solution.py:43
  383.1 75.1 %collective-permute-start.66 = (bf16[2,2,2,40,2048]{4,3,2,1,0:T(8,128)(2,1)}, bf16[2,2,2,40,2048]{4,3,2,1,0:T(8,128)(2,1)}, u32[]{:S(2)}, u32[]{:S(2)}) collective-permute-start(bf16[2,2,2,40,2048]{4,3,2,1,0:T(8,128)(2,1)} %get-tuple-element.200), channel_id=1, source_target_pairs={{0,8},{1,9},{2,10},{3,11},{4,12},{5,13},{6,14},{7,15},{8,0},{9,1},... | collective-permute-start | bytes 3932168 | tf_op jit(solution)/shard_map/ppermute | solution.py:43
  384.9 156.9 %collective-permute-start.58 = (bf16[2,2,2,48,2048]{4,3,2,1,0:T(8,128)(2,1)}, bf16[2,2,2,48,2048]{4,3,2,1,0:T(8,128)(2,1)}, u32[]{:S(2)}, u32[]{:S(2)}) collective-permute-start(bf16[2,2,2,48,2048]{4,3,2,1,0:T(8,128)(2,1)} %get-tuple-element.190), channel_id=1, source_target_pairs={{0,4},{1,5},{2,6},{3,7},{4,0},{5,1},{6,2},{7,3},{8,12},{9,13},{10,... | collective-permute-start | bytes 4718600 | tf_op jit(solution)/shard_map/ppermute | solution.py:43
  406.2 141.9 %collective-permute-start.29 = (bf16[2,2,2,48,2048]{4,3,2,1,0:T(8,128)(2,1)}, bf16[2,2,2,48,2048]{4,3,2,1,0:T(8,128)(2,1)}, u32[]{:S(2)}, u32[]{:S(2)}) collective-permute-start(bf16[2,2,2,48,2048]{4,3,2,1,0:T(8,128)(2,1)} %get-tuple-element.192), channel_id=1, source_target_pairs={{0,4},{1,5},{2,6},{3,7},{4,0},{5,1},{6,2},{7,3},{8,12},{9,13},{10,... | collective-permute-start | bytes 4718600 | tf_op jit(solution)/shard_map/ppermute | solution.py:43
  517.9 150.4 %collective-permute-start.75 = (bf16[2,2,2,40,2048]{4,3,2,1,0:T(8,128)(2,1)}, bf16[2,2,2,40,2048]{4,3,2,1,0:T(8,128)(2,1)}, u32[]{:S(2)}, u32[]{:S(2)}) collective-permute-start(bf16[2,2,2,40,2048]{4,3,2,1,0:T(8,128)(2,1)} %bitcast.202), channel_id=1, source_target_pairs={{0,2},{1,3},{2,0},{3,1},{4,6},{5,7},{6,4},{7,5},{8,10},{9,11},{10,... | collective-permute-start | bytes 3932168 | tf_op jit(solution)/shard_map/ppermute | solution.py:43
  521.2 150.5 %collective-permute-start.67 = (bf16[2,2,2,40,2048]{4,3,2,1,0:T(8,128)(2,1)}, bf16[2,2,2,40,2048]{4,3,2,1,0:T(8,128)(2,1)}, u32[]{:S(2)}, u32[]{:S(2)}) collective-permute-start(bf16[2,2,2,40,2048]{4,3,2,1,0:T(8,128)(2,1)} %bitcast.184), channel_id=1, source_target_pairs={{0,8},{1,9},{2,10},{3,11},{4,12},{5,13},{6,14},{7,15},{8,0},{9,1},... | collective-permute-start | bytes 3932168 | tf_op jit(solution)/shard_map/ppermute | solution.py:43
  528.3 145.6 %collective-permute-start.51 = (bf16[2,2,2,40,2048]{4,3,2,1,0:T(8,128)(2,1)}, bf16[2,2,2,40,2048]{4,3,2,1,0:T(8,128)(2,1)}, u32[]{:S(2)}, u32[]{:S(2)}) collective-permute-start(bf16[2,2,2,40,2048]{4,3,2,1,0:T(8,128)(2,1)} %bitcast.147), channel_id=1, source_target_pairs={{0,2},{1,3},{2,0},{3,1},{4,6},{5,7},{6,4},{7,5},{8,10},{9,11},{10,... | collective-permute-start | bytes 3932168 | tf_op jit(solution)/shard_map/ppermute | solution.py:43
  541.8 134.5 %collective-permute-start.43 = (bf16[2,2,2,40,2048]{4,3,2,1,0:T(8,128)(2,1)}, bf16[2,2,2,40,2048]{4,3,2,1,0:T(8,128)(2,1)}, u32[]{:S(2)}, u32[]{:S(2)}) collective-permute-start(bf16[2,2,2,40,2048]{4,3,2,1,0:T(8,128)(2,1)} %bitcast.130), channel_id=1, source_target_pairs={{0,8},{1,9},{2,10},{3,11},{4,12},{5,13},{6,14},{7,15},{8,0},{9,1},... | collective-permute-start | bytes 3932168 | tf_op jit(solution)/shard_map/ppermute | solution.py:43
  623.2 42.1 %collective-permute-start.106 = (bf16[176,2048]{1,0:T(8,128)(2,1)}, bf16[176,2048]{1,0:T(8,128)(2,1)}, u32[]{:S(2)}, u32[]{:S(2)}) collective-permute-start(bf16[176,2048]{1,0:T(8,128)(2,1)} %dynamic-slice_bitcast_fusion.6), channel_id=1, source_target_pairs={{0,1},{1,0},{2,3},{3,2},{4,5},{5,4},{6,7},{7,6},{8,9},{9,8},{10,11... | collective-permute-start | bytes 2162696 | tf_op jit(solution)/shard_map/ppermute | solution.py:43
  665.3 111.6 %collective-permute-start.59 = (bf16[2,2,2,48,2048]{4,3,2,1,0:T(8,128)(2,1)}, bf16[2,2,2,48,2048]{4,3,2,1,0:T(8,128)(2,1)}, u32[]{:S(2)}, u32[]{:S(2)}) collective-permute-start(bf16[2,2,2,48,2048]{4,3,2,1,0:T(8,128)(2,1)} %bitcast.166), channel_id=1, source_target_pairs={{0,4},{1,5},{2,6},{3,7},{4,0},{5,1},{6,2},{7,3},{8,12},{9,13},{10,... | collective-permute-start | bytes 4718600 | tf_op jit(solution)/shard_map/ppermute | solution.py:43
  668.3 112.8 %collective-permute-start.35 = (bf16[2,2,2,48,2048]{4,3,2,1,0:T(8,128)(2,1)}, bf16[2,2,2,48,2048]{4,3,2,1,0:T(8,128)(2,1)}, u32[]{:S(2)}, u32[]{:S(2)}) collective-permute-start(bf16[2,2,2,48,2048]{4,3,2,1,0:T(8,128)(2,1)} %bitcast.113), channel_id=1, source_target_pairs={{0,4},{1,5},{2,6},{3,7},{4,0},{5,1},{6,2},{7,3},{8,12},{9,13},{10,... | collective-permute-start | bytes 4718600 | tf_op jit(solution)/shard_map/ppermute | solution.py:43
  671.7 97.6 %collective-permute-start.105 = (bf16[16,64,768]{2,1,0:T(8,128)(2,1)S(1)}, bf16[16,64,768]{2,1,0:T(8,128)(2,1)S(1)}, u32[]{:S(2)}, u32[]{:S(2)}) collective-permute-start(bf16[16,64,768]{2,1,0:T(8,128)(2,1)S(1)} %dynamic-slice_bitcast_fusion.3), channel_id=1, source_target_pairs={{0,1},{1,0},{2,3},{3,2},{4,5},{5,4},{6,7},{7,6},{8,9},{9,8},{10,11... | collective-permute-start | bytes 4718600 | tf_op jit(solution)/shard_map/ppermute | solution.py:43
  679.9 70.2 %collective-permute-start.68 = (bf16[2,2,40,2048]{3,2,1,0:T(8,128)(2,1)S(1)}, bf16[2,2,40,2048]{3,2,1,0:T(8,128)(2,1)S(1)}, u32[]{:S(2)}, u32[]{:S(2)}) collective-permute-start(bf16[2,2,40,2048]{3,2,1,0:T(8,128)(2,1)S(1)} %slice_bitcast_fusion.6), channel_id=1, source_target_pairs={{0,4},{1,5},{2,6},{3,7},{4,0},{5,1},{6,2},{7,3},{8,12},{9,13},{10,... | collective-permute-start | bytes 1966088 | tf_op jit(solution)/shard_map/ppermute | solution.py:43
  693.1 57.2 %collective-permute-start.52 = (bf16[2,2,40,2048]{3,2,1,0:T(8,128)(2,1)S(1)}, bf16[2,2,40,2048]{3,2,1,0:T(8,128)(2,1)S(1)}, u32[]{:S(2)}, u32[]{:S(2)}) collective-permute-start(bf16[2,2,40,2048]{3,2,1,0:T(8,128)(2,1)S(1)} %slice_bitcast_fusion.8), channel_id=1, source_target_pairs={{0,8},{1,9},{2,10},{3,11},{4,12},{5,13},{6,14},{7,15},{8,0},{9,1},... | collective-permute-start | bytes 1966088 | tf_op jit(solution)/shard_map/ppermute | solution.py:43
  750.1 131.9 %collective-permute-start.107 = (bf16[2,512,1536]{2,1,0:T(8,128)(2,1)}, bf16[2,512,1536]{2,1,0:T(8,128)(2,1)}, u32[]{:S(2)}, u32[]{:S(2)}) collective-permute-start(bf16[2,512,1536]{2,1,0:T(8,128)(2,1)} %dynamic-slice_bitcast_fusion), channel_id=1, source_target_pairs={{0,1},{1,0},{2,3},{3,2},{4,5},{5,4},{6,7},{7,6},{8,9},{9,8},{10,11... | collective-permute-start | bytes 9437192 | tf_op jit(solution)/shard_map/ppermute | solution.py:43
  771.9 283.8 %all-to-all-start.6 = ((bf16[16,64,768]{2,1,0:T(8,128)(2,1)}), bf16[16,64,768]{2,1,0:T(8,128)(2,1)S(1)}, u32[]{:S(2)}, u32[]{:S(2)}) async-start(bf16[16,64,768]{2,1,0:T(8,128)(2,1)} %fusion.5), calls=%async_computation.6 | async-start | bytes 3145728 | tf_op jit(solution)/shard_map/all_to_all | solution.py:683
  776.9 20.8 %collective-permute-start.53 = (bf16[2,40,2048]{2,1,0:T(8,128)(2,1)}, bf16[2,40,2048]{2,1,0:T(8,128)(2,1)S(1)}, u32[]{:S(2)}, u32[]{:S(2)}) collective-permute-start(bf16[2,40,2048]{2,1,0:T(8,128)(2,1)} %slice_bitcast_fusion.28), channel_id=1, source_target_pairs={{0,4},{1,5},{2,6},{3,7},{4,0},{5,1},{6,2},{7,3},{8,12},{9,13},{10,... | collective-permute-start | bytes 983048 | tf_op jit(solution)/shard_map/ppermute | solution.py:43
  781.1 19.1 %collective-permute-start.45 = (bf16[2,40,2048]{2,1,0:T(8,128)(2,1)S(1)}, bf16[2,40,2048]{2,1,0:T(8,128)(2,1)S(1)}, u32[]{:S(2)}, u32[]{:S(2)}) collective-permute-start(bf16[2,40,2048]{2,1,0:T(8,128)(2,1)S(1)} %copy-done.121), channel_id=1, source_target_pairs={{0,2},{1,3},{2,0},{3,1},{4,6},{5,7},{6,4},{7,5},{8,10},{9,11},{10,... | collective-permute-start | bytes 983048 | tf_op jit(solution)/shard_map/ppermute | solution.py:43
  784.9 53.9 %collective-permute-start.60 = (bf16[2,2,48,2048]{3,2,1,0:T(8,128)(2,1)S(1)}, bf16[2,2,48,2048]{3,2,1,0:T(8,128)(2,1)S(1)}, u32[]{:S(2)}, u32[]{:S(2)}) collective-permute-start(bf16[2,2,48,2048]{3,2,1,0:T(8,128)(2,1)S(1)} %slice_bitcast_fusion), channel_id=1, source_target_pairs={{0,2},{1,3},{2,0},{3,1},{4,6},{5,7},{6,4},{7,5},{8,10},{9,11},{10,... | collective-permute-start | bytes 2359304 | tf_op jit(solution)/shard_map/ppermute | solution.py:43
  786.6 52.6 %collective-permute-start.36 = (bf16[2,2,48,2048]{3,2,1,0:T(8,128)(2,1)S(1)}, bf16[2,2,48,2048]{3,2,1,0:T(8,128)(2,1)S(1)}, u32[]{:S(2)}, u32[]{:S(2)}) collective-permute-start(bf16[2,2,48,2048]{3,2,1,0:T(8,128)(2,1)S(1)} %slice_bitcast_fusion.2), channel_id=1, source_target_pairs={{0,2},{1,3},{2,0},{3,1},{4,6},{5,7},{6,4},{7,5},{8,10},{9,11},{10,... | collective-permute-start | bytes 2359304 | tf_op jit(solution)/shard_map/ppermute | solution.py:43
  797.8 28.4 %collective-permute-start.78 = (bf16[40,2048]{1,0:T(8,128)(2,1)S(1)}, bf16[40,2048]{1,0:T(8,128)(2,1)S(1)}, u32[]{:S(2)}, u32[]{:S(2)}) collective-permute-start(bf16[40,2048]{1,0:T(8,128)(2,1)S(1)} %slice_bitcast_fusion.50), channel_id=1, source_target_pairs={{0,16},{1,17},{2,18},{3,19},{4,20},{5,21},{6,22},{7,23},{8,24},{9,... | collective-permute-start | bytes 491528 | tf_op jit(solution)/shard_map/ppermute | solution.py:43
  800.3 32.9 %collective-permute-start.70 = (bf16[40,2048]{1,0:T(8,128)(2,1)S(1)}, bf16[40,2048]{1,0:T(8,128)(2,1)S(1)}, u32[]{:S(2)}, u32[]{:S(2)}) collective-permute-start(bf16[40,2048]{1,0:T(8,128)(2,1)S(1)} %slice_bitcast_fusion.52), channel_id=1, source_target_pairs={{0,16},{1,17},{2,18},{3,19},{4,20},{5,21},{6,22},{7,23},{8,24},{9,... | collective-permute-start | bytes 491528 | tf_op jit(solution)/shard_map/ppermute | solution.py:43
  833.2 246.4 %collective-permute-start.46 = (bf16[40,2048]{1,0:T(8,128)(2,1)}, bf16[40,2048]{1,0:T(8,128)(2,1)}, u32[]{:S(2)}, u32[]{:S(2)}) collective-permute-start(bf16[40,2048]{1,0:T(8,128)(2,1)} %slice_bitcast_fusion.56), channel_id=1, source_target_pairs={{0,16},{1,17},{2,18},{3,19},{4,20},{5,21},{6,22},{7,23},{8,24},{9,... | collective-permute-start | bytes 491528 | tf_op jit(solution)/shard_map/ppermute | solution.py:43
  839.5 22.4 %collective-permute-start.37 = (bf16[2,48,2048]{2,1,0:T(8,128)(2,1)S(1)}, bf16[2,48,2048]{2,1,0:T(8,128)(2,1)S(1)}, u32[]{:S(2)}, u32[]{:S(2)}) collective-permute-start(bf16[2,48,2048]{2,1,0:T(8,128)(2,1)S(1)} %slice_bitcast_fusion.16), channel_id=1, source_target_pairs={{0,8},{1,9},{2,10},{3,11},{4,12},{5,13},{6,14},{7,15},{8,0},{9,1},... | collective-permute-start | bytes 1179656 | tf_op jit(solution)/shard_map/ppermute | solution.py:43
  862.8 218.4 %collective-permute-start.38 = (bf16[48,2048]{1,0:T(8,128)(2,1)}, bf16[48,2048]{1,0:T(8,128)(2,1)}, u32[]{:S(2)}, u32[]{:S(2)}) collective-permute-start(bf16[48,2048]{1,0:T(8,128)(2,1)} %slice_bitcast_fusion.40), channel_id=1, source_target_pairs={{0,16},{1,17},{2,18},{3,19},{4,20},{5,21},{6,22},{7,23},{8,24},{9,... | collective-permute-start | bytes 589832 | tf_op jit(solution)/shard_map/ppermute | solution.py:43
  907.3 177.6 %collective-permute-start.108 = (bf16[512,1536]{1,0:T(8,128)(2,1)}, bf16[512,1536]{1,0:T(8,128)(2,1)}, u32[]{:S(2)}, u32[]{:S(2)}) collective-permute-start(bf16[512,1536]{1,0:T(8,128)(2,1)} %get-tuple-element.165), channel_id=1, source_target_pairs={{0,2},{1,3},{2,0},{3,1},{4,6},{5,7},{6,4},{7,5},{8,10},{9,11},{10,... | collective-permute-start | bytes 4718600 | tf_op jit(solution)/shard_map/ppermute | solution.py:43
  978.6 90.3 %collective-permute-start.101 = (bf16[2048,384]{1,0:T(8,128)(2,1)}, bf16[2048,384]{1,0:T(8,128)(2,1)}, u32[]{:S(2)}, u32[]{:S(2)}) collective-permute-start(bf16[2048,384]{1,0:T(8,128)(2,1)} %broadcast_select_fusion), channel_id=1, source_target_pairs={{0,1},{1,0},{2,3},{3,2},{4,5},{5,4},{6,7},{7,6},{8,9},{9,8},{10,11... | collective-permute-start | bytes 4718600 | tf_op jit(solution)/shard_map/ppermute | solution.py:43
  1055.5 39.7 %collective-permute-start.102 = (bf16[2,64,2048]{2,1,0:T(8,128)(2,1)}, bf16[2,64,2048]{2,1,0:T(8,128)(2,1)}, u32[]{:S(2)}, u32[]{:S(2)}) collective-permute-start(bf16[2,64,2048]{2,1,0:T(8,128)(2,1)} %dynamic-slice_bitcast_fusion.7), channel_id=1, source_target_pairs={{0,1},{1,0},{2,3},{3,2},{4,5},{5,4},{6,7},{7,6},{8,9},{9,8},{10,11... | collective-permute-start | bytes 1572872 | tf_op jit(solution)/shard_map/ppermute | solution.py:43
  1076.6 50.9 %all-to-all-start.4 = ((bf16[32,64,384]{2,1,0:T(8,128)(2,1)}), bf16[32,64,384]{2,1,0:T(8,128)(2,1)S(1)}, u32[]{:S(2)}, u32[]{:S(2)}) async-start(bf16[32,64,384]{2,1,0:T(8,128)(2,1)} %bitcast.789), calls=%async_computation.4 | async-start | bytes 3145728 | tf_op jit(solution)/shard_map/all_to_all | solution.py:705
  1096.7 26.7 %collective-permute-start.104 = (bf16[64,2048]{1,0:T(8,128)(2,1)S(1)}, bf16[64,2048]{1,0:T(8,128)(2,1)S(1)}, u32[]{:S(2)}, u32[]{:S(2)}) collective-permute-start(bf16[64,2048]{1,0:T(8,128)(2,1)S(1)} %get-tuple-element.249), channel_id=1, source_target_pairs={{16,0},{17,1},{0,2},{1,3},{18,4},{19,5},{2,6},{3,7},{20,8},{21,9},... | collective-permute-start | bytes 786440 | tf_op jit(solution)/shard_map/ppermute | solution.py:43
  1098.5 24.9 %collective-permute-start.103 = (bf16[64,2048]{1,0:T(8,128)(2,1)S(1)}, bf16[64,2048]{1,0:T(8,128)(2,1)S(1)}, u32[]{:S(2)}, u32[]{:S(2)}) collective-permute-start(bf16[64,2048]{1,0:T(8,128)(2,1)S(1)} %get-tuple-element.248), channel_id=1, source_target_pairs={{0,0},{1,1},{16,2},{17,3},{2,4},{3,5},{18,6},{19,7},{4,8},{5,9},{2... | collective-permute-start | bytes 786440 | tf_op jit(solution)/shard_map/ppermute | solution.py:43
  (218 other events, 2484.2 us)

commit v3 on v2

--- a/solution.py
+++ b/solution.py
@@ -14,6 +14,7 @@
 AXES = ("dp", "x", "core")
 CHIPS = ("dp", "x")
 SPLITS = (48, 40, 40)
+PARTS = 1
 LOW = (1, 2, 3)
 
 epsilon = 1e-06
@@ -61,6 +62,10 @@
     for bit in reversed(bits):
         value = add_low(value[0], swap(value[1], bit))
     return value
+
+
+def after(value, *others):
+    return lax.optimization_barrier((value, others))[0]
 
 
 def pieces(rows):
@@ -276,6 +281,119 @@
         ),
         compiler_params=pltpu.CompilerParams(vmem_limit_bytes=40 * 1024 * 1024),
     )(flags, shared, shared_other, expert, expert_other, extra)
+
+
+def expert_kernel(
+    sizes,
+    expert_ref,
+    rows_ref,
+    branch_ref,
+    mask_ref,
+    gate_up_ref,
+    down_ref,
+    hidden_ref,
+    grad_ref,
+    out_ref,
+    back_out,
+    joined,
+    back,
+):
+    shared_wide, expert_wide, tail_lane, experts = sizes
+    padded = shared_wide + expert_wide
+    joined[...] = mm(rows_ref[...], gate_up_ref[...])
+    branch = branch_ref[...].reshape(rows_ref.shape)
+    back[...] = mm_nt(branch, down_ref[...])
+
+    tail_at = 2 * shared_wide + expert_wide - 128
+    logits = joined[:, tail_at : tail_at + 128]
+    lane = lax.broadcasted_iota(jnp.int32, logits.shape, 1)
+    routed = (lane >= tail_lane) & (lane < tail_lane + experts)
+    top = jnp.max(jnp.where(routed, logits, negative), axis=1, keepdims=True)
+    powers = jnp.where(routed, jnp.exp(jnp.where(routed, logits - top, 0.0)), 0.0)
+    router_probs = powers / jnp.sum(powers, axis=1, keepdims=True)
+    one_expert = lane == tail_lane + expert_ref[0]
+    my_prob = jnp.sum(jnp.where(one_expert, router_probs, 0.0), axis=1, keepdims=True)
+    is_gate = lane == tail_lane + experts
+    gate_logit = jnp.sum(jnp.where(is_gate, logits, 0.0), axis=1, keepdims=True)
+    shared_weight = jax.nn.sigmoid(gate_logit)
+    mask = mask_ref[...]
+    alongs = []
+    at = 0
+    for wide, weight in ((shared_wide, shared_weight), (expert_wide, my_prob * mask)):
+        along = jnp.zeros_like(my_prob)
+        for start in range(0, wide, 128):
+            gate_at = 2 * at + start
+            gate = joined[:, gate_at : gate_at + 128]
+            up = joined[:, gate_at + wide : gate_at + wide + 128]
+            back_part = back[:, at + start : at + start + 128]
+            sigmoid_gate = jax.nn.sigmoid(gate)
+            silu = gate * sigmoid_gate
+            hidden = silu * up
+            hidden_ref[:, at + start : at + start + 128] = (hidden * weight).astype(BF16)
+            along = along + jnp.sum(hidden * back_part, axis=1, keepdims=True)
+            grad_hidden = back_part * weight
+            gate_grad = grad_hidden * up * sigmoid_gate * (1.0 + gate * (1.0 - sigmoid_gate))
+            grad_ref[:, gate_at + wide : gate_at + wide + 128] = (grad_hidden * silu).astype(BF16)
+            if gate_at != tail_at:
+                grad_ref[:, gate_at : gate_at + 128] = gate_grad.astype(BF16)
+            else:
+                tail_grad = gate_grad
+        alongs.append(along)
+        at += wide
+    logit_grad = router_probs * (alongs[1] * mask) * (jnp.where(one_expert, 1.0, 0.0) - my_prob)
+    shared_logit_grad = alongs[0] * shared_weight * (1.0 - shared_weight)
+    tail_grad = tail_grad + jnp.where(is_gate, shared_logit_grad, logit_grad)
+    grad_ref[:, tail_at : tail_at + 128] = tail_grad.astype(BF16)
+
+    out_ref[...] = mm(hidden_ref[...], down_ref[...]).astype(BF16)
+    back_out[...] = mm_nt(grad_ref[...], gate_up_ref[...]).astype(BF16)
+
+
+def expert_pass(sizes, my_expert, part, rows, branch, mask, gate_up, down):
+    shared_wide, expert_wide, _, _ = sizes
+    padded = shared_wide + expert_wide
+    count, width = rows.shape
+    own = count // branch.shape[0]
+    tile = 256
+    once = dict(pipeline_mode=pl.Buffered(1))
+
+    def at(i):
+        return (i, 0)
+
+    def fixed(i):
+        return (0, 0)
+
+    return pl.pallas_call(
+        lambda *refs: expert_kernel(sizes, *refs),
+        grid=(count // tile,),
+        in_specs=[
+            pl.BlockSpec(memory_space=pltpu.SMEM),
+            pl.BlockSpec((tile, width), at),
+            pl.BlockSpec((tile // own, own, width), lambda i: (i, part, 0)),
+            pl.BlockSpec((tile, 1), at),
+            pl.BlockSpec((width, 2 * padded), fixed, **once),
+            pl.BlockSpec((padded, width), fixed, **once),
+        ],
+        out_specs=[
+            pl.BlockSpec((tile, padded), at),
+            pl.BlockSpec((tile, 2 * padded), at),
+            pl.BlockSpec((tile, width), at),
+            pl.BlockSpec((tile, width), at),
+        ],
+        out_shape=[
+            shape_of((count, padded)),
+            shape_of((count, 2 * padded)),
+            shape_of((count, width)),
+            shape_of((count, width)),
+        ],
+        scratch_shapes=[pltpu.VMEM((tile, 2 * padded), F32), pltpu.VMEM((tile, padded), F32)],
+        cost_estimate=pl.CostEstimate(
+            flops=count * width * padded,
+            bytes_accessed=8 * count * width,
+            transcendentals=0,
+        ),
+        compiler_params=pltpu.CompilerParams(vmem_limit_bytes=58 * 1024 * 1024),
+    )(my_expert.reshape(1), rows, branch, mask, gate_up, down)
 
 
 def rotary_tables(positions):
@@ -365,7 +483,6 @@
     capacity = (5 * group_rows * TOP + 4 * experts - 1) // (4 * experts)
     score_scale = HEAD ** (-0.5)
     low_orders = rotations(())
-    full_orders = rotations(tuple(reversed(high)))
 
     small = jnp.concatenate(
         [
@@ -422,14 +539,13 @@
     live_own = (own_positions[None, :] < lengths[:, None]).astype(F32)[:, :, None]
     grad_out = cotangent.astype(F32)
     branch_own = (live_own * grad_out).astype(BF16).reshape(rows, width)
-    branch_parts = [
-        gather_bits(value, bits)
-        for value, bits in zip(pieces(branch_own), full_orders, strict=True)
-    ]
+    branch_own = after(branch_own, *token_parts)
+    branch_all = lax.all_gather(branch_own, CHIPS, axis=0)
 
     shared_pieces = whole_kernel(
         split_columns, [shape_of((chips, depth, 2 * shared_wide))], shared_gate_up
     )[0]
+    shared_pieces = after(shared_pieces, *token_parts)
     shared_in = lax.all_to_all(shared_pieces, CHIPS, split_axis=0, concat_axis=0, tiled=True)
     shared_other = swap(shared_in, 0)
     expert_rows = expert_gate_up.shape[1]
@@ -438,6 +554,7 @@
     )[0]
     keep_half = lax.dynamic_index_in_dim(expert_halves, x_bit, 0, keepdims=False)
     give_half = lax.dynamic_index_in_dim(expert_halves, 1 - x_bit, 0, keepdims=False)
+    give_half = after(give_half, *token_parts)
     expert_in = jnp.stack([keep_half, swap(give_half, 1)])
     expert_other = swap(expert_in, 0)
     extra = jnp.concatenate(
@@ -542,10 +659,13 @@
         found = jnp.concatenate(found).reshape(
             (2,) * (1 + len(high)) + (own_seq, piece, width)
         )
-        return undeal(found, part, high)
+        return found
 
     attended_parts = to_parts(attended.astype(BF16)[None])
-    attn_out = reduce_low([mm(value, o_rows) for value in attended_parts])
+    attn_out = undeal(
+        reduce_low([mm(value, o_rows) for value in attended_parts]), part, high
+    )
+    attn_out = after(attn_out, branch_all)
     inputs = tokens.astype(F32)
     residual = (inputs + live_own * attn_out.astype(F32)).reshape(rows, width)
     normal_two, factor_two = normalize(residual)
@@ -553,61 +673,60 @@
 
     expert_column = jnp.arange(experts, dtype=jnp.int32)[None, :]
     one_expert = (expert_column == my_expert).astype(F32)
-    out_parts = []
-    grad_parts = []
-    grad_gate_up = grad_down = 0.0
-    for normed, branch, bits, start in zip(
-        pieces(normed_own), branch_parts, full_orders, (0, 48, 88), strict=True
-    ):
-        count = normed.shape[0]
-        everyone = gather_bits(normed, bits)
-        lead = everyone.shape[:-1]
-        everyone = everyone.reshape(-1, width)
-        branch = branch.reshape(-1, width)
-        mask = jnp.take(
-            kept[:, start : start + count], me ^ jnp.asarray(relative(bits), jnp.int32), axis=0
-        ).reshape(-1, 1)
-        joined_gu = mm(everyone, gate_up_weight)
-        back = mm_nt(branch, down_weight)
-        router_probs = jax.nn.softmax(joined_gu[:, tail_at : tail_at + experts], axis=-1)
-        shared_weight = jax.nn.sigmoid(joined_gu[:, tail_at + experts : tail_at + experts + 1])
-        my_prob = jnp.sum(router_probs * one_expert, axis=1, keepdims=True)
-        hidden_low = []
-        joined_grad = []
-        alongs = []
-        at = 0
-        for wide, weight in ((shared_wide, shared_weight), (expert_wide, my_prob * mask)):
-            gate = joined_gu[:, 2 * at : 2 * at + wide]
-            up = joined_gu[:, 2 * at + wide : 2 * at + 2 * wide]
-            back_part = back[:, at : at + wide]
-            sigmoid_gate = jax.nn.sigmoid(gate)
-            hidden = gate * sigmoid_gate * up
-            hidden_low.append((hidden * weight).astype(BF16))
-            alongs.append(jnp.sum(hidden * back_part, axis=1, keepdims=True))
-            grad_hidden = back_part * weight
-            joined_grad.append(
-                grad_hidden * up * sigmoid_gate * (1.0 + gate * (1.0 - sigmoid_gate))
-            )
-            joined_grad.append(grad_hidden * gate * sigmoid_gate)
-            at += wide
-        logit_grad = router_probs * (alongs[1] * mask) * (one_expert - my_prob)
-        shared_logit_grad = alongs[0] * shared_weight * (1.0 - shared_weight)
-        tail = jnp.concatenate([logit_grad, shared_logit_grad], axis=1)
-        joined_grad[2] = joined_grad[2] + jnp.pad(
-            tail, ((0, 0), (expert_width, expert_wide - expert_width - experts - 1))
+    own_rows = rows // PARTS
+    everyone = [
+        lax.all_gather(
+            normed_own[number * own_rows : (number + 1) * own_rows], CHIPS, axis=0, tiled=True
         )
-        joined_grad = jnp.concatenate([value.astype(BF16) for value in joined_grad], axis=1)
-        hidden_low = jnp.concatenate(hidden_low, axis=1)
-        grad_down = grad_down + mm_tn(hidden_low, branch)
-        grad_gate_up = grad_gate_up + mm_tn(everyone, joined_grad)
-        back_rows = mm_nt(joined_grad, gate_up_weight)
-        grad_parts.append(scatter_bits(back_rows.astype(BF16).reshape(lead + (width,)), bits))
-        out_parts.append(
-            scatter_bits(mm(hidden_low, down_weight).astype(BF16).reshape(lead + (width,)), bits)
+        for number in range(PARTS)
+    ]
+    kept = kept.reshape(chips, 2, PARTS, own_rows)
+    kept = lax.dynamic_index_in_dim(kept, core, 1, keepdims=False)
+    masks = [kept[:, number].reshape(-1, 1) for number in range(PARTS)]
+    branch = [
+        branch_all[:, number * own_rows : (number + 1) * own_rows].reshape(-1, width)
+        for number in range(PARTS)
+    ]
+
+    sizes = (shared_wide, expert_wide, expert_width - expert_wide + 128, experts)
+
+    def expert_part(number, *others):
+        return expert_pass(
+            sizes,
+            my_expert,
+            number,
+            after(everyone[number], *others),
+            branch_all,
+            masks[number],
+            gate_up_weight,
+            down_weight,
         )
+
+    def reduce(value):
+        return lax.psum_scatter(value, CHIPS, scatter_dimension=0, tiled=True)
+
+    def weight_grad(number, total_grad, *others):
+        return total_grad + mm_tn(everyone[number], after(joined[number], total_grad, *others))
+
+    def down_grad(number, total_grad, *others):
+        return total_grad + mm_tn(after(hidden[number], total_grad, *others), branch[number])
+
+    hidden = [None] * PARTS
+    joined = [None] * PARTS
+    outs = [None] * PARTS
+    grad_parts = [None] * PARTS
+    before_it = ()
+    for number in range(PARTS):
+        hidden[number], joined[number], outs[number], back_rows = expert_part(number, *before_it)
+        grad_parts[number] = reduce(back_rows)
+        before_it = (joined[number],)
+    grad_gate_up = 0.0
+    grad_down = 0.0
+    for number in range(PARTS):
+        grad_gate_up = weight_grad(number, grad_gate_up, joined[-1], *grad_parts[:-1])
+    for number in range(PARTS):
+        grad_down = down_grad(number, grad_down, grad_gate_up)
     live_rows = jnp.broadcast_to(live_own, (sequences, piece, 1)).reshape(rows, 1)
-    moe_out = jnp.concatenate(out_parts).astype(F32)
-    mixed = (residual + live_rows * moe_out).astype(BF16).reshape(tokens.shape)
     grad_normed = jnp.concatenate(grad_parts).astype(F32)
     grad_residual_in, grad_gain_moe = norm_back(grad_normed, normal_two, factor_two, gain_moe)
     grad_residual = grad_out.reshape(rows, width) + grad_residual_in
@@ -619,6 +738,7 @@
             pieces(deal(attn_grad, part, high).reshape(rows, width)), low_orders, strict=True
         )
     ]
+    attn_grad_parts[0] = after(attn_grad_parts[0], grad_down)
     attended_grads = []
     grad_o = 0.0
     for value, ahead, bits in zip(attn_grad_parts, attended_parts, low_orders, strict=True):
@@ -626,7 +746,49 @@
         back = mm_nt(flat, o_rows).astype(BF16).reshape(value.shape[:-1] + (2 * HEAD,))
         attended_grads.append(to_order(back, bits, wanted))
         grad_o = grad_o + mm_tn(ahead, flat)
-    attended_grad = jnp.concatenate(attended_grads, axis=-2)
+    outs = [after(value, *attn_grad_parts) for value in outs]
+    moe_out = jnp.concatenate([reduce(value) for value in outs]).astype(F32)
+
+    def pick(value, axis, number):
+        return lax.dynamic_index_in_dim(value, number, axis, keepdims=False)
+
+    def to_core(value, axis):
+        given_rows = swap(pick(value, axis, 1 - core), 0)
+        return pick(value, axis, core).astype(F32) + given_rows.astype(F32)
+
+    def to_owners(vectors):
+        vectors = vectors.reshape(-1, total, depth).transpose(1, 0, 2)
+        vectors = lax.all_to_all(vectors, AXES, split_axis=0, concat_axis=0, tiled=True)
+        return jnp.sum(vectors, axis=0)
+
+    tail_grads = grad_gate_up[:, tail_at : tail_at + experts + 1]
+    grad_gate_up = grad_gate_up.astype(BF16)
+    grad_shared_gu = to_core(
+        grad_gate_up[:, : 2 * shared_wide].reshape(chips, 2, depth, 2 * shared_wide), 1
+    ).astype(BF16)
+    grad_expert_gu = to_core(
+        grad_gate_up[:, 2 * shared_wide :].reshape(2, 2, expert_rows, 2 * expert_wide), 1
+    ).astype(BF16)
+    grad_down = grad_down.astype(BF16)
+    grad_shared_down = to_core(grad_down[:shared_width].reshape(2, -1, width), 0)
+    grad_expert_down = to_core(
+        grad_down[shared_wide : shared_wide + expert_width].reshape(2, -1, width), 0
+    )
+    vectors = to_owners(jnp.concatenate([grad_gain_moe[None], tail_grads.T], axis=0))
+    attended_grad = after(
+        jnp.concatenate(attended_grads, axis=-2), grad_shared_gu, grad_expert_gu
+    )
+    grad_shared_gu = lax.all_to_all(
+        grad_shared_gu, CHIPS, split_axis=0, concat_axis=0, tiled=True
+    )
+    mine_gu = pick(grad_expert_gu, 0, x_bit)
+    theirs_gu = swap(pick(grad_expert_gu, 0, 1 - x_bit), 1)
+    grad_o = to_core(grad_o.astype(BF16).reshape(uppers, 2, depth, width), 1).astype(BF16)
+    grad_o = xor_order(grad_o, upper)
+    grad_o = sum(
+        permute(grad_o[k], [(b, a) for a, b in places]).astype(F32)
+        for k, places in enumerate(o_places)
+    )
     attended_grad = (
         attended_grad.reshape(8, parts, own_seq, piece, 2, HEAD)
         .transpose(2, 4, 0, 1, 3, 5)
@@ -651,67 +813,43 @@
             grad_value.astype(BF16),
         ]
     )
+    grads = after(grads, vectors)
     bias_grads = jnp.sum(grads.astype(F32), axis=(1, 3))
     grads_parts = to_parts(grads)
     grad_qkv = 0.0
-    normed_grads = []
     for value, normed in zip(grads_parts, normed_parts, strict=True):
-        normed_grads.append(mm_nt(value, qkv_weight))
         grad_qkv = grad_qkv + mm_tn(normed, value)
-    grad_normed_one = reduce_low(normed_grads).astype(F32).reshape(rows, width)
-    normal_one, factor_one = normalize(inputs.reshape(rows, width))
-    grad_input, grad_gain_attn = norm_back(grad_normed_one, normal_one, factor_one, gain_attn)
-    grad_tokens = (grad_residual + grad_input).astype(BF16).reshape(tokens.shape)
-
-    def pick(value, axis, number):
-        return lax.dynamic_index_in_dim(value, number, axis, keepdims=False)
-
-    def to_core(value, axis):
-        given_rows = swap(pick(value, axis, 1 - core), 0)
-        return pick(value, axis, core).astype(F32) + given_rows.astype(F32)
-
-    grad_down = grad_down.astype(BF16)
-    grad_shared_down = to_core(grad_down[:shared_width].reshape(2, -1, width), 0)
-    grad_expert_down = to_core(
-        grad_down[shared_wide : shared_wide + expert_width].reshape(2, -1, width), 0
-    )
-    tail_grads = grad_gate_up[:, tail_at : tail_at + experts + 1]
-    grad_gate_up = grad_gate_up.astype(BF16)
-    grad_shared_gu = to_core(
-        grad_gate_up[:, : 2 * shared_wide].reshape(chips, 2, depth, 2 * shared_wide), 1
-    ).astype(BF16)
-    grad_shared_gu = lax.all_to_all(
-        grad_shared_gu, CHIPS, split_axis=0, concat_axis=0, tiled=True
-    )
+    grad_qkv = grad_qkv.astype(BF16)
+    low_head = grad_qkv[:, : 3 * HEAD]
+    high_head = grad_qkv[:, 3 * HEAD :]
+    give_head = jnp.where(core == 0, high_head, low_head)
+    grads_parts[0] = after(grads_parts[0], give_head)
+    keep_head = jnp.where(core == 0, low_head, high_head)
+    grad_qkv = lax.all_to_all(
+        add_low(keep_head, swap(give_head, 0)).reshape(total, depth, 3 * HEAD),
+        AXES,
+        split_axis=0,
+        concat_axis=0,
+        tiled=True,
+    )
+    grad_normed_one = reduce_low([mm_nt(value, qkv_weight) for value in grads_parts])
+    grad_normed_one = after(grad_normed_one, grad_shared_gu, theirs_gu, grad_o)
+    grad_normed_one = undeal(grad_normed_one, part, high).astype(F32).reshape(rows, width)
+    grad_qkv = whole_kernel(join_heads, [shape_of((depth, width), F32)] * 3, grad_qkv)
     grad_shared_gu = whole_kernel(
         join_columns, [shape_of((depth, 2 * chips * shared_width), F32)], grad_shared_gu
     )[0]
-    grad_expert_gu = to_core(
-        grad_gate_up[:, 2 * shared_wide :].reshape(2, 2, expert_rows, 2 * expert_wide), 1
-    ).astype(BF16)
     grad_expert_gu = whole_kernel(
         join_halves,
         [shape_of((expert_rows, 4 * expert_width), F32)],
         x_bit.reshape(1),
-        pick(grad_expert_gu, 0, x_bit),
-        swap(pick(grad_expert_gu, 0, 1 - x_bit), 1),
+        mine_gu,
+        theirs_gu,
     )[0][None]
-
-    grad_qkv = grad_qkv.astype(BF16)
-    low_head = grad_qkv[:, : 3 * HEAD]
-    high_head = grad_qkv[:, 3 * HEAD :]
-    given_head = swap(jnp.where(core == 0, high_head, low_head), 0)
-    grad_qkv = add_low(jnp.where(core == 0, low_head, high_head), given_head)
-    grad_qkv = lax.all_to_all(
-        grad_qkv.reshape(total, depth, 3 * HEAD), AXES, split_axis=0, concat_axis=0, tiled=True
-    )
-    grad_qkv = whole_kernel(join_heads, [shape_of((depth, width), F32)] * 3, grad_qkv)
-    grad_o = to_core(grad_o.astype(BF16).reshape(uppers, 2, depth, width), 1).astype(BF16)
-    grad_o = xor_order(grad_o, upper)
-    grad_o = sum(
-        permute(grad_o[k], [(b, a) for a, b in places]).astype(F32)
-        for k, places in enumerate(o_places)
-    )
+    normal_one, factor_one = normalize(inputs.reshape(rows, width))
+    grad_input, grad_gain_attn = norm_back(grad_normed_one, normal_one, factor_one, gain_attn)
+    grad_tokens = (grad_residual + grad_input).astype(BF16).reshape(tokens.shape)
+    mixed = (residual + live_rows * moe_out).astype(BF16).reshape(tokens.shape)
 
     bias_rows = lax.dynamic_update_slice_in_dim(
         jnp.zeros((3, heads // 2, 2 * HEAD), F32),
@@ -719,28 +857,21 @@
         pair,
         axis=1,
     ).reshape(3, width)
-
-    def to_owners(vectors):
-        vectors = vectors.reshape(-1, total, depth).transpose(1, 0, 2)
-        vectors = lax.all_to_all(vectors, AXES, split_axis=0, concat_axis=0, tiled=True)
-        return jnp.sum(vectors, axis=0)
-
-    vectors = to_owners(jnp.concatenate([bias_rows, grad_gain_moe[None], tail_grads.T], axis=0))
-    grad_gain_attn = to_owners(grad_gain_attn[None])[0]
+    ends = to_owners(jnp.concatenate([bias_rows, grad_gain_attn[None]], axis=0))
     return (
         mixed,
         grad_tokens,
-        grad_gain_attn,
+        ends[3],
         grad_qkv[0],
         grad_qkv[1],
         grad_qkv[2],
+        ends[0],
+        ends[1],
+        ends[2],
+        grad_o,
         vectors[0],
-        vectors[1],
-        vectors[2],
-        grad_o,
-        vectors[3],
-        vectors[4 : 4 + experts].T,
-        vectors[4 + experts],
+        vectors[1 : 1 + experts].T,
+        vectors[1 + experts],
         grad_shared_gu,
         grad_shared_down,
         grad_expert_gu,

time: 1140 us -> 1020 us (0.89)
  matrix products: 189 us -> 81.8 us
  Pallas kernels: 24.3 us -> 96.5 us
  other arithmetic: 136 us -> 77.9 us
  starting transfers between devices: 148 us -> 124 us
  local copies, waits for them, and re-layouts: 96.4 us -> 81.7 us
  between operations: 4.6 us -> 16.4 us
    ppermute x110 -> x62, waiting for transfers between devices: 521 us -> 291 us  [permute(): return lax.ppermute(value, AXES, pairs)]
    reduce_scatter x0 -> x2, waiting for transfers between devices: none -> 144 us  [reduce(): return lax.psum_scatter(value, CHIPS, scatter_dimension=0, tiled=True)]
    pallas_call x0 -> x1, Pallas kernels: none -> 72.9 us  [expert_pass(): pl.pallas_call(lambda *refs: expert_kernel(sizes, *refs), grid=(count //...]
    all_gather x0 -> x2, waiting for transfers between devices: none -> 53.2 us  [the longest x1 36.8 us: on_device(): lax.all_gather(normed_own[number * own_rows:(number + 1) * own_rows], CHI...]
    dot_general x13 -> x7, matrix products: 50.4 us -> 7.45 us  [mm(): lax.dot_general(a, b, (((1,), (0,)), ((), ())), preferred_element_type=F32)]
    dot_general x12 -> x6, matrix products: 48.2 us -> 5.52 us  [mm_nt(): lax.dot_general(a, b, (((1,), (1,)), ((), ())), preferred_element_type=F32)]
    ppermute x110 -> x62, starting transfers between devices: 119 us -> 85.7 us  [permute(): return lax.ppermute(value, AXES, pairs)]
    all_to_all x1, waiting for transfers between devices: 0.01 us -> 29.2 us  [on_device(): lax.all_to_all(add_low(keep_head, swap(give_head, 0)).reshape(total, dept...]
  transfers between devices with their start and end apart: 117 -> 73, of which waited for: 60 -> 36; matrix products, arithmetic and copies ran while one was open for 35% -> 21% of each run, Pallas kernels for 2% -> 2%
where the time goes in v3:
time: 1020 us; the launch traced here: 1010 us
  waiting for transfers between devices  530 us (52%)
  starting transfers between devices  124 us (12%)
  Pallas kernels  96.5 us (9%)
  matrix products  81.8 us (8%)
  local copies, waits for them, and re-layouts  81.7 us (8%)
  other arithmetic  77.9 us (8%)
  between operations  16.4 us (2%)
    ppermute x62, waiting for transfers between devices, permute(): return lax.ppermute(value, AXES, pairs)  291 us
    reduce_scatter x2, waiting for transfers between devices, reduce(): return lax.psum_scatter(value, CHIPS, scatter_dimension=0, tiled=True)  144 us
    ppermute x62, starting transfers between devices, permute(): return lax.ppermute(value, AXES, pairs)  85.7 us
    pallas_call x1, Pallas kernels, expert_pass(): pl.pallas_call(lambda *refs: expert_kernel(sizes, *refs), grid=(count //...  72.9 us
    dot_general x8, matrix products, mm_tn(): lax.dot_general(a, b, (((0,), (0,)), ((), ())), preferred_element_type=F32)  65.8 us
    all_gather x1, waiting for transfers between devices, on_device(): lax.all_gather(normed_own[number * own_rows:(number + 1) * own_rows], CHI...  36.8 us
    unnamed x216, local copies, waits for them, and re-layouts  29.4 us
    all_to_all x1, waiting for transfers between devices, on_device(): lax.all_to_all(add_low(keep_head, swap(give_head, 0)).reshape(total, dept...  29.2 us
  transfers between devices with their start and end apart: 73, of which 36 were waited for; matrix products, arithmetic and copies ran while one was open for 21% of the time, Pallas kernels for 2%

profile of v3, /device:TPU:0, one launch (start us, length us, event | category | flops | bytes accessed | tf_op | source)
XLA Modules:
  0.0 1008.3 jit_solution(9044399028784593780)
XLA Ops:
  7.2 3.7 collective-permute-start.12
  10.9 2.9 collective-permute-start.13
  16.2 5.0 all-to-all-start
  23.1 2.7 collective-permute-start
  31.1 8.1 all-to-all-done
  39.2 4.4 all-to-all-start.1
  53.2 7.3 collective-permute-done.6
  60.5 3.7 collective-permute-start.7
  64.4 10.2 %collective-permute-done.2 = bf16[48,2048]{1,0:T(8,128)(2,1)S(1)} collective-permute-done((bf16[48,2048]{1,0:T(8,128)(2,1)S(1)}, bf16[48,2048]{1,0:T(8,128)(2,1)S(1)}, u32[]{:S(2)}, u32[]{:S(2)}) %collective-permute-start.2) | collective-permute-done | bytes 196640 | tf_op jit(solution)/shard_map/ppermute | solution.py:44
  78.9 4.6 collective-permute-done.10
  89.0 8.1 collective-permute-done.8
  97.4 3.2 collective-permute-done.11
  102.9 3.7 fusion.15
  114.4 2.6 fusion.25
  124.8 2.9 collective-permute-start.18
  131.4 23.9 %collective-permute-done.18 = bf16[2,2,40,2048]{3,2,1,0:T(8,128)(2,1)S(1)} collective-permute-done((bf16[2,2,40,2048]{3,2,1,0:T(8,128)(2,1)S(1)}, bf16[2,2,40,2048]{3,2,1,0:T(8,128)(2,1)S(1)}, u32[]{:S(2)}, u32[]{:S(2)}) %collective-permute-start.18) | collective-permute-done | bytes 655392 | tf_op jit(solution)/shard_map/ppermute | solution.py:44
  159.0 6.4 collective-permute-done.19
  167.1 8.3 collective-permute-done.22
  176.9 5.1 collective-permute-done.23
  182.1 9.4 collective-permute-done.17
  193.3 29.8 %collective-permute-done.25 = bf16[2,4,8,2048]{3,2,1,0:T(8,128)(2,1)S(1)} collective-permute-done((bf16[2,4,8,2048]{3,2,1,0:T(8,128)(2,1)S(1)}, bf16[2,4,8,2048]{3,2,1,0:T(8,128)(2,1)S(1)}, u32[]{:S(2)}, u32[]{:S(2)}) %collective-permute-start.25) | collective-permute-done | bytes 262176 | tf_op jit(solution)/shard_map/ppermute | solution.py:44
  223.3 16.4 %all-gather.6.cloned.1.call-done = bf16[2048,2048]{1,0:T(8,128)(2,1)} async-done(((bf16[128,2048]{1,0:T(8,128)(2,1)}), bf16[2048,2048]{1,0:T(8,128)(2,1)}) %all-gather.6.cloned.1.call-update) | async-done | bytes 8388624 | tf_op jit(solution)/shard_map/all_gather | solution.py:543
  249.5 4.4 all-to-all-start.2
  253.9 55.3 %collective-permute-done.27 = bf16[512,1536]{1,0:T(8,128)(2,1)S(1)} collective-permute-done((bf16[512,1536]{1,0:T(8,128)(2,1)}, bf16[512,1536]{1,0:T(8,128)(2,1)S(1)}, u32[]{:S(2)}, u32[]{:S(2)}) %collective-permute-start.27) | collective-permute-done | bytes 1572896 | tf_op jit(solution)/shard_map/ppermute | solution.py:44
  331.7 3.4 shard_map.336.refs_5_
  337.3 10.3 %shard_map.335.refs_4_ = bf16[2048,2304]{1,0:T(8,128)(2,1)} custom-call(s32[2]{0:T(128)S(1)} %pad_add_fusion.flags_ref, bf16[16,64,768]{2,1,0:T(8,128)(2,1)} %all-to-all-done.2.shared_ref, bf16[16,64,768]{2,1,0:T(8,128)(2,1)} %collective-permute-done.26.shared_other, bf16[2,512,1536]{2,1,0:T(8,128)(2,1)S(1)} %pad_maximum_fusion.2.expert_ref, ...), custom_call_target="tpu_custom_call" | custom-call | bytes 28311552 | tf_op jit(solution)/shard_map/pallas_call | solution.py:264
  347.6 36.8 %all-gather.4.cloned.1.call-done.refs_1_ = bf16[2048,2048]{1,0:T(8,128)(2,1)} async-done(((bf16[128,2048]{1,0:T(8,128)(2,1)}), bf16[2048,2048]{1,0:T(8,128)(2,1)}) %all-gather.4.cloned.1.call-update) | async-done | bytes 8388624 | tf_op jit(solution)/shard_map/all_gather | solution.py:678
  384.4 72.9 %shard_map.337 = (bf16[2048,1152]{1,0:T(8,128)(2,1)}, bf16[2048,2304]{1,0:T(8,128)(2,1)}, bf16[2048,2048]{1,0:T(8,128)(2,1)}, bf16[2048,2048]{1,0:T(8,128)(2,1)}) custom-call(s32[1]{0:T(128)} %bitcast.90.refs_0_, bf16[2048,2048]{1,0:T(8,128)(2,1)} %all-gather.4.cloned.1.call-done.refs_1_, bf16[16,128,2048]{2,1,0:T(8,128)(2,1)} %bitcast.549, ...), custom_call_target="tpu_custom_call" | custom-call | flops 4831838208 | bytes 33554432 | tf_op jit(solution)/shard_map/pallas_call | solution.py:366
  457.4 28.4 %fusion.143 = (bf16[2048,2304]{1,0:T(8,128)(2,1)S(1)}, f32[2048,2304]{1,0:T(8,128)}) fusion(bf16[2048,2048]{1,0:T(8,128)(2,1)} %all-gather.4.cloned.1.call-done.refs_1_, bf16[2048,2304]{1,0:T(8,128)(2,1)} %get-tuple-element.44), kind=kOutput, calls=%fused_computation.388 | convolution fusion | flops 19332071424 | bytes 46137344 | tf_op jit(solution)/shard_map/dot_general | solution.py:32
  491.9 15.4 %fusion.144 = bf16[1152,2048]{1,0:T(8,128)(2,1)} fusion(bf16[2048,1152]{1,0:T(8,128)(2,1)} %get-tuple-element.45, bf16[2048,2048]{1,0:T(8,128)(2,1)} %all-gather.6.cloned.1.call-done), kind=kOutput, calls=%fused_computation.389 | convolution fusion | flops 9663676416 | bytes 17825792 | tf_op jit(solution)/shard_map/dot_general | solution.py:32
  507.4 2.7 slice.462
  511.7 121.8 %reduce-scatter.3.cloned.1.call-done = bf16[128,2048]{1,0:T(8,128)(2,1)} async-done(((bf16[2048,2048]{1,0:T(8,128)(2,1)}), bf16[128,2048]{1,0:T(8,128)(2,1)}) %reduce-scatter.3.cloned.1.call-update) | async-done | bytes 524304 | tf_op jit(solution)/shard_map/reduce_scatter | solution.py:706
  638.7 3.1 fusion.5
  641.8 9.1 collective-permute-done.31
  651.1 4.5 fusion.1
  656.5 7.0 all-to-all-start.3
  676.7 3.8 collective-permute-done.40
  686.1 5.5 all-to-all-start.4
  707.0 24.6 %collective-permute-done.38 = bf16[2,2,40,2048]{3,2,1,0:T(8,128)(2,1)S(1)} collective-permute-done((bf16[2,2,40,2048]{3,2,1,0:T(8,128)(2,1)S(1)}, bf16[2,2,40,2048]{3,2,1,0:T(8,128)(2,1)S(1)}, u32[]{:S(2)}, u32[]{:S(2)}) %collective-permute-start.38) | collective-permute-done | bytes 655392 | tf_op jit(solution)/shard_map/ppermute | solution.py:44
  732.8 3.1 convolution_bitcast_fusion
  745.2 2.8 copy.266
  751.3 4.5 fusion.115
  755.9 5.9 fusion.42
  769.7 7.0 fusion
  787.8 4.7 collective-permute-done.50
  796.9 28.8 %collective-permute-done.44 = bf16[2,2,48,2048]{3,2,1,0:T(8,128)(2,1)S(1)} collective-permute-done((bf16[2,2,48,2048]{3,2,1,0:T(8,128)(2,1)S(1)}, bf16[2,2,48,2048]{3,2,1,0:T(8,128)(2,1)S(1)}, u32[]{:S(2)}, u32[]{:S(2)}) %collective-permute-start.44) | collective-permute-done | bytes 786464 | tf_op jit(solution)/shard_map/ppermute | solution.py:44
  828.5 12.2 %collective-permute-start.45 = (bf16[2,48,2048]{2,1,0:T(8,128)(2,1)S(1)}, bf16[2,48,2048]{2,1,0:T(8,128)(2,1)S(1)}, u32[]{:S(2)}, u32[]{:S(2)}) collective-permute-start(bf16[2,48,2048]{2,1,0:T(8,128)(2,1)S(1)} %slice_bitcast_fusion), channel_id=1, source_target_pairs={{0,2},{1,3},{2,0},{3,1},{4,6},{5,7},{6,4},{7,5},{8,10},{9,11},{10,... | collective-permute-start | bytes 1179656 | tf_op jit(solution)/shard_map/ppermute | solution.py:44
  844.3 4.8 collective-permute-start.49
  850.1 12.5 %collective-permute-done.45 = bf16[2,48,2048]{2,1,0:T(8,128)(2,1)S(1)} collective-permute-done((bf16[2,48,2048]{2,1,0:T(8,128)(2,1)S(1)}, bf16[2,48,2048]{2,1,0:T(8,128)(2,1)S(1)}, u32[]{:S(2)}, u32[]{:S(2)}) %collective-permute-start.45) | collective-permute-done | bytes 393248 | tf_op jit(solution)/shard_map/ppermute | solution.py:44
  862.8 12.3 %collective-permute-done.49 = bf16[40,2048]{1,0:T(8,128)(2,1)S(1)} collective-permute-done((bf16[40,2048]{1,0:T(8,128)(2,1)S(1)}, bf16[40,2048]{1,0:T(8,128)(2,1)S(1)}, u32[]{:S(2)}, u32[]{:S(2)}) %collective-permute-start.49) | collective-permute-done | bytes 163872 | tf_op jit(solution)/shard_map/ppermute | solution.py:44
  881.4 2.6 slice.491
  884.0 3.9 slice.492
  888.4 12.5 %collective-permute-done.58 = bf16[2,4,8,2048]{3,2,1,0:T(8,128)(2,1)} collective-permute-done((bf16[2,4,8,2048]{3,2,1,0:T(8,128)(2,1)}, bf16[2,4,8,2048]{3,2,1,0:T(8,128)(2,1)}, u32[]{:S(2)}, u32[]{:S(2)}) %collective-permute-start.58) | collective-permute-done | bytes 262176 | tf_op jit(solution)/shard_map/ppermute | solution.py:44
  904.1 9.0 all-to-all-start.5
  913.2 4.2 add_convert_fusion
  917.3 3.1 all-to-all-done.5
  920.4 2.8 all-to-all-start.6
  923.2 2.8 dynamic-slice_bitcast_fusion.5
  927.5 3.1 collective-permute-done.60
  933.2 3.5 fusion.12
  939.6 3.3 shard_map.340
  945.8 29.2 %all-to-all-done.6.in_ref = bf16[32,64,384]{2,1,0:T(8,128)(2,1)S(1)} async-done(((bf16[32,64,384]{2,1,0:T(8,128)(2,1)}), bf16[32,64,384]{2,1,0:T(8,128)(2,1)S(1)}, u32[]{:S(2)}, u32[]{:S(2)}) %all-to-all-start.6) | async-done | bytes 1572896 | tf_op jit(solution)/shard_map/all_to_all | solution.py:828
  976.2 21.7 %reduce-scatter.5.cloned.1.call-done = bf16[128,2048]{1,0:T(8,128)(2,1)} async-done(((bf16[2048,2048]{1,0:T(8,128)(2,1)}), bf16[128,2048]{1,0:T(8,128)(2,1)}) %reduce-scatter.5.cloned.1.call-update) | async-done | bytes 524304 | tf_op jit(solution)/shard_map/reduce_scatter | solution.py:706
  998.0 3.3 fusion.59
  (566 shorter events, 207.3 us)
Async XLA Ops:
  7.2 39.4 %collective-permute-start.12 = (bf16[64,2048]{1,0:T(8,128)(2,1)}, bf16[64,2048]{1,0:T(8,128)(2,1)}, u32[]{:S(2)}, u32[]{:S(2)}) collective-permute-start(bf16[64,2048]{1,0:T(8,128)(2,1)} %param.33), channel_id=1, source_target_pairs={{0,0},{1,1},{2,16},{3,17},{4,2},{5,3},{6,18},{7,19},{8,4},{9,5},{1... | collective-permute-start | bytes 786440 | tf_op jit(solution)/shard_map/ppermute | solution.py:44
  10.9 35.7 %collective-permute-start.13 = (bf16[64,2048]{1,0:T(8,128)(2,1)}, bf16[64,2048]{1,0:T(8,128)(2,1)}, u32[]{:S(2)}, u32[]{:S(2)}) collective-permute-start(bf16[64,2048]{1,0:T(8,128)(2,1)} %param.33), channel_id=1, source_target_pairs={{0,16},{1,17},{2,0},{3,1},{4,18},{5,19},{6,2},{7,3},{8,20},{9,21},... | collective-permute-start | bytes 786440 | tf_op jit(solution)/shard_map/ppermute | solution.py:44
  16.2 23.0 %all-to-all-start = ((bf16[32,2,512]{2,1,0:T(2,128)(2,1)}), bf16[32,2,512]{2,1,0:T(2,128)(2,1)S(1)}, u32[]{:S(2)}, u32[]{:S(2)}) async-start(bf16[32,2,512]{2,1,0:T(2,128)(2,1)} %reshape.781), calls=%async_computation | async-start | bytes 131072 | tf_op jit(solution)/shard_map/all_to_all | solution.py:495
  23.1 22.2 %collective-permute-start = (bf16[2,4,8,2048]{3,2,1,0:T(8,128)(2,1)}, bf16[2,4,8,2048]{3,2,1,0:T(8,128)(2,1)}, u32[]{:S(2)}, u32[]{:S(2)}) collective-permute-start(bf16[2,4,8,2048]{3,2,1,0:T(8,128)(2,1)} %pad_maximum_fusion.37), channel_id=1, source_target_pairs={{0,16},{1,17},{2,18},{3,19},{4,20},{5,21},{6,22},{7,23},{8,24},{9,... | collective-permute-start | bytes 786440 | tf_op jit(solution)/shard_map/ppermute | solution.py:44
  39.2 63.0 %all-to-all-start.1 = ((bf16[32,64,384]{2,1,0:T(8,128)(2,1)}), bf16[32,64,384]{2,1,0:T(8,128)(2,1)S(1)}, u32[]{:S(2)}, u32[]{:S(2)}) async-start(bf16[32,64,384]{2,1,0:T(8,128)(2,1)} %shard_map.332), calls=%async_computation.1 | async-start | bytes 3145728 | tf_op jit(solution)/shard_map/all_to_all | solution.py:512
  43.6 196.1 %all-gather.6.cloned.1.call-start = ((), (), s32[]{:S(2)}) async-start(), calls=%async_computation.12 | async-start | bytes 8912896 | tf_op jit(solution)/shard_map/all_gather | solution.py:543
  47.9 37.8 %collective-permute-start.14 = (bf16[2,64,2048]{2,1,0:T(8,128)(2,1)S(1)}, bf16[2,64,2048]{2,1,0:T(8,128)(2,1)S(1)}, u32[]{:S(2)}, u32[]{:S(2)}) collective-permute-start(bf16[2,64,2048]{2,1,0:T(8,128)(2,1)S(1)} %pad_maximum_fusion.18), channel_id=1, source_target_pairs={{0,1},{1,0},{2,3},{3,2},{4,5},{5,4},{6,7},{7,6},{8,9},{9,8},{10,11... | collective-permute-start | bytes 1572872 | tf_op jit(solution)/shard_map/ppermute | solution.py:44
  48.4 12.1 %collective-permute-start.6 = (bf16[40,2048]{1,0:T(8,128)(2,1)S(1)}, bf16[40,2048]{1,0:T(8,128)(2,1)S(1)}, u32[]{:S(2)}, u32[]{:S(2)}) collective-permute-start(bf16[40,2048]{1,0:T(8,128)(2,1)S(1)} %get-tuple-element.199), channel_id=1, source_target_pairs={{0,2},{1,3},{2,0},{3,1},{4,6},{5,7},{6,4},{7,5},{8,10},{9,11},{10,... | collective-permute-start | bytes 491528 | tf_op jit(solution)/shard_map/ppermute | solution.py:44
  50.2 14.0 %collective-permute-start.9 = (bf16[40,2048]{1,0:T(8,128)(2,1)S(1)}, bf16[40,2048]{1,0:T(8,128)(2,1)S(1)}, u32[]{:S(2)}, u32[]{:S(2)}) collective-permute-start(bf16[40,2048]{1,0:T(8,128)(2,1)S(1)} %get-tuple-element.198), channel_id=1, source_target_pairs={{0,4},{1,5},{2,6},{3,7},{4,0},{5,1},{6,2},{7,3},{8,12},{9,13},{10,... | collective-permute-start | bytes 491528 | tf_op jit(solution)/shard_map/ppermute | solution.py:44
  51.8 22.8 %collective-permute-start.2 = (bf16[48,2048]{1,0:T(8,128)(2,1)S(1)}, bf16[48,2048]{1,0:T(8,128)(2,1)S(1)}, u32[]{:S(2)}, u32[]{:S(2)}) collective-permute-start(bf16[48,2048]{1,0:T(8,128)(2,1)S(1)} %get-tuple-element.195), channel_id=1, source_target_pairs={{0,8},{1,9},{2,10},{3,11},{4,12},{5,13},{6,14},{7,15},{8,0},{9,1},... | collective-permute-start | bytes 589832 | tf_op jit(solution)/shard_map/ppermute | solution.py:44
  60.5 15.7 %collective-permute-start.7 = (bf16[2,40,2048]{2,1,0:T(8,128)(2,1)S(1)}, bf16[2,40,2048]{2,1,0:T(8,128)(2,1)S(1)}, u32[]{:S(2)}, u32[]{:S(2)}) collective-permute-start(bf16[2,40,2048]{2,1,0:T(8,128)(2,1)S(1)} %get-tuple-element.215), channel_id=1, source_target_pairs={{0,4},{1,5},{2,6},{3,7},{4,0},{5,1},{6,2},{7,3},{8,12},{9,13},{10,... | collective-permute-start | bytes 983048 | tf_op jit(solution)/shard_map/ppermute | solution.py:44
  64.3 19.2 %collective-permute-start.10 = (bf16[2,40,2048]{2,1,0:T(8,128)(2,1)S(1)}, bf16[2,40,2048]{2,1,0:T(8,128)(2,1)S(1)}, u32[]{:S(2)}, u32[]{:S(2)}) collective-permute-start(bf16[2,40,2048]{2,1,0:T(8,128)(2,1)S(1)} %get-tuple-element.217), channel_id=1, source_target_pairs={{0,8},{1,9},{2,10},{3,11},{4,12},{5,13},{6,14},{7,15},{8,0},{9,1},... | collective-permute-start | bytes 983048 | tf_op jit(solution)/shard_map/ppermute | solution.py:44
  74.7 12.7 %collective-permute-start.3 = (bf16[2,48,2048]{2,1,0:T(8,128)(2,1)S(1)}, bf16[2,48,2048]{2,1,0:T(8,128)(2,1)S(1)}, u32[]{:S(2)}, u32[]{:S(2)}) collective-permute-start(bf16[2,48,2048]{2,1,0:T(8,128)(2,1)S(1)} %get-tuple-element.209), channel_id=1, source_target_pairs={{0,2},{1,3},{2,0},{3,1},{4,6},{5,7},{6,4},{7,5},{8,10},{9,11},{10,... | collective-permute-start | bytes 1179656 | tf_op jit(solution)/shard_map/ppermute | solution.py:44
  76.4 20.7 %collective-permute-start.8 = (bf16[2,2,40,2048]{3,2,1,0:T(8,128)(2,1)S(1)}, bf16[2,2,40,2048]{3,2,1,0:T(8,128)(2,1)S(1)}, u32[]{:S(2)}, u32[]{:S(2)}) collective-permute-start(bf16[2,2,40,2048]{3,2,1,0:T(8,128)(2,1)S(1)} %get-tuple-element.159), channel_id=1, source_target_pairs={{0,8},{1,9},{2,10},{3,11},{4,12},{5,13},{6,14},{7,15},{8,0},{9,1},... | collective-permute-start | bytes 1966088 | tf_op jit(solution)/shard_map/ppermute | solution.py:44
  83.6 17.0 %collective-permute-start.11 = (bf16[2,2,40,2048]{3,2,1,0:T(8,128)(2,1)S(1)}, bf16[2,2,40,2048]{3,2,1,0:T(8,128)(2,1)S(1)}, u32[]{:S(2)}, u32[]{:S(2)}) collective-permute-start(bf16[2,2,40,2048]{3,2,1,0:T(8,128)(2,1)S(1)} %get-tuple-element.161), channel_id=1, source_target_pairs={{0,2},{1,3},{2,0},{3,1},{4,6},{5,7},{6,4},{7,5},{8,10},{9,11},{10,... | collective-permute-start | bytes 1966088 | tf_op jit(solution)/shard_map/ppermute | solution.py:44
  88.7 18.3 %collective-permute-start.4 = (bf16[2,2,48,2048]{3,2,1,0:T(8,128)(2,1)}, bf16[2,2,48,2048]{3,2,1,0:T(8,128)(2,1)}, u32[]{:S(2)}, u32[]{:S(2)}) collective-permute-start(bf16[2,2,48,2048]{3,2,1,0:T(8,128)(2,1)} %get-tuple-element.153), channel_id=1, source_target_pairs={{0,4},{1,5},{2,6},{3,7},{4,0},{5,1},{6,2},{7,3},{8,12},{9,13},{10,... | collective-permute-start | bytes 2359304 | tf_op jit(solution)/shard_map/ppermute | solution.py:44
  107.0 277.4 %all-gather.4.cloned.1.call-start = ((), (), s32[]{:S(2)}) async-start(), calls=%async_computation.9 | async-start | bytes 8912896 | tf_op jit(solution)/shard_map/all_gather | solution.py:678
  124.8 30.5 %collective-permute-start.18 = (bf16[2,2,40,2048]{3,2,1,0:T(8,128)(2,1)S(1)}, bf16[2,2,40,2048]{3,2,1,0:T(8,128)(2,1)S(1)}, u32[]{:S(2)}, u32[]{:S(2)}) collective-permute-start(bf16[2,2,40,2048]{3,2,1,0:T(8,128)(2,1)S(1)} %bitcast.607), channel_id=1, source_target_pairs={{0,8},{1,9},{2,10},{3,11},{4,12},{5,13},{6,14},{7,15},{8,0},{9,1},... | collective-permute-start | bytes 1966088 | tf_op jit(solution)/shard_map/ppermute | solution.py:44
  128.5 28.9 %collective-permute-start.15 = (bf16[2,2,48,2048]{3,2,1,0:T(8,128)(2,1)S(1)}, bf16[2,2,48,2048]{3,2,1,0:T(8,128)(2,1)S(1)}, u32[]{:S(2)}, u32[]{:S(2)}) collective-permute-start(bf16[2,2,48,2048]{3,2,1,0:T(8,128)(2,1)S(1)} %bitcast.600), channel_id=1, source_target_pairs={{0,4},{1,5},{2,6},{3,7},{4,0},{5,1},{6,2},{7,3},{8,12},{9,13},{10,... | collective-permute-start | bytes 2359304 | tf_op jit(solution)/shard_map/ppermute | solution.py:44
  129.5 27.5 %collective-permute-start.21 = (bf16[2,2,40,2048]{3,2,1,0:T(8,128)(2,1)S(1)}, bf16[2,2,40,2048]{3,2,1,0:T(8,128)(2,1)S(1)}, u32[]{:S(2)}, u32[]{:S(2)}) collective-permute-start(bf16[2,2,40,2048]{3,2,1,0:T(8,128)(2,1)S(1)} %bitcast.608), channel_id=1, source_target_pairs={{0,2},{1,3},{2,0},{3,1},{4,6},{5,7},{6,4},{7,5},{8,10},{9,11},{10,... | collective-permute-start | bytes 1966088 | tf_op jit(solution)/shard_map/ppermute | solution.py:44
  155.5 9.9 collective-permute-start.19
  157.2 18.1 %collective-permute-start.22 = (bf16[2,40,2048]{2,1,0:T(8,128)(2,1)S(1)}, bf16[2,40,2048]{2,1,0:T(8,128)(2,1)S(1)}, u32[]{:S(2)}, u32[]{:S(2)}) collective-permute-start(bf16[2,40,2048]{2,1,0:T(8,128)(2,1)S(1)} %slice_bitcast_fusion.8), channel_id=1, source_target_pairs={{0,8},{1,9},{2,10},{3,11},{4,12},{5,13},{6,14},{7,15},{8,0},{9,1},... | collective-permute-start | bytes 983048 | tf_op jit(solution)/shard_map/ppermute | solution.py:44
  157.6 19.1 %collective-permute-start.16 = (bf16[2,48,2048]{2,1,0:T(8,128)(2,1)S(1)}, bf16[2,48,2048]{2,1,0:T(8,128)(2,1)S(1)}, u32[]{:S(2)}, u32[]{:S(2)}) collective-permute-start(bf16[2,48,2048]{2,1,0:T(8,128)(2,1)S(1)} %slice_bitcast_fusion.2), channel_id=1, source_target_pairs={{0,2},{1,3},{2,0},{3,1},{4,6},{5,7},{6,4},{7,5},{8,10},{9,11},{10,... | collective-permute-start | bytes 1179656 | tf_op jit(solution)/shard_map/ppermute | solution.py:44
  165.5 11.1 %collective-permute-start.20 = (bf16[40,2048]{1,0:T(8,128)(2,1)S(1)}, bf16[40,2048]{1,0:T(8,128)(2,1)S(1)}, u32[]{:S(2)}, u32[]{:S(2)}) collective-permute-start(bf16[40,2048]{1,0:T(8,128)(2,1)S(1)} %slice_bitcast_fusion.24), channel_id=1, source_target_pairs={{0,2},{1,3},{2,0},{3,1},{4,6},{5,7},{6,4},{7,5},{8,10},{9,11},{10,... | collective-permute-start | bytes 491528 | tf_op jit(solution)/shard_map/ppermute | solution.py:44
  176.9 14.6 %collective-permute-start.17 = (bf16[48,2048]{1,0:T(8,128)(2,1)S(1)}, bf16[48,2048]{1,0:T(8,128)(2,1)S(1)}, u32[]{:S(2)}, u32[]{:S(2)}) collective-permute-start(bf16[48,2048]{1,0:T(8,128)(2,1)S(1)} %slice_bitcast_fusion.16), channel_id=1, source_target_pairs={{0,8},{1,9},{2,10},{3,11},{4,12},{5,13},{6,14},{7,15},{8,0},{9,1},... | collective-permute-start | bytes 589832 | tf_op jit(solution)/shard_map/ppermute | solution.py:44
  193.2 29.9 %collective-permute-start.25 = (bf16[2,4,8,2048]{3,2,1,0:T(8,128)(2,1)S(1)}, bf16[2,4,8,2048]{3,2,1,0:T(8,128)(2,1)S(1)}, u32[]{:S(2)}, u32[]{:S(2)}) collective-permute-start(bf16[2,4,8,2048]{3,2,1,0:T(8,128)(2,1)S(1)} %get-tuple-element.189), channel_id=1, source_target_pairs={{0,16},{1,17},{2,18},{3,19},{4,20},{5,21},{6,22},{7,23},{8,24},{9,... | collective-permute-start | bytes 786440 | tf_op jit(solution)/shard_map/ppermute | solution.py:44
  246.4 62.8 %collective-permute-start.27 = (bf16[512,1536]{1,0:T(8,128)(2,1)}, bf16[512,1536]{1,0:T(8,128)(2,1)S(1)}, u32[]{:S(2)}, u32[]{:S(2)}) collective-permute-start(bf16[512,1536]{1,0:T(8,128)(2,1)} %get-tuple-element.39), channel_id=1, source_target_pairs={{0,2},{1,3},{2,0},{3,1},{4,6},{5,7},{6,4},{7,5},{8,10},{9,11},{10,... | collective-permute-start | bytes 4718600 | tf_op jit(solution)/shard_map/ppermute | solution.py:44
  249.5 67.2 %all-to-all-start.2 = ((bf16[16,64,768]{2,1,0:T(8,128)(2,1)}), bf16[16,64,768]{2,1,0:T(8,128)(2,1)}, u32[]{:S(2)}, u32[]{:S(2)}) async-start(bf16[16,64,768]{2,1,0:T(8,128)(2,1)} %shard_map.333), calls=%async_computation.2 | async-start | bytes 3145728 | tf_op jit(solution)/shard_map/all_to_all | solution.py:549
  253.9 379.6 %reduce-scatter.3.cloned.1.call-start = ((), (), s32[]{:S(2)}) async-start(), calls=%async_computation.10 | async-start | bytes 8912896 | tf_op jit(solution)/shard_map/reduce_scatter | solution.py:706
  312.7 24.6 %collective-permute-start.28 = (bf16[2,512,1536]{2,1,0:T(8,128)(2,1)S(1)}, bf16[2,512,1536]{2,1,0:T(8,128)(2,1)}, u32[]{:S(2)}, u32[]{:S(2)}) collective-permute-start(bf16[2,512,1536]{2,1,0:T(8,128)(2,1)S(1)} %pad_maximum_fusion.2.expert_ref), channel_id=1, source_target_pairs={{0,1},{1,0},{2,3},{3,2},{4,5},{5,4},{6,7},{7,6},{8,9},{9,8},{10,11... | collective-permute-start | bytes 9437192 | tf_op jit(solution)/shard_map/ppermute | solution.py:44
  312.7 18.9 %collective-permute-start.29 = (bf16[176,2048]{1,0:T(8,128)(2,1)}, bf16[176,2048]{1,0:T(8,128)(2,1)}, u32[]{:S(2)}, u32[]{:S(2)}) collective-permute-start(bf16[176,2048]{1,0:T(8,128)(2,1)} %shared_ref.1), channel_id=1, source_target_pairs={{0,1},{1,0},{2,3},{3,2},{4,5},{5,4},{6,7},{7,6},{8,9},{9,8},{10,11... | collective-permute-start | bytes 2162696 | tf_op jit(solution)/shard_map/ppermute | solution.py:44
  313.2 18.4 %collective-permute-start.30 = (bf16[352,2048]{1,0:T(8,128)(2,1)}, bf16[352,2048]{1,0:T(8,128)(2,1)}, u32[]{:S(2)}, u32[]{:S(2)}) collective-permute-start(bf16[352,2048]{1,0:T(8,128)(2,1)} %bitcast.105.expert_ref), channel_id=1, source_target_pairs={{0,1},{1,0},{2,3},{3,2},{4,5},{5,4},{6,7},{7,6},{8,9},{9,8},{10,11... | collective-permute-start | bytes 4325384 | tf_op jit(solution)/shard_map/ppermute | solution.py:44
  316.6 20.7 %collective-permute-start.26 = (bf16[16,64,768]{2,1,0:T(8,128)(2,1)}, bf16[16,64,768]{2,1,0:T(8,128)(2,1)}, u32[]{:S(2)}, u32[]{:S(2)}) collective-permute-start(bf16[16,64,768]{2,1,0:T(8,128)(2,1)} %all-to-all-done.2.shared_ref), channel_id=1, source_target_pairs={{0,1},{1,0},{2,3},{3,2},{4,5},{5,4},{6,7},{7,6},{8,9},{9,8},{10,11... | collective-permute-start | bytes 4718600 | tf_op jit(solution)/shard_map/ppermute | solution.py:44
  489.5 149.2 %collective-permute-start.42 = (bf16[16,64,768]{2,1,0:T(8,128)(2,1)}, bf16[16,64,768]{2,1,0:T(8,128)(2,1)}, u32[]{:S(2)}, u32[]{:S(2)}) collective-permute-start(bf16[16,64,768]{2,1,0:T(8,128)(2,1)} %dynamic-slice_bitcast_fusion.3), channel_id=1, source_target_pairs={{0,1},{1,0},{2,3},{3,2},{4,5},{5,4},{6,7},{7,6},{8,9},{9,8},{10,11... | collective-permute-start | bytes 4718600 | tf_op jit(solution)/shard_map/ppermute | solution.py:44
  491.4 159.6 %collective-permute-start.43 = (bf16[2,512,1536]{2,1,0:T(8,128)(2,1)}, bf16[2,512,1536]{2,1,0:T(8,128)(2,1)}, u32[]{:S(2)}, u32[]{:S(2)}) collective-permute-start(bf16[2,512,1536]{2,1,0:T(8,128)(2,1)} %dynamic-slice_bitcast_fusion), channel_id=1, source_target_pairs={{0,1},{1,0},{2,3},{3,2},{4,5},{5,4},{6,7},{7,6},{8,9},{9,8},{10,11... | collective-permute-start | bytes 9437192 | tf_op jit(solution)/shard_map/ppermute | solution.py:44
  636.5 14.4 %collective-permute-start.31 = (bf16[2,4,8,2048]{3,2,1,0:T(8,128)(2,1)S(1)}, bf16[2,4,8,2048]{3,2,1,0:T(8,128)(2,1)S(1)}, u32[]{:S(2)}, u32[]{:S(2)}) collective-permute-start(bf16[2,4,8,2048]{3,2,1,0:T(8,128)(2,1)S(1)} %pad_maximum_fusion.38), channel_id=1, source_target_pairs={{0,16},{1,17},{2,18},{3,19},{4,20},{5,21},{6,22},{7,23},{8,24},{9,... | collective-permute-start | bytes 786440 | tf_op jit(solution)/shard_map/ppermute | solution.py:44
  651.0 12.5 %collective-permute-start.32 = (bf16[2,4,8,2048]{3,2,1,0:T(8,128)(2,1)S(1)}, bf16[2,4,8,2048]{3,2,1,0:T(8,128)(2,1)S(1)}, u32[]{:S(2)}, u32[]{:S(2)}) collective-permute-start(bf16[2,4,8,2048]{3,2,1,0:T(8,128)(2,1)S(1)} %get-tuple-element.179), channel_id=1, source_target_pairs={{0,1},{1,0},{2,3},{3,2},{4,5},{5,4},{6,7},{7,6},{8,9},{9,8},{10,11... | collective-permute-start | bytes 786440 | tf_op jit(solution)/shard_map/ppermute | solution.py:44
  656.5 29.1 %all-to-all-start.3 = ((f32[32,1,640]{2,1,0:T(1,128)}), f32[32,1,640]{2,1,0:T(1,128)S(1)}, u32[]{:S(2)}, u32[]{:S(2)}) async-start(f32[32,1,640]{2,1,0:T(1,128)} %reshape.783), calls=%async_computation.5 | async-start | bytes 163840 | tf_op jit(solution)/shard_map/all_to_all | solution.py:761
  667.0 7.7 collective-permute-start.33
  670.8 9.7 collective-permute-start.40
  673.5 25.9 %collective-permute-start.37 = (bf16[2,40,2048]{2,1,0:T(8,128)(2,1)}, bf16[2,40,2048]{2,1,0:T(8,128)(2,1)}, u32[]{:S(2)}, u32[]{:S(2)}) collective-permute-start(bf16[2,40,2048]{2,1,0:T(8,128)(2,1)} %get-tuple-element.213), channel_id=1, source_target_pairs={{0,4},{1,5},{2,6},{3,7},{4,0},{5,1},{6,2},{7,3},{8,12},{9,13},{10,... | collective-permute-start | bytes 983048 | tf_op jit(solution)/shard_map/ppermute | solution.py:44
  675.5 27.1 %collective-permute-start.34 = (bf16[2,48,2048]{2,1,0:T(8,128)(2,1)}, bf16[2,48,2048]{2,1,0:T(8,128)(2,1)}, u32[]{:S(2)}, u32[]{:S(2)}) collective-permute-start(bf16[2,48,2048]{2,1,0:T(8,128)(2,1)} %get-tuple-element.207), channel_id=1, source_target_pairs={{0,2},{1,3},{2,0},{3,1},{4,6},{5,7},{6,4},{7,5},{8,10},{9,11},{10,... | collective-permute-start | bytes 1179656 | tf_op jit(solution)/shard_map/ppermute | solution.py:44
  681.7 23.6 %collective-permute-start.41 = (bf16[2,2,40,2048]{3,2,1,0:T(8,128)(2,1)}, bf16[2,2,40,2048]{3,2,1,0:T(8,128)(2,1)}, u32[]{:S(2)}, u32[]{:S(2)}) collective-permute-start(bf16[2,2,40,2048]{3,2,1,0:T(8,128)(2,1)} %get-tuple-element.155), channel_id=1, source_target_pairs={{0,2},{1,3},{2,0},{3,1},{4,6},{5,7},{6,4},{7,5},{8,10},{9,11},{10,... | collective-permute-start | bytes 1966088 | tf_op jit(solution)/shard_map/ppermute | solution.py:44
  684.6 191.4 %collective-permute-start.53 = (bf16[512,1536]{1,0:T(8,128)(2,1)}, bf16[512,1536]{1,0:T(8,128)(2,1)S(1)}, u32[]{:S(2)}, u32[]{:S(2)}) collective-permute-start(bf16[512,1536]{1,0:T(8,128)(2,1)} %get-tuple-element.117), channel_id=1, source_target_pairs={{0,2},{1,3},{2,0},{3,1},{4,6},{5,7},{6,4},{7,5},{8,10},{9,11},{10,... | collective-permute-start | bytes 4718600 | tf_op jit(solution)/shard_map/ppermute | solution.py:44
  686.1 189.9 %all-to-all-start.4 = ((bf16[16,64,768]{2,1,0:T(8,128)(2,1)}), bf16[16,64,768]{2,1,0:T(8,128)(2,1)S(1)}, u32[]{:S(2)}, u32[]{:S(2)}) async-start(bf16[16,64,768]{2,1,0:T(8,128)(2,1)} %fusion.5), calls=%async_computation.6 | async-start | bytes 3145728 | tf_op jit(solution)/shard_map/all_to_all | solution.py:781
  691.6 306.4 %reduce-scatter.5.cloned.1.call-start = ((), (), s32[]{:S(2)}) async-start(), calls=%async_computation.11 | async-start | bytes 8912896 | tf_op jit(solution)/shard_map/reduce_scatter | solution.py:706
  700.6 31.1 %collective-permute-start.38 = (bf16[2,2,40,2048]{3,2,1,0:T(8,128)(2,1)S(1)}, bf16[2,2,40,2048]{3,2,1,0:T(8,128)(2,1)S(1)}, u32[]{:S(2)}, u32[]{:S(2)}) collective-permute-start(bf16[2,2,40,2048]{3,2,1,0:T(8,128)(2,1)S(1)} %get-tuple-element.157), channel_id=1, source_target_pairs={{0,8},{1,9},{2,10},{3,11},{4,12},{5,13},{6,14},{7,15},{8,0},{9,1},... | collective-permute-start | bytes 1966088 | tf_op jit(solution)/shard_map/ppermute | solution.py:44
  703.7 32.2 %collective-permute-start.35 = (bf16[2,2,48,2048]{3,2,1,0:T(8,128)(2,1)S(1)}, bf16[2,2,48,2048]{3,2,1,0:T(8,128)(2,1)S(1)}, u32[]{:S(2)}, u32[]{:S(2)}) collective-permute-start(bf16[2,2,48,2048]{3,2,1,0:T(8,128)(2,1)S(1)} %get-tuple-element.151), channel_id=1, source_target_pairs={{0,4},{1,5},{2,6},{3,7},{4,0},{5,1},{6,2},{7,3},{8,12},{9,13},{10,... | collective-permute-start | bytes 2359304 | tf_op jit(solution)/shard_map/ppermute | solution.py:44
  764.3 28.2 %collective-permute-start.50 = (bf16[2,2,40,2048]{3,2,1,0:T(8,128)(2,1)}, bf16[2,2,40,2048]{3,2,1,0:T(8,128)(2,1)}, u32[]{:S(2)}, u32[]{:S(2)}) collective-permute-start(bf16[2,2,40,2048]{3,2,1,0:T(8,128)(2,1)} %bitcast.183), channel_id=1, source_target_pairs={{0,2},{1,3},{2,0},{3,1},{4,6},{5,7},{6,4},{7,5},{8,10},{9,11},{10,... | collective-permute-start | bytes 1966088 | tf_op jit(solution)/shard_map/ppermute | solution.py:44
  768.3 27.3 %collective-permute-start.47 = (bf16[2,2,40,2048]{3,2,1,0:T(8,128)(2,1)}, bf16[2,2,40,2048]{3,2,1,0:T(8,128)(2,1)}, u32[]{:S(2)}, u32[]{:S(2)}) collective-permute-start(bf16[2,2,40,2048]{3,2,1,0:T(8,128)(2,1)} %bitcast.176), channel_id=1, source_target_pairs={{0,8},{1,9},{2,10},{3,11},{4,12},{5,13},{6,14},{7,15},{8,0},{9,1},... | collective-permute-start | bytes 1966088 | tf_op jit(solution)/shard_map/ppermute | solution.py:44
  785.3 40.4 %collective-permute-start.44 = (bf16[2,2,48,2048]{3,2,1,0:T(8,128)(2,1)S(1)}, bf16[2,2,48,2048]{3,2,1,0:T(8,128)(2,1)S(1)}, u32[]{:S(2)}, u32[]{:S(2)}) collective-permute-start(bf16[2,2,48,2048]{3,2,1,0:T(8,128)(2,1)S(1)} %bitcast.599), channel_id=1, source_target_pairs={{0,4},{1,5},{2,6},{3,7},{4,0},{5,1},{6,2},{7,3},{8,12},{9,13},{10,... | collective-permute-start | bytes 2359304 | tf_op jit(solution)/shard_map/ppermute | solution.py:44
  787.1 41.4 %collective-permute-start.56 = (bf16[64,2048]{1,0:T(8,128)(2,1)S(1)}, bf16[64,2048]{1,0:T(8,128)(2,1)S(1)}, u32[]{:S(2)}, u32[]{:S(2)}) collective-permute-start(bf16[64,2048]{1,0:T(8,128)(2,1)S(1)} %get-tuple-element.171), channel_id=1, source_target_pairs={{16,0},{17,1},{0,2},{1,3},{18,4},{19,5},{2,6},{3,7},{20,8},{21,9},... | collective-permute-start | bytes 786440 | tf_op jit(solution)/shard_map/ppermute | solution.py:44
  792.5 48.2 %collective-permute-start.55 = (bf16[64,2048]{1,0:T(8,128)(2,1)S(1)}, bf16[64,2048]{1,0:T(8,128)(2,1)S(1)}, u32[]{:S(2)}, u32[]{:S(2)}) collective-permute-start(bf16[64,2048]{1,0:T(8,128)(2,1)S(1)} %get-tuple-element.170), channel_id=1, source_target_pairs={{0,0},{1,1},{16,2},{17,3},{2,4},{3,5},{18,6},{19,7},{4,8},{5,9},{2... | collective-permute-start | bytes 786440 | tf_op jit(solution)/shard_map/ppermute | solution.py:44
  795.6 46.0 %collective-permute-start.51 = (bf16[2,40,2048]{2,1,0:T(8,128)(2,1)S(1)}, bf16[2,40,2048]{2,1,0:T(8,128)(2,1)S(1)}, u32[]{:S(2)}, u32[]{:S(2)}) collective-permute-start(bf16[2,40,2048]{2,1,0:T(8,128)(2,1)S(1)} %slice_bitcast_fusion.4), channel_id=1, source_target_pairs={{0,8},{1,9},{2,10},{3,11},{4,12},{5,13},{6,14},{7,15},{8,0},{9,1},... | collective-permute-start | bytes 983048 | tf_op jit(solution)/shard_map/ppermute | solution.py:44
  825.7 18.5 %collective-permute-start.48 = (bf16[2,40,2048]{2,1,0:T(8,128)(2,1)S(1)}, bf16[2,40,2048]{2,1,0:T(8,128)(2,1)S(1)}, u32[]{:S(2)}, u32[]{:S(2)}) collective-permute-start(bf16[2,40,2048]{2,1,0:T(8,128)(2,1)S(1)} %slice_bitcast_fusion.6), channel_id=1, source_target_pairs={{0,4},{1,5},{2,6},{3,7},{4,0},{5,1},{6,2},{7,3},{8,12},{9,13},{10,... | collective-permute-start | bytes 983048 | tf_op jit(solution)/shard_map/ppermute | solution.py:44
  828.5 34.1 %collective-permute-start.45 = (bf16[2,48,2048]{2,1,0:T(8,128)(2,1)S(1)}, bf16[2,48,2048]{2,1,0:T(8,128)(2,1)S(1)}, u32[]{:S(2)}, u32[]{:S(2)}) collective-permute-start(bf16[2,48,2048]{2,1,0:T(8,128)(2,1)S(1)} %slice_bitcast_fusion), channel_id=1, source_target_pairs={{0,2},{1,3},{2,0},{3,1},{4,6},{5,7},{6,4},{7,5},{8,10},{9,11},{10,... | collective-permute-start | bytes 1179656 | tf_op jit(solution)/shard_map/ppermute | solution.py:44
  841.7 8.3 collective-permute-start.52
  844.3 30.8 %collective-permute-start.49 = (bf16[40,2048]{1,0:T(8,128)(2,1)S(1)}, bf16[40,2048]{1,0:T(8,128)(2,1)S(1)}, u32[]{:S(2)}, u32[]{:S(2)}) collective-permute-start(bf16[40,2048]{1,0:T(8,128)(2,1)S(1)} %slice_bitcast_fusion.20), channel_id=1, source_target_pairs={{0,2},{1,3},{2,0},{3,1},{4,6},{5,7},{6,4},{7,5},{8,10},{9,11},{10,... | collective-permute-start | bytes 491528 | tf_op jit(solution)/shard_map/ppermute | solution.py:44
  862.7 12.5 %collective-permute-start.46 = (bf16[48,2048]{1,0:T(8,128)(2,1)S(1)}, bf16[48,2048]{1,0:T(8,128)(2,1)S(1)}, u32[]{:S(2)}, u32[]{:S(2)}) collective-permute-start(bf16[48,2048]{1,0:T(8,128)(2,1)S(1)} %slice_bitcast_fusion.14), channel_id=1, source_target_pairs={{0,8},{1,9},{2,10},{3,11},{4,12},{5,13},{6,14},{7,15},{8,0},{9,1},... | collective-permute-start | bytes 589832 | tf_op jit(solution)/shard_map/ppermute | solution.py:44
  877.6 35.6 %collective-permute-start.59 = (bf16[2048,384]{1,0:T(8,128)(2,1)}, bf16[2048,384]{1,0:T(8,128)(2,1)}, u32[]{:S(2)}, u32[]{:S(2)}) collective-permute-start(bf16[2048,384]{1,0:T(8,128)(2,1)} %broadcast_select_fusion), channel_id=1, source_target_pairs={{0,1},{1,0},{2,3},{3,2},{4,5},{5,4},{6,7},{7,6},{8,9},{9,8},{10,11... | collective-permute-start | bytes 4718600 | tf_op jit(solution)/shard_map/ppermute | solution.py:44
  879.9 20.9 %collective-permute-start.58 = (bf16[2,4,8,2048]{3,2,1,0:T(8,128)(2,1)}, bf16[2,4,8,2048]{3,2,1,0:T(8,128)(2,1)}, u32[]{:S(2)}, u32[]{:S(2)}) collective-permute-start(bf16[2,4,8,2048]{3,2,1,0:T(8,128)(2,1)} %get-tuple-element.167), channel_id=1, source_target_pairs={{0,16},{1,17},{2,18},{3,19},{4,20},{5,21},{6,22},{7,23},{8,24},{9,... | collective-permute-start | bytes 786440 | tf_op jit(solution)/shard_map/ppermute | solution.py:44
  904.1 16.3 %all-to-all-start.5 = ((f32[32,1,256]{2,1,0:T(1,128)}), f32[32,1,256]{2,1,0:T(1,128)S(1)}, u32[]{:S(2)}, u32[]{:S(2)}) async-start(f32[32,1,256]{2,1,0:T(1,128)} %reshape.785), calls=%async_computation.7 | async-start | bytes 65536 | tf_op jit(solution)/shard_map/all_to_all | solution.py:761
  920.4 54.6 %all-to-all-start.6 = ((bf16[32,64,384]{2,1,0:T(8,128)(2,1)}), bf16[32,64,384]{2,1,0:T(8,128)(2,1)S(1)}, u32[]{:S(2)}, u32[]{:S(2)}) async-start(bf16[32,64,384]{2,1,0:T(8,128)(2,1)} %bitcast.557), calls=%async_computation.8 | async-start | bytes 3145728 | tf_op jit(solution)/shard_map/all_to_all | solution.py:828
  926.0 7.2 collective-permute-start.61
  (111 other events, 1593.2 us)
Sparse Core Ops, SparseCore 0:
  107.1 132.5 all-gather.5
  243.0 141.2 all-gather.3
  457.4 176.0 reduce-scatter.2
  769.8 228.1 reduce-scatter.4

commit v4 on v3

--- a/solution.py
+++ b/solution.py
@@ -14,7 +14,6 @@
 AXES = ("dp", "x", "core")
 CHIPS = ("dp", "x")
 SPLITS = (48, 40, 40)
-PARTS = 1
 LOW = (1, 2, 3)
 
 epsilon = 1e-06
@@ -66,6 +65,76 @@
 
 def after(value, *others):
     return lax.optimization_barrier((value, others))[0]
+
+
+def together(*lists):
+    return lax.optimization_barrier(tuple(tuple(values) for values in lists))
+
+
+def gather_parts(parts, orders):
+    parts = list(parts)
+    for step in range(len(orders[0])):
+        got = [swap(part, order[step]) for part, order in zip(parts, orders, strict=True)]
+        parts = [jnp.stack(pair) for pair in zip(*together(parts, got), strict=True)]
+    return parts
+
+
+def rest_of(high, order):
+    return tuple(reversed(high)) + order
+
+
+class Gather:
+    def __init__(self, rows, high):
+        self.value = gather_bits(rows, tuple(reversed(high)))
+
+    def split(self):
+        self.parts = pieces(self.value)
+        self.orders = rotations(())
+
+    def step(self):
+        got = [swap(part, order[0]) for part, order in zip(self.parts, self.orders, strict=True)]
+        self.pairs = list(zip(*together(self.parts, got), strict=True))
+        self.orders = [order[1:] for order in self.orders]
+        self.parts = [jnp.stack(pair) for pair in self.pairs]
+        return got
+
+    def whole(self):
+        width = self.value.shape[-1]
+        return jnp.concatenate([half.reshape(-1, width) for pair in self.pairs for half in pair])
+
+
+class Reduction:
+    def __init__(self, value, high, chips):
+        self.high = tuple(reversed(high))
+        self.bits = [order[::-1] for order in rotations(())]
+        width = value.shape[-1]
+        start = 0
+        self.keep = []
+        self.give = []
+        for count in SPLITS:
+            half = chips // 2 * count
+            shape = (2,) * (2 + len(high)) + (count, width)
+            self.keep.append(value[start : start + half].reshape(shape))
+            self.give.append(value[start + half : start + 2 * half].reshape(shape))
+            start += 2 * half
+
+    def send(self, *others):
+        give = after(tuple(self.give), *others) if others else self.give
+        self.got = [swap(part, bits[0]) for part, bits in zip(give, self.bits, strict=True)]
+        self.bits = [bits[1:] for bits in self.bits]
+        return self.got
+
+    def add(self):
+        keeps, gots = together(self.keep, self.got)
+        parts = [add_low(keep, got) for keep, got in zip(keeps, gots, strict=True)]
+        if self.bits[0]:
+            self.keep = [part[0] for part in parts]
+            self.give = [part[1] for part in parts]
+        else:
+            self.value = jnp.concatenate(parts, axis=-2)
+
+    def finish(self):
+        return scatter_bits(self.value, self.high)
 
 
 def pieces(rows):
@@ -114,10 +183,12 @@
     value = xor_order(value.reshape((parts, shape[0] // parts) + shape[1:]), part)
     value = value.reshape((2,) * (len(high) + 1) + value.shape[1:])
     left = len(high) + 1
+    arrived = []
     for bit in tuple(reversed(high)) + (0,):
         left -= 1
-        value = jnp.stack([value[0], swap(value[1], bit)], axis=left)
-    return value
+        arrived.append(swap(value[1], bit))
+        value = jnp.stack([value[0], arrived[-1]], axis=left)
+    return value, arrived
 
 
 def undeal(value, part, high):
@@ -301,8 +372,7 @@
     shared_wide, expert_wide, tail_lane, experts = sizes
     padded = shared_wide + expert_wide
     joined[...] = mm(rows_ref[...], gate_up_ref[...])
-    branch = branch_ref[...].reshape(rows_ref.shape)
-    back[...] = mm_nt(branch, down_ref[...])
+    back[...] = mm_nt(branch_ref[...], down_ref[...])
 
     tail_at = 2 * shared_wide + expert_wide - 128
     logits = joined[:, tail_at : tail_at + 128]
@@ -349,11 +419,53 @@
     back_out[...] = mm_nt(grad_ref[...], gate_up_ref[...]).astype(BF16)
 
 
-def expert_pass(sizes, my_expert, part, rows, branch, mask, gate_up, down):
+def relative_kernel(places_ref, in_ref, out_ref, sems):
+    group = in_ref.shape[0]
+    chips = pl.num_programs(0) * group
+    copies = []
+    start = 0
+    from_row = 0
+    for number, count in enumerate(SPLITS):
+        for own in range(group):
+            place = places_ref[number * chips + pl.program_id(0) * group + own]
+            copies.append(
+                pltpu.make_async_copy(
+                    in_ref.at[own, pl.ds(from_row, count), :],
+                    out_ref.at[pl.ds(pl.multiple_of(start + place * count, 8), count), :],
+                    sems.at[number * group + own],
+                )
+            )
+        start += chips * count
+        from_row += count
+    for copy in copies:
+        copy.start()
+    for copy in copies:
+        copy.wait()
+
+
+def to_relative(places, value):
+    chips, rows, width = value.shape
+    group = 4
+    return pl.pallas_call(
+        relative_kernel,
+        grid=(chips // group,),
+        out_shape=shape_of((chips * rows, width)),
+        in_specs=[
+            pl.BlockSpec(memory_space=pltpu.SMEM),
+            pl.BlockSpec((group, rows, width), lambda c: (c, 0, 0)),
+        ],
+        out_specs=pl.BlockSpec(memory_space=pl.ANY),
+        scratch_shapes=[pltpu.SemaphoreType.DMA((len(SPLITS) * group,))],
+        cost_estimate=pl.CostEstimate(
+            flops=0, bytes_accessed=4 * chips * rows * width, transcendentals=0
+        ),
+    )(places, value)
+
+
+def expert_pass(sizes, my_expert, rows, branch, mask, gate_up, down):
     shared_wide, expert_wide, _, _ = sizes
     padded = shared_wide + expert_wide
     count, width = rows.shape
-    own = count // branch.shape[0]
     tile = 256
     once = dict(pipeline_mode=pl.Buffered(1))
 
@@ -369,7 +481,7 @@
         in_specs=[
             pl.BlockSpec(memory_space=pltpu.SMEM),
             pl.BlockSpec((tile, width), at),
-            pl.BlockSpec((tile // own, own, width), lambda i: (i, part, 0)),
+            pl.BlockSpec((tile, width), at),
             pl.BlockSpec((tile, 1), at),
             pl.BlockSpec((width, 2 * padded), fixed, **once),
             pl.BlockSpec((padded, width), fixed, **once),
@@ -491,6 +603,8 @@
             jnp.zeros((2, depth), BF16),
         ]
     )
+    dealt_tokens, tokens_arrived = deal(tokens, part, high)
+    small = after(small, *tokens_arrived)
     small = jnp.broadcast_to(small[None], (total,) + small.shape)
     small = lax.all_to_all(small, AXES, split_axis=0, concat_axis=0, tiled=True)
     small = small.transpose(1, 0, 2).reshape(small.shape[1], width)
@@ -499,12 +613,7 @@
     biases = lax.dynamic_slice_in_dim(small[1:4].reshape(3, heads // 2, 2, HEAD), pair, 1, axis=1)
     biases = biases[:, 0].transpose(1, 0, 2).astype(F32)
 
-    token_parts = [
-        gather_bits(value, bits)
-        for value, bits in zip(
-            pieces(deal(tokens, part, high).reshape(rows, width)), low_orders, strict=True
-        )
-    ]
+    token_parts = gather_parts(pieces(dealt_tokens.reshape(rows, width)), low_orders)
 
     by_head = whole_kernel(
         split_heads, [shape_of((total, depth, 3 * HEAD))], q_weight, k_weight, v_weight
@@ -539,8 +648,14 @@
     live_own = (own_positions[None, :] < lengths[:, None]).astype(F32)[:, :, None]
     grad_out = cotangent.astype(F32)
     branch_own = (live_own * grad_out).astype(BF16).reshape(rows, width)
-    branch_own = after(branch_own, *token_parts)
-    branch_all = lax.all_gather(branch_own, CHIPS, axis=0)
+    branch_all = lax.all_gather(after(branch_own, *token_parts), CHIPS, axis=0)
+    chip_number = jnp.arange(chips, dtype=jnp.int32) ^ (me >> 1)
+    chip_places = []
+    for order_of in rotations(()):
+        place_of_chip = np.zeros((chips,), np.int32)
+        place_of_chip[relative(rest_of(high, order_of)) >> 1] = np.arange(chips)
+        chip_places.append(jnp.take(jnp.asarray(place_of_chip), chip_number))
+    branch = to_relative(jnp.concatenate(chip_places), branch_all)
 
     shared_pieces = whole_kernel(
         split_columns, [shape_of((chips, depth, 2 * shared_wide))], shared_gate_up
@@ -555,7 +670,8 @@
     keep_half = lax.dynamic_index_in_dim(expert_halves, x_bit, 0, keepdims=False)
     give_half = lax.dynamic_index_in_dim(expert_halves, 1 - x_bit, 0, keepdims=False)
     give_half = after(give_half, *token_parts)
-    expert_in = jnp.stack([keep_half, swap(give_half, 1)])
+    expert_got = swap(give_half, 1)
+    expert_in = jnp.stack([keep_half, expert_got])
     expert_other = swap(expert_in, 0)
     extra = jnp.concatenate(
         [
@@ -652,19 +768,23 @@
         ]
 
     def reduce_low(parts_in):
-        found = [
-            scatter_bits(value.astype(BF16).reshape(2, 2, 2, -1, width), bits)
-            for value, bits in zip(parts_in, low_orders, strict=True)
-        ]
+        found = [value.astype(BF16).reshape(2, 2, 2, -1, width) for value in parts_in]
+        for step in range(len(LOW)):
+            got = [
+                swap(value[1], bits[-1 - step])
+                for value, bits in zip(found, low_orders, strict=True)
+            ]
+            keeps, got = together([value[0] for value in found], got)
+            found = [add_low(keep, other) for keep, other in zip(keeps, got, strict=True)]
         found = jnp.concatenate(found).reshape(
             (2,) * (1 + len(high)) + (own_seq, piece, width)
         )
         return found
 
     attended_parts = to_parts(attended.astype(BF16)[None])
-    attn_out = undeal(
-        reduce_low([mm(value, o_rows) for value in attended_parts]), part, high
-    )
+    attended_parts[0] = after(attended_parts[0], shared_in, expert_got)
+    attn_out = reduce_low([mm(value, o_rows) for value in attended_parts])
+    attn_out = undeal(attn_out, part, high)
     attn_out = after(attn_out, branch_all)
     inputs = tokens.astype(F32)
     residual = (inputs + live_own * attn_out.astype(F32)).reshape(rows, width)
@@ -673,72 +793,44 @@
 
     expert_column = jnp.arange(experts, dtype=jnp.int32)[None, :]
     one_expert = (expert_column == my_expert).astype(F32)
-    own_rows = rows // PARTS
-    everyone = [
-        lax.all_gather(
-            normed_own[number * own_rows : (number + 1) * own_rows], CHIPS, axis=0, tiled=True
-        )
-        for number in range(PARTS)
-    ]
-    kept = kept.reshape(chips, 2, PARTS, own_rows)
-    kept = lax.dynamic_index_in_dim(kept, core, 1, keepdims=False)
-    masks = [kept[:, number].reshape(-1, 1) for number in range(PARTS)]
-    branch = [
-        branch_all[:, number * own_rows : (number + 1) * own_rows].reshape(-1, width)
-        for number in range(PARTS)
-    ]
+    everyone = Gather(normed_own, high)
+    everyone.value = after(everyone.value, gate_up_weight, down_weight, branch)
+    everyone.split()
+    for _ in LOW:
+        everyone.step()
+    everyone = everyone.whole()
+    masks = []
+    start = 0
+    for count, order_of in zip(SPLITS, rotations(()), strict=True):
+        places = me ^ jnp.asarray(relative(rest_of(high, order_of)), jnp.int32)
+        masks.append(jnp.take(kept[:, start : start + count], places, axis=0).reshape(-1, 1))
+        start += count
 
     sizes = (shared_wide, expert_wide, expert_width - expert_wide + 128, experts)
 
-    def expert_part(number, *others):
-        return expert_pass(
-            sizes,
-            my_expert,
-            number,
-            after(everyone[number], *others),
-            branch_all,
-            masks[number],
-            gate_up_weight,
-            down_weight,
-        )
-
-    def reduce(value):
-        return lax.psum_scatter(value, CHIPS, scatter_dimension=0, tiled=True)
-
-    def weight_grad(number, total_grad, *others):
-        return total_grad + mm_tn(everyone[number], after(joined[number], total_grad, *others))
-
-    def down_grad(number, total_grad, *others):
-        return total_grad + mm_tn(after(hidden[number], total_grad, *others), branch[number])
-
-    hidden = [None] * PARTS
-    joined = [None] * PARTS
-    outs = [None] * PARTS
-    grad_parts = [None] * PARTS
-    before_it = ()
-    for number in range(PARTS):
-        hidden[number], joined[number], outs[number], back_rows = expert_part(number, *before_it)
-        grad_parts[number] = reduce(back_rows)
-        before_it = (joined[number],)
-    grad_gate_up = 0.0
-    grad_down = 0.0
-    for number in range(PARTS):
-        grad_gate_up = weight_grad(number, grad_gate_up, joined[-1], *grad_parts[:-1])
-    for number in range(PARTS):
-        grad_down = down_grad(number, grad_down, grad_gate_up)
+    hidden, joined_grad, out_rows, back_rows = expert_pass(
+        sizes, my_expert, everyone, branch, jnp.concatenate(masks), gate_up_weight, down_weight
+    )
+    grad_sum = Reduction(back_rows, high, chips)
+    out_sum = Reduction(out_rows, high, chips)
+    grad_sum.send()
+    grad_gate_up = mm_tn(everyone, joined_grad).astype(BF16)
+    grad_sum.add()
+    grad_sum.send(grad_gate_up)
+    grad_down = mm_tn(after(hidden, grad_gate_up), branch).astype(BF16)
+    grad_sum.add()
+    grad_sum.send(grad_down)
+    grad_sum.add()
+    grad_parts = [grad_sum.finish()]
     live_rows = jnp.broadcast_to(live_own, (sequences, piece, 1)).reshape(rows, 1)
-    grad_normed = jnp.concatenate(grad_parts).astype(F32)
+    grad_normed = grad_parts[0].astype(F32)
     grad_residual_in, grad_gain_moe = norm_back(grad_normed, normal_two, factor_two, gain_moe)
     grad_residual = grad_out.reshape(rows, width) + grad_residual_in
 
     attn_grad = (live_rows * grad_residual).astype(BF16).reshape(tokens.shape)
-    attn_grad_parts = [
-        gather_bits(value, bits)
-        for value, bits in zip(
-            pieces(deal(attn_grad, part, high).reshape(rows, width)), low_orders, strict=True
-        )
-    ]
-    attn_grad_parts[0] = after(attn_grad_parts[0], grad_down)
+    dealt_grad, grad_arrived = deal(attn_grad, part, high)
+    attn_grad_parts = gather_parts(pieces(dealt_grad.reshape(rows, width)), low_orders)
+    out_sum.send(*attn_grad_parts)
     attended_grads = []
     grad_o = 0.0
     for value, ahead, bits in zip(attn_grad_parts, attended_parts, low_orders, strict=True):
@@ -746,9 +838,6 @@
         back = mm_nt(flat, o_rows).astype(BF16).reshape(value.shape[:-1] + (2 * HEAD,))
         attended_grads.append(to_order(back, bits, wanted))
         grad_o = grad_o + mm_tn(ahead, flat)
-    outs = [after(value, *attn_grad_parts) for value in outs]
-    moe_out = jnp.concatenate([reduce(value) for value in outs]).astype(F32)
-
     def pick(value, axis, number):
         return lax.dynamic_index_in_dim(value, number, axis, keepdims=False)
 
@@ -761,15 +850,14 @@
         vectors = lax.all_to_all(vectors, AXES, split_axis=0, concat_axis=0, tiled=True)
         return jnp.sum(vectors, axis=0)
 
-    tail_grads = grad_gate_up[:, tail_at : tail_at + experts + 1]
-    grad_gate_up = grad_gate_up.astype(BF16)
+    grad_gate_up, grad_down = after((grad_gate_up, grad_down), *grad_arrived)
+    tail_grads = grad_gate_up[:, tail_at : tail_at + experts + 1].astype(F32)
     grad_shared_gu = to_core(
         grad_gate_up[:, : 2 * shared_wide].reshape(chips, 2, depth, 2 * shared_wide), 1
     ).astype(BF16)
     grad_expert_gu = to_core(
         grad_gate_up[:, 2 * shared_wide :].reshape(2, 2, expert_rows, 2 * expert_wide), 1
     ).astype(BF16)
-    grad_down = grad_down.astype(BF16)
     grad_shared_down = to_core(grad_down[:shared_width].reshape(2, -1, width), 0)
     grad_expert_down = to_core(
         grad_down[shared_wide : shared_wide + expert_width].reshape(2, -1, width), 0
@@ -778,6 +866,7 @@
     attended_grad = after(
         jnp.concatenate(attended_grads, axis=-2), grad_shared_gu, grad_expert_gu
     )
+    grad_shared_gu, grad_expert_gu = after((grad_shared_gu, grad_expert_gu), *attn_grad_parts)
     grad_shared_gu = lax.all_to_all(
         grad_shared_gu, CHIPS, split_axis=0, concat_axis=0, tiled=True
     )
@@ -785,10 +874,6 @@
     theirs_gu = swap(pick(grad_expert_gu, 0, 1 - x_bit), 1)
     grad_o = to_core(grad_o.astype(BF16).reshape(uppers, 2, depth, width), 1).astype(BF16)
     grad_o = xor_order(grad_o, upper)
-    grad_o = sum(
-        permute(grad_o[k], [(b, a) for a, b in places]).astype(F32)
-        for k, places in enumerate(o_places)
-    )
     attended_grad = (
         attended_grad.reshape(8, parts, own_seq, piece, 2, HEAD)
         .transpose(2, 4, 0, 1, 3, 5)
@@ -813,7 +898,10 @@
             grad_value.astype(BF16),
         ]
     )
-    grads = after(grads, vectors)
+    out_waits = list(out_sum.got)
+    out_sum.add()
+    grads = after(grads, vectors, *out_waits)
+    out_sum.send()
     bias_grads = jnp.sum(grads.astype(F32), axis=(1, 3))
     grads_parts = to_parts(grads)
     grad_qkv = 0.0
@@ -823,17 +911,42 @@
     low_head = grad_qkv[:, : 3 * HEAD]
     high_head = grad_qkv[:, 3 * HEAD :]
     give_head = jnp.where(core == 0, high_head, low_head)
-    grads_parts[0] = after(grads_parts[0], give_head)
+    out_waits = list(out_sum.got)
+    out_sum.add()
+    given_head = swap(give_head, 0)
+    grads_parts[0] = after(grads_parts[0], given_head, *out_waits)
+    out_sum.send()
     keep_head = jnp.where(core == 0, low_head, high_head)
     grad_qkv = lax.all_to_all(
-        add_low(keep_head, swap(give_head, 0)).reshape(total, depth, 3 * HEAD),
+        add_low(keep_head, given_head).reshape(total, depth, 3 * HEAD),
         AXES,
         split_axis=0,
         concat_axis=0,
         tiled=True,
     )
-    grad_normed_one = reduce_low([mm_nt(value, qkv_weight) for value in grads_parts])
-    grad_normed_one = after(grad_normed_one, grad_shared_gu, theirs_gu, grad_o)
+    normed_sum = [
+        mm_nt(value, qkv_weight).astype(BF16).reshape(2, 2, 2, -1, width) for value in grads_parts
+    ]
+    for step in range(len(LOW)):
+        got = [
+            swap(value[1], order_of[-1 - step])
+            for value, order_of in zip(normed_sum, low_orders, strict=True)
+        ]
+        waits = list(got)
+        if step == 0:
+            waits += [grad_shared_gu, theirs_gu, *out_sum.got]
+            out_sum.add()
+        if step == 1:
+            waits += [grad_qkv]
+        keeps, got = together([value[0] for value in normed_sum], after(tuple(got), *waits[3:]))
+        normed_sum = [add_low(keep, other) for keep, other in zip(keeps, got, strict=True)]
+    moe_out = out_sum.finish().astype(F32)
+    grad_o = after(grad_o, *got)
+    grad_o = sum(
+        permute(grad_o[k], [(b, a) for a, b in places]).astype(F32)
+        for k, places in enumerate(o_places)
+    )
+    grad_normed_one = jnp.concatenate(normed_sum).reshape(dealt_grad.shape)
     grad_normed_one = undeal(grad_normed_one, part, high).astype(F32).reshape(rows, width)
     grad_qkv = whole_kernel(join_heads, [shape_of((depth, width), F32)] * 3, grad_qkv)
     grad_shared_gu = whole_kernel(

time: 1020 us -> 937 us (0.919)
  waiting for transfers between devices: 530 us -> 365 us
  local copies, waits for them, and re-layouts: 81.7 us -> 123 us
  other arithmetic: 77.9 us -> 116 us
    reduce_scatter x2 -> x0, waiting for transfers between devices: 144 us -> none  [reduce(): return lax.psum_scatter(value, CHIPS, scatter_dimension=0, tiled=True)]
    ppermute x62 -> x92, waiting for transfers between devices: 291 us -> 348 us  [permute(): return lax.ppermute(value, AXES, pairs)]
    all_gather x2 -> x1, waiting for transfers between devices: 53.2 us -> 2.35 us  [on_device(): branch_all = lax.all_gather(after(branch_own, *token_parts), CHIPS, axis=0)]
    all_to_all x1, waiting for transfers between devices: 29.2 us -> 0.01 us  [on_device(): lax.all_to_all(add_low(keep_head, given_head).reshape(total, depth, 3 * H...]
    another operation x5 -> x27, other arithmetic: 2.35 us -> 29.6 us  [the longest x15 16.4 us: gather_parts(): jnp.stack(pair)]
    dot_general x8, matrix products: 65.8 us -> 50.5 us  [mm_tn(): lax.dot_general(a, b, (((0,), (0,)), ((), ())), preferred_element_type=F32)]
    slice x8 -> x12, local copies, waits for them, and re-layouts: 7.2 us -> 21.1 us  [the longest x4 14.8 us: __init__(): self.give.append(value[start + half:start + 2 * half].reshape(shape))]
    convert_element_type x19 -> x37, other arithmetic: 8.47 us -> 22.1 us  [add_low(): return (a.astype(F32) + b.astype(F32)).astype(BF16)]
  transfers between devices with their start and end apart: 73 -> 100, of which waited for: 36 -> 52; matrix products, arithmetic and copies ran while one was open for 21% -> 27% of each run, Pallas kernels for 2% -> 3%
where the time goes in v4:
time: 937 us; the launch traced here: 928 us
  waiting for transfers between devices  365 us (39%)
  starting transfers between devices  130 us (14%)
  local copies, waits for them, and re-layouts  123 us (13%)
  other arithmetic  116 us (12%)
  Pallas kernels  104 us (11%)
  matrix products  72 us (8%)
  between operations  17.2 us (2%)
    ppermute x92, waiting for transfers between devices, permute(): return lax.ppermute(value, AXES, pairs)  348 us
    ppermute x92, starting transfers between devices, permute(): return lax.ppermute(value, AXES, pairs)  98.8 us
    pallas_call x1, Pallas kernels, expert_pass(): pl.pallas_call(lambda *refs: expert_kernel(sizes, *refs), grid=(count //...  73 us
    dot_general x8, matrix products, mm_tn(): lax.dot_general(a, b, (((0,), (0,)), ((), ())), preferred_element_type=F32)  50.5 us
    unnamed x338, local copies, waits for them, and re-layouts  39.5 us
    convert_element_type x37, other arithmetic, add_low(): return (a.astype(F32) + b.astype(F32)).astype(BF16)  22.1 us
  transfers between devices with their start and end apart: 100, of which 52 were waited for; matrix products, arithmetic and copies ran while one was open for 27% of the time, Pallas kernels for 3%

profile of v4, /device:TPU:0, one launch (start us, length us, event | category | flops | bytes accessed | tf_op | source)
XLA Modules:
  0.0 928.4 jit_solution(7622263060726793272)
XLA Ops:
  7.2 3.7 collective-permute-start.13
  11.0 2.8 collective-permute-start.14
  44.1 5.4 all-to-all-start
  50.6 6.4 all-to-all-done
  57.0 3.4 all-to-all-start.1
  66.4 11.0 %collective-permute-done.3 = bf16[40,2048]{1,0:T(8,128)(2,1)S(1)} collective-permute-done((bf16[40,2048]{1,0:T(8,128)(2,1)S(1)}, bf16[40,2048]{1,0:T(8,128)(2,1)S(1)}, u32[]{:S(2)}, u32[]{:S(2)}) %collective-permute-start.3) | collective-permute-done | bytes 163872 | tf_op jit(solution)/shard_map/ppermute | solution.py:43
  77.4 13.4 %collective-permute-done.2 = bf16[48,2048]{1,0:T(8,128)(2,1)S(1)} collective-permute-done((bf16[48,2048]{1,0:T(8,128)(2,1)S(1)}, bf16[48,2048]{1,0:T(8,128)(2,1)S(1)}, u32[]{:S(2)}, u32[]{:S(2)}) %collective-permute-start.2) | collective-permute-done | bytes 196640 | tf_op jit(solution)/shard_map/ppermute | solution.py:43
  97.7 5.9 collective-permute-done.7
  109.9 11.0 %collective-permute-done.10 = bf16[2,2,40,2048]{3,2,1,0:T(8,128)(2,1)S(1)} collective-permute-done((bf16[2,2,40,2048]{3,2,1,0:T(8,128)(2,1)S(1)}, bf16[2,2,40,2048]{3,2,1,0:T(8,128)(2,1)S(1)}, u32[]{:S(2)}, u32[]{:S(2)}) %collective-permute-start.10) | collective-permute-done | bytes 655392 | tf_op jit(solution)/shard_map/ppermute | solution.py:43
  120.9 3.1 collective-permute-done.9
  126.8 5.1 all-to-all-start.2
  138.2 3.1 broadcast_select_fusion.2
  141.4 3.2 fusion.22
  159.1 20.6 %collective-permute-done.12 = bf16[512,1536]{1,0:T(8,128)(2,1)} collective-permute-done((bf16[512,1536]{1,0:T(8,128)(2,1)}, bf16[512,1536]{1,0:T(8,128)(2,1)}, u32[]{:S(2)}, u32[]{:S(2)}) %collective-permute-start.12) | collective-permute-done | bytes 1572896 | tf_op jit(solution)/shard_map/ppermute | solution.py:43
  179.7 4.1 all-to-all-done.2.shared_ref
  188.0 22.4 %collective-permute-done.18 = bf16[2,2,40,2048]{3,2,1,0:T(8,128)(2,1)} collective-permute-done((bf16[2,2,40,2048]{3,2,1,0:T(8,128)(2,1)}, bf16[2,2,40,2048]{3,2,1,0:T(8,128)(2,1)}, u32[]{:S(2)}, u32[]{:S(2)}) %collective-permute-start.18) | collective-permute-done | bytes 655392 | tf_op jit(solution)/shard_map/ppermute | solution.py:43
  210.4 3.5 collective-permute-done.17
  220.1 9.2 collective-permute-done.21
  240.1 12.6 %collective-permute-done.22 = bf16[48,2048]{1,0:T(8,128)(2,1)S(1)} collective-permute-done((bf16[48,2048]{1,0:T(8,128)(2,1)S(1)}, bf16[48,2048]{1,0:T(8,128)(2,1)S(1)}, u32[]{:S(2)}, u32[]{:S(2)}) %collective-permute-start.22) | collective-permute-done | bytes 196640 | tf_op jit(solution)/shard_map/ppermute | solution.py:43
  265.2 25.1 %collective-permute-done.26 = bf16[2,4,8,2048]{3,2,1,0:T(8,128)(2,1)} collective-permute-done((bf16[2,4,8,2048]{3,2,1,0:T(8,128)(2,1)}, bf16[2,4,8,2048]{3,2,1,0:T(8,128)(2,1)}, u32[]{:S(2)}, u32[]{:S(2)}) %collective-permute-start.26) | collective-permute-done | bytes 262176 | tf_op jit(solution)/shard_map/ppermute | solution.py:43
  304.8 9.8 %shard_map.389.refs_4_ = bf16[2048,2304]{1,0:T(8,128)(2,1)} custom-call(s32[2]{0:T(128)S(1)} %pad_add_fusion.flags_ref, bf16[16,64,768]{2,1,0:T(8,128)(2,1)S(1)} %copy-done.4, bf16[16,64,768]{2,1,0:T(8,128)(2,1)} %collective-permute-done.28.shared_other, bf16[2,512,1536]{2,1,0:T(8,128)(2,1)S(1)} %pad_maximum_fusion.2.expert_ref, ...), custom_call_target="tpu_custom_call" | custom-call | bytes 28311552 | tf_op jit(solution)/shard_map/pallas_call | solution.py:335
  314.6 8.2 shard_map.391.refs_2_
  329.6 5.9 collective-permute-done.33
  349.0 5.2 collective-permute-done.37
  354.2 3.7 collective-permute-done.36
  372.6 16.1 %collective-permute-done.40 = bf16[2,2,2,40,2048]{4,3,2,1,0:T(8,128)(2,1)} collective-permute-done((bf16[2,2,2,40,2048]{4,3,2,1,0:T(8,128)(2,1)}, bf16[2,2,2,40,2048]{4,3,2,1,0:T(8,128)(2,1)}, u32[]{:S(2)}, u32[]{:S(2)}) %collective-permute-start.40) | collective-permute-done | bytes 1310752 | tf_op jit(solution)/shard_map/ppermute | solution.py:43
  388.7 6.0 collective-permute-done.39
  410.9 73.0 %shard_map.392 = (bf16[2048,1152]{1,0:T(8,128)(2,1)}, bf16[2048,2304]{1,0:T(8,128)(2,1)}, bf16[2048,2048]{1,0:T(8,128)(2,1)}, bf16[2048,2048]{1,0:T(8,128)(2,1)}) custom-call(s32[1]{0:T(128)} %bitcast.91.refs_0_, bf16[2048,2048]{1,0:T(8,128)(2,1)} %constant_dynamic-update-slice_fusion.refs_1_, bf16[2048,2048]{1,0:T(8,128)(2,1)} %shard_map.391.refs_2_, ...), custom_call_target="tpu_custom_call" | custom-call | flops 4831838208 | bytes 33554432 | tf_op jit(solution)/shard_map/pallas_call | solution.py:478
  483.9 3.1 fusion.100
  493.8 25.1 %convolution_convert_fusion = bf16[2048,2304]{1,0:T(8,128)(2,1)} fusion(bf16[2048,2048]{1,0:T(8,128)(2,1)} %constant_dynamic-update-slice_fusion.refs_1_, bf16[2048,2304]{1,0:T(8,128)(2,1)S(1)} %copy-done.152), kind=kOutput, calls=%fused_computation.8 | convolution fusion | flops 19332071424 | bytes 27262976 | tf_op jit(solution)/shard_map/dot_general | solution.py:31
  518.9 5.2 collective-permute-done.41
  529.2 13.5 %convolution_convert_fusion.1 = bf16[1152,2048]{1,0:T(8,128)(2,1)} fusion(bf16[2048,1152]{1,0:T(8,128)(2,1)} %get-tuple-element.266, bf16[2048,2048]{1,0:T(8,128)(2,1)S(1)} %bitcast.551), kind=kOutput, calls=%fused_computation.9 | convolution fusion | flops 9666035712 | bytes 17825792 | tf_op jit(solution)/shard_map/dot_general | solution.py:31
  546.7 5.6 collective-permute-done.48
  554.5 3.4 collective-permute-start.50
  558.7 14.1 %collective-permute-done.50 = bf16[128,2048]{1,0:T(8,128)(2,1)S(1)} collective-permute-done((bf16[128,2048]{1,0:T(8,128)(2,1)}, bf16[128,2048]{1,0:T(8,128)(2,1)S(1)}, u32[]{:S(2)}, u32[]{:S(2)}) %collective-permute-start.50) | collective-permute-done | bytes 524320 | tf_op jit(solution)/shard_map/ppermute | solution.py:43
  574.3 5.2 fusion.102
  579.5 5.8 collective-permute-done.51
  585.4 4.0 fusion.103
  590.9 3.2 slice.560
  594.2 3.0 slice_convert_fusion.1
  610.8 4.1 all-to-all-start.3
  646.9 6.7 collective-permute-done.61
  655.8 5.1 collective-permute-done.59
  676.1 3.5 fusion.12
  682.2 19.6 %collective-permute-done.63 = bf16[2,2,2,40,2048]{4,3,2,1,0:T(8,128)(2,1)S(1)} collective-permute-done((bf16[2,2,2,40,2048]{4,3,2,1,0:T(8,128)(2,1)S(1)}, bf16[2,2,2,40,2048]{4,3,2,1,0:T(8,128)(2,1)S(1)}, u32[]{:S(2)}, u32[]{:S(2)}) %collective-permute-start.63) | collective-permute-done | bytes 1310752 | tf_op jit(solution)/shard_map/ppermute | solution.py:43
  701.8 3.4 collective-permute-done.64
  726.6 3.2 fusion.35
  740.1 5.3 all-to-all-start.4
  745.4 4.5 convolution_convert_fusion.4
  769.1 4.2 collective-permute-done.70
  774.6 21.2 %collective-permute-done.69 = bf16[2,40,2048]{2,1,0:T(8,128)(2,1)S(1)} collective-permute-done((bf16[2,40,2048]{2,1,0:T(8,128)(2,1)S(1)}, bf16[2,40,2048]{2,1,0:T(8,128)(2,1)S(1)}, u32[]{:S(2)}, u32[]{:S(2)}) %collective-permute-start.69) | collective-permute-done | bytes 327712 | tf_op jit(solution)/shard_map/ppermute | solution.py:43
  801.3 3.2 add_convert_fusion
  804.5 4.1 all-to-all-start.5
  809.0 18.9 %collective-permute-done.75 = bf16[2,2,48,2048]{3,2,1,0:T(8,128)(2,1)} collective-permute-done((bf16[2,2,48,2048]{3,2,1,0:T(8,128)(2,1)}, bf16[2,2,48,2048]{3,2,1,0:T(8,128)(2,1)}, u32[]{:S(2)}, u32[]{:S(2)}) %collective-permute-start.75) | collective-permute-done | bytes 786464 | tf_op jit(solution)/shard_map/ppermute | solution.py:43
  838.0 4.0 collective-permute-done.81
  843.5 3.3 collective-permute-done.79
  854.7 3.1 collective-permute-done.82
  858.5 3.3 collective-permute-start.89
  863.9 4.7 shard_map.395
  873.8 18.5 %collective-permute-done.89 = bf16[64,2048]{1,0:T(8,128)(2,1)S(1)} collective-permute-done((bf16[64,2048]{1,0:T(8,128)(2,1)S(1)}, bf16[64,2048]{1,0:T(8,128)(2,1)S(1)}, u32[]{:S(2)}, u32[]{:S(2)}) %collective-permute-start.89) | collective-permute-done | bytes 262176 | tf_op jit(solution)/shard_map/ppermute | solution.py:43
  893.2 13.1 %collective-permute-done.86 = bf16[2,4,8,2048]{3,2,1,0:T(8,128)(2,1)S(1)} collective-permute-done((bf16[2,4,8,2048]{3,2,1,0:T(8,128)(2,1)S(1)}, bf16[2,4,8,2048]{3,2,1,0:T(8,128)(2,1)S(1)}, u32[]{:S(2)}, u32[]{:S(2)}) %collective-permute-start.86) | collective-permute-done | bytes 262176 | tf_op jit(solution)/shard_map/ppermute | solution.py:43
  908.6 4.0 all-to-all-start.6
  912.8 3.1 fusion.52
  915.9 3.9 all-to-all-done.6
  (816 shorter events, 348.9 us)
Async XLA Ops:
  7.2 54.9 %collective-permute-start.13 = (bf16[64,2048]{1,0:T(8,128)(2,1)}, bf16[64,2048]{1,0:T(8,128)(2,1)}, u32[]{:S(2)}, u32[]{:S(2)}) collective-permute-start(bf16[64,2048]{1,0:T(8,128)(2,1)} %param.43), channel_id=1, source_target_pairs={{0,0},{1,1},{2,16},{3,17},{4,2},{5,3},{6,18},{7,19},{8,4},{9,5},{1... | collective-permute-start | bytes 786440 | tf_op jit(solution)/shard_map/ppermute | solution.py:43
  11.0 52.6 %collective-permute-start.14 = (bf16[64,2048]{1,0:T(8,128)(2,1)}, bf16[64,2048]{1,0:T(8,128)(2,1)}, u32[]{:S(2)}, u32[]{:S(2)}) collective-permute-start(bf16[64,2048]{1,0:T(8,128)(2,1)} %param.43), channel_id=1, source_target_pairs={{0,16},{1,17},{2,0},{3,1},{4,18},{5,19},{6,2},{7,3},{8,20},{9,21},... | collective-permute-start | bytes 786440 | tf_op jit(solution)/shard_map/ppermute | solution.py:43
  16.4 24.0 %collective-permute-start = (bf16[2,4,8,2048]{3,2,1,0:T(8,128)(2,1)}, bf16[2,4,8,2048]{3,2,1,0:T(8,128)(2,1)}, u32[]{:S(2)}, u32[]{:S(2)}) collective-permute-start(bf16[2,4,8,2048]{3,2,1,0:T(8,128)(2,1)} %pad_maximum_fusion.48), channel_id=1, source_target_pairs={{0,16},{1,17},{2,18},{3,19},{4,20},{5,21},{6,22},{7,23},{8,24},{9,... | collective-permute-start | bytes 786440 | tf_op jit(solution)/shard_map/ppermute | solution.py:43
  18.8 281.0 %collective-permute-start.31 = (bf16[352,2048]{1,0:T(8,128)(2,1)}, bf16[352,2048]{1,0:T(8,128)(2,1)}, u32[]{:S(2)}, u32[]{:S(2)}) collective-permute-start(bf16[352,2048]{1,0:T(8,128)(2,1)} %bitcast.99.expert_ref), channel_id=1, source_target_pairs={{0,1},{1,0},{2,3},{3,2},{4,5},{5,4},{6,7},{7,6},{8,9},{9,8},{10,11... | collective-permute-start | bytes 4325384 | tf_op jit(solution)/shard_map/ppermute | solution.py:43
  18.8 281.0 %collective-permute-start.30 = (bf16[176,2048]{1,0:T(8,128)(2,1)}, bf16[176,2048]{1,0:T(8,128)(2,1)}, u32[]{:S(2)}, u32[]{:S(2)}) collective-permute-start(bf16[176,2048]{1,0:T(8,128)(2,1)} %shared_ref.1), channel_id=1, source_target_pairs={{0,1},{1,0},{2,3},{3,2},{4,5},{5,4},{6,7},{7,6},{8,9},{9,8},{10,11... | collective-permute-start | bytes 2162696 | tf_op jit(solution)/shard_map/ppermute | solution.py:43
  57.0 68.8 %all-to-all-start.1 = ((bf16[32,64,384]{2,1,0:T(8,128)(2,1)}), bf16[32,64,384]{2,1,0:T(8,128)(2,1)}, u32[]{:S(2)}, u32[]{:S(2)}) async-start(bf16[32,64,384]{2,1,0:T(8,128)(2,1)} %copy-done.1), calls=%async_computation.1 | async-start | bytes 3145728 | tf_op jit(solution)/shard_map/all_to_all | solution.py:621
  60.5 16.9 %collective-permute-start.3 = (bf16[40,2048]{1,0:T(8,128)(2,1)S(1)}, bf16[40,2048]{1,0:T(8,128)(2,1)S(1)}, u32[]{:S(2)}, u32[]{:S(2)}) collective-permute-start(bf16[40,2048]{1,0:T(8,128)(2,1)S(1)} %get-tuple-element.188), channel_id=1, source_target_pairs={{0,2},{1,3},{2,0},{3,1},{4,6},{5,7},{6,4},{7,5},{8,10},{9,11},{10,... | collective-permute-start | bytes 491528 | tf_op jit(solution)/shard_map/ppermute | solution.py:43
  62.1 15.3 %collective-permute-start.4 = (bf16[40,2048]{1,0:T(8,128)(2,1)S(1)}, bf16[40,2048]{1,0:T(8,128)(2,1)S(1)}, u32[]{:S(2)}, u32[]{:S(2)}) collective-permute-start(bf16[40,2048]{1,0:T(8,128)(2,1)S(1)} %get-tuple-element.190), channel_id=1, source_target_pairs={{0,4},{1,5},{2,6},{3,7},{4,0},{5,1},{6,2},{7,3},{8,12},{9,13},{10,... | collective-permute-start | bytes 491528 | tf_op jit(solution)/shard_map/ppermute | solution.py:43
  63.6 27.2 %collective-permute-start.2 = (bf16[48,2048]{1,0:T(8,128)(2,1)S(1)}, bf16[48,2048]{1,0:T(8,128)(2,1)S(1)}, u32[]{:S(2)}, u32[]{:S(2)}) collective-permute-start(bf16[48,2048]{1,0:T(8,128)(2,1)S(1)} %slice.624), channel_id=1, source_target_pairs={{0,8},{1,9},{2,10},{3,11},{4,12},{5,13},{6,14},{7,15},{8,0},{9,1},... | collective-permute-start | bytes 589832 | tf_op jit(solution)/shard_map/ppermute | solution.py:43
  105.3 15.7 %collective-permute-start.10 = (bf16[2,2,40,2048]{3,2,1,0:T(8,128)(2,1)S(1)}, bf16[2,2,40,2048]{3,2,1,0:T(8,128)(2,1)S(1)}, u32[]{:S(2)}, u32[]{:S(2)}) collective-permute-start(bf16[2,2,40,2048]{3,2,1,0:T(8,128)(2,1)S(1)} %pad_maximum_fusion.21), channel_id=1, source_target_pairs={{0,2},{1,3},{2,0},{3,1},{4,6},{5,7},{6,4},{7,5},{8,10},{9,11},{10,... | collective-permute-start | bytes 1966088 | tf_op jit(solution)/shard_map/ppermute | solution.py:43
  107.9 17.9 %collective-permute-start.8 = (bf16[2,2,48,2048]{3,2,1,0:T(8,128)(2,1)S(1)}, bf16[2,2,48,2048]{3,2,1,0:T(8,128)(2,1)}, u32[]{:S(2)}, u32[]{:S(2)}) collective-permute-start(bf16[2,2,48,2048]{3,2,1,0:T(8,128)(2,1)S(1)} %pad_maximum_fusion.17), channel_id=1, source_target_pairs={{0,4},{1,5},{2,6},{3,7},{4,0},{5,1},{6,2},{7,3},{8,12},{9,13},{10,... | collective-permute-start | bytes 2359304 | tf_op jit(solution)/shard_map/ppermute | solution.py:43
  108.6 15.5 %collective-permute-start.9 = (bf16[2,2,40,2048]{3,2,1,0:T(8,128)(2,1)S(1)}, bf16[2,2,40,2048]{3,2,1,0:T(8,128)(2,1)S(1)}, u32[]{:S(2)}, u32[]{:S(2)}) collective-permute-start(bf16[2,2,40,2048]{3,2,1,0:T(8,128)(2,1)S(1)} %pad_maximum_fusion.20), channel_id=1, source_target_pairs={{0,8},{1,9},{2,10},{3,11},{4,12},{5,13},{6,14},{7,15},{8,0},{9,1},... | collective-permute-start | bytes 1966088 | tf_op jit(solution)/shard_map/ppermute | solution.py:43
  125.8 53.9 %collective-permute-start.12 = (bf16[512,1536]{1,0:T(8,128)(2,1)}, bf16[512,1536]{1,0:T(8,128)(2,1)}, u32[]{:S(2)}, u32[]{:S(2)}) collective-permute-start(bf16[512,1536]{1,0:T(8,128)(2,1)} %get-tuple-element.206), channel_id=1, source_target_pairs={{0,2},{1,3},{2,0},{3,1},{4,6},{5,7},{6,4},{7,5},{8,10},{9,11},{10,... | collective-permute-start | bytes 4718600 | tf_op jit(solution)/shard_map/ppermute | solution.py:43
  126.8 57.0 %all-to-all-start.2 = ((bf16[16,64,768]{2,1,0:T(8,128)(2,1)}), bf16[16,64,768]{2,1,0:T(8,128)(2,1)S(1)}, u32[]{:S(2)}, u32[]{:S(2)}) async-start(bf16[16,64,768]{2,1,0:T(8,128)(2,1)} %shard_map.387), calls=%async_computation.2 | async-start | bytes 3145728 | tf_op jit(solution)/shard_map/all_to_all | solution.py:664
  131.9 162.7 %all-gather.3.cloned.1.call-start = ((), (), s32[]{:S(2)}) async-start(), calls=%async_computation.7 | async-start | bytes 8912896 | tf_op jit(solution)/shard_map/all_gather | solution.py:651
  155.6 54.8 %collective-permute-start.18 = (bf16[2,2,40,2048]{3,2,1,0:T(8,128)(2,1)}, bf16[2,2,40,2048]{3,2,1,0:T(8,128)(2,1)}, u32[]{:S(2)}, u32[]{:S(2)}) collective-permute-start(bf16[2,2,40,2048]{3,2,1,0:T(8,128)(2,1)} %bitcast.67), channel_id=1, source_target_pairs={{0,2},{1,3},{2,0},{3,1},{4,6},{5,7},{6,4},{7,5},{8,10},{9,11},{10,... | collective-permute-start | bytes 1966088 | tf_op jit(solution)/shard_map/ppermute | solution.py:43
  184.9 29.0 %collective-permute-start.16 = (bf16[2,2,48,2048]{3,2,1,0:T(8,128)(2,1)S(1)}, bf16[2,2,48,2048]{3,2,1,0:T(8,128)(2,1)S(1)}, u32[]{:S(2)}, u32[]{:S(2)}) collective-permute-start(bf16[2,2,48,2048]{3,2,1,0:T(8,128)(2,1)S(1)} %bitcast.662), channel_id=1, source_target_pairs={{0,4},{1,5},{2,6},{3,7},{4,0},{5,1},{6,2},{7,3},{8,12},{9,13},{10,... | collective-permute-start | bytes 2359304 | tf_op jit(solution)/shard_map/ppermute | solution.py:43
  186.5 27.4 %collective-permute-start.17 = (bf16[2,2,40,2048]{3,2,1,0:T(8,128)(2,1)S(1)}, bf16[2,2,40,2048]{3,2,1,0:T(8,128)(2,1)S(1)}, u32[]{:S(2)}, u32[]{:S(2)}) collective-permute-start(bf16[2,2,40,2048]{3,2,1,0:T(8,128)(2,1)S(1)} %bitcast.665), channel_id=1, source_target_pairs={{0,8},{1,9},{2,10},{3,11},{4,12},{5,13},{6,14},{7,15},{8,0},{9,1},... | collective-permute-start | bytes 1966088 | tf_op jit(solution)/shard_map/ppermute | solution.py:43
  231.9 20.8 %collective-permute-start.22 = (bf16[48,2048]{1,0:T(8,128)(2,1)S(1)}, bf16[48,2048]{1,0:T(8,128)(2,1)S(1)}, u32[]{:S(2)}, u32[]{:S(2)}) collective-permute-start(bf16[48,2048]{1,0:T(8,128)(2,1)S(1)} %get-tuple-element.543), channel_id=1, source_target_pairs={{0,8},{1,9},{2,10},{3,11},{4,12},{5,13},{6,14},{7,15},{8,0},{9,1},... | collective-permute-start | bytes 589832 | tf_op jit(solution)/shard_map/ppermute | solution.py:43
  237.7 67.1 %collective-permute-start.29 = (bf16[2,512,1536]{2,1,0:T(8,128)(2,1)S(1)}, bf16[2,512,1536]{2,1,0:T(8,128)(2,1)}, u32[]{:S(2)}, u32[]{:S(2)}) collective-permute-start(bf16[2,512,1536]{2,1,0:T(8,128)(2,1)S(1)} %pad_maximum_fusion.2.expert_ref), channel_id=1, source_target_pairs={{0,1},{1,0},{2,3},{3,2},{4,5},{5,4},{6,7},{7,6},{8,9},{9,8},{10,11... | collective-permute-start | bytes 9437192 | tf_op jit(solution)/shard_map/ppermute | solution.py:43
  258.0 32.3 %collective-permute-start.26 = (bf16[2,4,8,2048]{3,2,1,0:T(8,128)(2,1)}, bf16[2,4,8,2048]{3,2,1,0:T(8,128)(2,1)}, u32[]{:S(2)}, u32[]{:S(2)}) collective-permute-start(bf16[2,4,8,2048]{3,2,1,0:T(8,128)(2,1)} %get-tuple-element.528), channel_id=1, source_target_pairs={{0,16},{1,17},{2,18},{3,19},{4,20},{5,21},{6,22},{7,23},{8,24},{9,... | collective-permute-start | bytes 786440 | tf_op jit(solution)/shard_map/ppermute | solution.py:43
  265.0 39.7 %collective-permute-start.28 = (bf16[16,64,768]{2,1,0:T(8,128)(2,1)}, bf16[16,64,768]{2,1,0:T(8,128)(2,1)}, u32[]{:S(2)}, u32[]{:S(2)}) collective-permute-start(bf16[16,64,768]{2,1,0:T(8,128)(2,1)} %copy-done.3), channel_id=1, source_target_pairs={{0,1},{1,0},{2,3},{3,2},{4,5},{5,4},{6,7},{7,6},{8,9},{9,8},{10,11... | collective-permute-start | bytes 4718600 | tf_op jit(solution)/shard_map/ppermute | solution.py:43
  299.3 25.1 %collective-permute-start.27 = (bf16[128,2048]{1,0:T(8,128)(2,1)}, bf16[128,2048]{1,0:T(8,128)(2,1)}, u32[]{:S(2)}, u32[]{:S(2)}) collective-permute-start(bf16[128,2048]{1,0:T(8,128)(2,1)} %multiply_convert_fusion.2), channel_id=1, source_target_pairs={{0,16},{1,17},{2,18},{3,19},{4,20},{5,21},{6,22},{7,23},{8,24},{9,... | collective-permute-start | bytes 1572872 | tf_op jit(solution)/shard_map/ppermute | solution.py:43
  338.8 15.4 %collective-permute-start.37 = (bf16[2,2,40,2048]{3,2,1,0:T(8,128)(2,1)S(1)}, bf16[2,2,40,2048]{3,2,1,0:T(8,128)(2,1)}, u32[]{:S(2)}, u32[]{:S(2)}) collective-permute-start(bf16[2,2,40,2048]{3,2,1,0:T(8,128)(2,1)S(1)} %pad_maximum_fusion.23), channel_id=1, source_target_pairs={{0,8},{1,9},{2,10},{3,11},{4,12},{5,13},{6,14},{7,15},{8,0},{9,1},... | collective-permute-start | bytes 1966088 | tf_op jit(solution)/shard_map/ppermute | solution.py:43
  340.5 17.7 %collective-permute-start.35 = (bf16[2,2,48,2048]{3,2,1,0:T(8,128)(2,1)S(1)}, bf16[2,2,48,2048]{3,2,1,0:T(8,128)(2,1)}, u32[]{:S(2)}, u32[]{:S(2)}) collective-permute-start(bf16[2,2,48,2048]{3,2,1,0:T(8,128)(2,1)S(1)} %pad_maximum_fusion.18), channel_id=1, source_target_pairs={{0,2},{1,3},{2,0},{3,1},{4,6},{5,7},{6,4},{7,5},{8,10},{9,11},{10,... | collective-permute-start | bytes 2359304 | tf_op jit(solution)/shard_map/ppermute | solution.py:43
  360.5 28.2 %collective-permute-start.40 = (bf16[2,2,2,40,2048]{4,3,2,1,0:T(8,128)(2,1)}, bf16[2,2,2,40,2048]{4,3,2,1,0:T(8,128)(2,1)}, u32[]{:S(2)}, u32[]{:S(2)}) collective-permute-start(bf16[2,2,2,40,2048]{4,3,2,1,0:T(8,128)(2,1)} %pad_maximum_fusion.10), channel_id=1, source_target_pairs={{0,2},{1,3},{2,0},{3,1},{4,6},{5,7},{6,4},{7,5},{8,10},{9,11},{10,... | collective-permute-start | bytes 3932168 | tf_op jit(solution)/shard_map/ppermute | solution.py:43
  363.5 33.3 %collective-permute-start.38 = (bf16[2,2,2,48,2048]{4,3,2,1,0:T(8,128)(2,1)S(1)}, bf16[2,2,2,48,2048]{4,3,2,1,0:T(8,128)(2,1)}, u32[]{:S(2)}, u32[]{:S(2)}) collective-permute-start(bf16[2,2,2,48,2048]{4,3,2,1,0:T(8,128)(2,1)S(1)} %pad_maximum_fusion.4), channel_id=1, source_target_pairs={{0,4},{1,5},{2,6},{3,7},{4,0},{5,1},{6,2},{7,3},{8,12},{9,13},{10,... | collective-permute-start | bytes 4718600 | tf_op jit(solution)/shard_map/ppermute | solution.py:43
  367.0 27.7 %collective-permute-start.39 = (bf16[2,2,2,40,2048]{4,3,2,1,0:T(8,128)(2,1)}, bf16[2,2,2,40,2048]{4,3,2,1,0:T(8,128)(2,1)}, u32[]{:S(2)}, u32[]{:S(2)}) collective-permute-start(bf16[2,2,2,40,2048]{4,3,2,1,0:T(8,128)(2,1)} %pad_maximum_fusion.9), channel_id=1, source_target_pairs={{0,8},{1,9},{2,10},{3,11},{4,12},{5,13},{6,14},{7,15},{8,0},{9,1},... | collective-permute-start | bytes 3932168 | tf_op jit(solution)/shard_map/ppermute | solution.py:43
  489.6 29.2 %collective-permute-start.42 = (bf16[2,2,2,40,2048]{4,3,2,1,0:T(8,128)(2,1)S(1)}, bf16[2,2,2,40,2048]{4,3,2,1,0:T(8,128)(2,1)S(1)}, u32[]{:S(2)}, u32[]{:S(2)}) collective-permute-start(bf16[2,2,2,40,2048]{4,3,2,1,0:T(8,128)(2,1)S(1)} %bitcast.650), channel_id=1, source_target_pairs={{0,8},{1,9},{2,10},{3,11},{4,12},{5,13},{6,14},{7,15},{8,0},{9,1},... | collective-permute-start | bytes 3932168 | tf_op jit(solution)/shard_map/ppermute | solution.py:43
  491.6 27.2 %collective-permute-start.43 = (bf16[2,2,2,40,2048]{4,3,2,1,0:T(8,128)(2,1)S(1)}, bf16[2,2,2,40,2048]{4,3,2,1,0:T(8,128)(2,1)S(1)}, u32[]{:S(2)}, u32[]{:S(2)}) collective-permute-start(bf16[2,2,2,40,2048]{4,3,2,1,0:T(8,128)(2,1)S(1)} %bitcast.649), channel_id=1, source_target_pairs={{0,2},{1,3},{2,0},{3,1},{4,6},{5,7},{6,4},{7,5},{8,10},{9,11},{10,... | collective-permute-start | bytes 3932168 | tf_op jit(solution)/shard_map/ppermute | solution.py:43
  492.2 32.0 %collective-permute-start.41 = (bf16[2,2,2,48,2048]{4,3,2,1,0:T(8,128)(2,1)S(1)}, bf16[2,2,2,48,2048]{4,3,2,1,0:T(8,128)(2,1)S(1)}, u32[]{:S(2)}, u32[]{:S(2)}) collective-permute-start(bf16[2,2,2,48,2048]{4,3,2,1,0:T(8,128)(2,1)S(1)} %bitcast.646), channel_id=1, source_target_pairs={{0,4},{1,5},{2,6},{3,7},{4,0},{5,1},{6,2},{7,3},{8,12},{9,13},{10,... | collective-permute-start | bytes 4718600 | tf_op jit(solution)/shard_map/ppermute | solution.py:43
  526.1 16.5 %collective-permute-start.44 = (bf16[2,2,48,2048]{3,2,1,0:T(8,128)(2,1)S(1)}, bf16[2,2,48,2048]{3,2,1,0:T(8,128)(2,1)S(1)}, u32[]{:S(2)}, u32[]{:S(2)}) collective-permute-start(bf16[2,2,48,2048]{3,2,1,0:T(8,128)(2,1)S(1)} %get-tuple-element.256), channel_id=1, source_target_pairs={{0,2},{1,3},{2,0},{3,1},{4,6},{5,7},{6,4},{7,5},{8,10},{9,11},{10,... | collective-permute-start | bytes 2359304 | tf_op jit(solution)/shard_map/ppermute | solution.py:43
  527.8 14.8 %collective-permute-start.45 = (bf16[2,2,40,2048]{3,2,1,0:T(8,128)(2,1)S(1)}, bf16[2,2,40,2048]{3,2,1,0:T(8,128)(2,1)S(1)}, u32[]{:S(2)}, u32[]{:S(2)}) collective-permute-start(bf16[2,2,40,2048]{3,2,1,0:T(8,128)(2,1)S(1)} %get-tuple-element.257), channel_id=1, source_target_pairs={{0,4},{1,5},{2,6},{3,7},{4,0},{5,1},{6,2},{7,3},{8,12},{9,13},{10,... | collective-permute-start | bytes 1966088 | tf_op jit(solution)/shard_map/ppermute | solution.py:43
  554.5 18.3 %collective-permute-start.50 = (bf16[128,2048]{1,0:T(8,128)(2,1)}, bf16[128,2048]{1,0:T(8,128)(2,1)S(1)}, u32[]{:S(2)}, u32[]{:S(2)}) collective-permute-start(bf16[128,2048]{1,0:T(8,128)(2,1)} %slice_bitcast_fusion.14), channel_id=1, source_target_pairs={{0,16},{1,17},{2,18},{3,19},{4,20},{5,21},{6,22},{7,23},{8,24},{9,... | collective-permute-start | bytes 1572872 | tf_op jit(solution)/shard_map/ppermute | solution.py:43
  597.5 17.4 %collective-permute-start.54 = (bf16[40,2048]{1,0:T(8,128)(2,1)}, bf16[40,2048]{1,0:T(8,128)(2,1)}, u32[]{:S(2)}, u32[]{:S(2)}) collective-permute-start(bf16[40,2048]{1,0:T(8,128)(2,1)} %get-tuple-element.278), channel_id=1, source_target_pairs={{0,2},{1,3},{2,0},{3,1},{4,6},{5,7},{6,4},{7,5},{8,10},{9,11},{10,... | collective-permute-start | bytes 491528 | tf_op jit(solution)/shard_map/ppermute | solution.py:43
  598.2 16.7 %collective-permute-start.55 = (bf16[40,2048]{1,0:T(8,128)(2,1)}, bf16[40,2048]{1,0:T(8,128)(2,1)}, u32[]{:S(2)}, u32[]{:S(2)}) collective-permute-start(bf16[40,2048]{1,0:T(8,128)(2,1)} %get-tuple-element.280), channel_id=1, source_target_pairs={{0,4},{1,5},{2,6},{3,7},{4,0},{5,1},{6,2},{7,3},{8,12},{9,13},{10,... | collective-permute-start | bytes 491528 | tf_op jit(solution)/shard_map/ppermute | solution.py:43
  600.1 14.8 %collective-permute-start.53 = (bf16[48,2048]{1,0:T(8,128)(2,1)}, bf16[48,2048]{1,0:T(8,128)(2,1)}, u32[]{:S(2)}, u32[]{:S(2)}) collective-permute-start(bf16[48,2048]{1,0:T(8,128)(2,1)} %slice.681), channel_id=1, source_target_pairs={{0,8},{1,9},{2,10},{3,11},{4,12},{5,13},{6,14},{7,15},{8,0},{9,1},... | collective-permute-start | bytes 589832 | tf_op jit(solution)/shard_map/ppermute | solution.py:43
  606.7 67.8 %collective-permute-start.91 = (bf16[352,2048]{1,0:T(8,128)(2,1)}, bf16[352,2048]{1,0:T(8,128)(2,1)}, u32[]{:S(2)}, u32[]{:S(2)}) collective-permute-start(bf16[352,2048]{1,0:T(8,128)(2,1)} %dynamic-slice_bitcast_fusion.5), channel_id=1, source_target_pairs={{0,1},{1,0},{2,3},{3,2},{4,5},{5,4},{6,7},{7,6},{8,9},{9,8},{10,11... | collective-permute-start | bytes 4325384 | tf_op jit(solution)/shard_map/ppermute | solution.py:43
  610.8 15.7 %all-to-all-start.3 = ((f32[32,1,640]{2,1,0:T(1,128)}), f32[32,1,640]{2,1,0:T(1,128)}, u32[]{:S(2)}, u32[]{:S(2)}) async-start(f32[32,1,640]{2,1,0:T(1,128)} %reshape.974), calls=%async_computation.3 | async-start | bytes 163840 | tf_op jit(solution)/shard_map/all_to_all | solution.py:850
  616.8 17.4 %collective-permute-start.58 = (bf16[2,40,2048]{2,1,0:T(8,128)(2,1)}, bf16[2,40,2048]{2,1,0:T(8,128)(2,1)}, u32[]{:S(2)}, u32[]{:S(2)}) collective-permute-start(bf16[2,40,2048]{2,1,0:T(8,128)(2,1)} %pad_maximum_fusion.39), channel_id=1, source_target_pairs={{0,8},{1,9},{2,10},{3,11},{4,12},{5,13},{6,14},{7,15},{8,0},{9,1},... | collective-permute-start | bytes 983048 | tf_op jit(solution)/shard_map/ppermute | solution.py:43
  625.2 19.1 %collective-permute-start.90 = (bf16[176,2048]{1,0:T(8,128)(2,1)}, bf16[176,2048]{1,0:T(8,128)(2,1)}, u32[]{:S(2)}, u32[]{:S(2)}) collective-permute-start(bf16[176,2048]{1,0:T(8,128)(2,1)} %dynamic-slice_bitcast_fusion.6), channel_id=1, source_target_pairs={{0,1},{1,0},{2,3},{3,2},{4,5},{5,4},{6,7},{7,6},{8,9},{9,8},{10,11... | collective-permute-start | bytes 2162696 | tf_op jit(solution)/shard_map/ppermute | solution.py:43
  636.1 17.5 %collective-permute-start.61 = (bf16[2,2,40,2048]{3,2,1,0:T(8,128)(2,1)}, bf16[2,2,40,2048]{3,2,1,0:T(8,128)(2,1)}, u32[]{:S(2)}, u32[]{:S(2)}) collective-permute-start(bf16[2,2,40,2048]{3,2,1,0:T(8,128)(2,1)} %pad_maximum_fusion.25), channel_id=1, source_target_pairs={{0,2},{1,3},{2,0},{3,1},{4,6},{5,7},{6,4},{7,5},{8,10},{9,11},{10,... | collective-permute-start | bytes 1966088 | tf_op jit(solution)/shard_map/ppermute | solution.py:43
  638.9 16.9 %collective-permute-start.60 = (bf16[2,2,40,2048]{3,2,1,0:T(8,128)(2,1)}, bf16[2,2,40,2048]{3,2,1,0:T(8,128)(2,1)}, u32[]{:S(2)}, u32[]{:S(2)}) collective-permute-start(bf16[2,2,40,2048]{3,2,1,0:T(8,128)(2,1)} %pad_maximum_fusion.24), channel_id=1, source_target_pairs={{0,8},{1,9},{2,10},{3,11},{4,12},{5,13},{6,14},{7,15},{8,0},{9,1},... | collective-permute-start | bytes 1966088 | tf_op jit(solution)/shard_map/ppermute | solution.py:43
  641.5 19.4 %collective-permute-start.59 = (bf16[2,2,48,2048]{3,2,1,0:T(8,128)(2,1)}, bf16[2,2,48,2048]{3,2,1,0:T(8,128)(2,1)}, u32[]{:S(2)}, u32[]{:S(2)}) collective-permute-start(bf16[2,2,48,2048]{3,2,1,0:T(8,128)(2,1)} %pad_maximum_fusion.19), channel_id=1, source_target_pairs={{0,4},{1,5},{2,6},{3,7},{4,0},{5,1},{6,2},{7,3},{8,12},{9,13},{10,... | collective-permute-start | bytes 2359304 | tf_op jit(solution)/shard_map/ppermute | solution.py:43
  644.3 35.2 %collective-permute-start.72 = (bf16[16,64,768]{2,1,0:T(8,128)(2,1)}, bf16[16,64,768]{2,1,0:T(8,128)(2,1)S(1)}, u32[]{:S(2)}, u32[]{:S(2)}) collective-permute-start(bf16[16,64,768]{2,1,0:T(8,128)(2,1)} %dynamic-slice_bitcast_fusion.3), channel_id=1, source_target_pairs={{0,1},{1,0},{2,3},{3,2},{4,5},{5,4},{6,7},{7,6},{8,9},{9,8},{10,11... | collective-permute-start | bytes 4718600 | tf_op jit(solution)/shard_map/ppermute | solution.py:43
  670.6 36.7 %collective-permute-start.62 = (bf16[2,2,2,48,2048]{4,3,2,1,0:T(8,128)(2,1)S(1)}, bf16[2,2,2,48,2048]{4,3,2,1,0:T(8,128)(2,1)S(1)}, u32[]{:S(2)}, u32[]{:S(2)}) collective-permute-start(bf16[2,2,2,48,2048]{4,3,2,1,0:T(8,128)(2,1)S(1)} %bitcast.645), channel_id=1, source_target_pairs={{0,4},{1,5},{2,6},{3,7},{4,0},{5,1},{6,2},{7,3},{8,12},{9,13},{10,... | collective-permute-start | bytes 4718600 | tf_op jit(solution)/shard_map/ppermute | solution.py:43
  670.9 30.8 %collective-permute-start.63 = (bf16[2,2,2,40,2048]{4,3,2,1,0:T(8,128)(2,1)S(1)}, bf16[2,2,2,40,2048]{4,3,2,1,0:T(8,128)(2,1)S(1)}, u32[]{:S(2)}, u32[]{:S(2)}) collective-permute-start(bf16[2,2,2,40,2048]{4,3,2,1,0:T(8,128)(2,1)S(1)} %bitcast.648), channel_id=1, source_target_pairs={{0,8},{1,9},{2,10},{3,11},{4,12},{5,13},{6,14},{7,15},{8,0},{9,1},... | collective-permute-start | bytes 3932168 | tf_op jit(solution)/shard_map/ppermute | solution.py:43
  674.6 30.6 %collective-permute-start.64 = (bf16[2,2,2,40,2048]{4,3,2,1,0:T(8,128)(2,1)S(1)}, bf16[2,2,2,40,2048]{4,3,2,1,0:T(8,128)(2,1)S(1)}, u32[]{:S(2)}, u32[]{:S(2)}) collective-permute-start(bf16[2,2,2,40,2048]{4,3,2,1,0:T(8,128)(2,1)S(1)} %bitcast.647), channel_id=1, source_target_pairs={{0,2},{1,3},{2,0},{3,1},{4,6},{5,7},{6,4},{7,5},{8,10},{9,11},{10,... | collective-permute-start | bytes 3932168 | tf_op jit(solution)/shard_map/ppermute | solution.py:43
  679.5 37.0 %collective-permute-start.73 = (bf16[2,512,1536]{2,1,0:T(8,128)(2,1)S(1)}, bf16[2,512,1536]{2,1,0:T(8,128)(2,1)S(1)}, u32[]{:S(2)}, u32[]{:S(2)}) collective-permute-start(bf16[2,512,1536]{2,1,0:T(8,128)(2,1)S(1)} %copy-done.48), channel_id=1, source_target_pairs={{0,1},{1,0},{2,3},{3,2},{4,5},{5,4},{6,7},{7,6},{8,9},{9,8},{10,11... | collective-permute-start | bytes 9437192 | tf_op jit(solution)/shard_map/ppermute | solution.py:43
  709.0 48.9 %collective-permute-start.67 = (bf16[2,2,40,2048]{3,2,1,0:T(8,128)(2,1)}, bf16[2,2,40,2048]{3,2,1,0:T(8,128)(2,1)}, u32[]{:S(2)}, u32[]{:S(2)}) collective-permute-start(bf16[2,2,40,2048]{3,2,1,0:T(8,128)(2,1)} %get-tuple-element.455), channel_id=1, source_target_pairs={{0,8},{1,9},{2,10},{3,11},{4,12},{5,13},{6,14},{7,15},{8,0},{9,1},... | collective-permute-start | bytes 1966088 | tf_op jit(solution)/shard_map/ppermute | solution.py:43
  712.2 45.7 %collective-permute-start.66 = (bf16[2,2,40,2048]{3,2,1,0:T(8,128)(2,1)}, bf16[2,2,40,2048]{3,2,1,0:T(8,128)(2,1)}, u32[]{:S(2)}, u32[]{:S(2)}) collective-permute-start(bf16[2,2,40,2048]{3,2,1,0:T(8,128)(2,1)} %get-tuple-element.457), channel_id=1, source_target_pairs={{0,4},{1,5},{2,6},{3,7},{4,0},{5,1},{6,2},{7,3},{8,12},{9,13},{10,... | collective-permute-start | bytes 1966088 | tf_op jit(solution)/shard_map/ppermute | solution.py:43
  715.1 42.8 %collective-permute-start.65 = (bf16[2,2,48,2048]{3,2,1,0:T(8,128)(2,1)}, bf16[2,2,48,2048]{3,2,1,0:T(8,128)(2,1)}, u32[]{:S(2)}, u32[]{:S(2)}) collective-permute-start(bf16[2,2,48,2048]{3,2,1,0:T(8,128)(2,1)} %get-tuple-element.445), channel_id=1, source_target_pairs={{0,2},{1,3},{2,0},{3,1},{4,6},{5,7},{6,4},{7,5},{8,10},{9,11},{10,... | collective-permute-start | bytes 2359304 | tf_op jit(solution)/shard_map/ppermute | solution.py:43
  734.4 74.6 %collective-permute-start.78 = (bf16[512,1536]{1,0:T(8,128)(2,1)}, bf16[512,1536]{1,0:T(8,128)(2,1)}, u32[]{:S(2)}, u32[]{:S(2)}) collective-permute-start(bf16[512,1536]{1,0:T(8,128)(2,1)} %get-tuple-element.434), channel_id=1, source_target_pairs={{0,2},{1,3},{2,0},{3,1},{4,6},{5,7},{6,4},{7,5},{8,10},{9,11},{10,... | collective-permute-start | bytes 4718600 | tf_op jit(solution)/shard_map/ppermute | solution.py:43
  740.1 56.5 %collective-permute-start.74 = (bf16[2048,384]{1,0:T(8,128)(2,1)}, bf16[2048,384]{1,0:T(8,128)(2,1)}, u32[]{:S(2)}, u32[]{:S(2)}) collective-permute-start(bf16[2048,384]{1,0:T(8,128)(2,1)} %broadcast_select_fusion), channel_id=1, source_target_pairs={{0,1},{1,0},{2,3},{3,2},{4,5},{5,4},{6,7},{7,6},{8,9},{9,8},{10,11... | collective-permute-start | bytes 4718600 | tf_op jit(solution)/shard_map/ppermute | solution.py:43
  740.1 64.4 %all-to-all-start.4 = ((bf16[16,64,768]{2,1,0:T(8,128)(2,1)}), bf16[16,64,768]{2,1,0:T(8,128)(2,1)S(1)}, u32[]{:S(2)}, u32[]{:S(2)}) async-start(bf16[16,64,768]{2,1,0:T(8,128)(2,1)} %fusion.5), calls=%async_computation.4 | async-start | bytes 3145728 | tf_op jit(solution)/shard_map/all_to_all | solution.py:870
  763.4 32.5 %collective-permute-start.69 = (bf16[2,40,2048]{2,1,0:T(8,128)(2,1)S(1)}, bf16[2,40,2048]{2,1,0:T(8,128)(2,1)S(1)}, u32[]{:S(2)}, u32[]{:S(2)}) collective-permute-start(bf16[2,40,2048]{2,1,0:T(8,128)(2,1)S(1)} %get-tuple-element.495), channel_id=1, source_target_pairs={{0,2},{1,3},{2,0},{3,1},{4,6},{5,7},{6,4},{7,5},{8,10},{9,11},{10,... | collective-permute-start | bytes 983048 | tf_op jit(solution)/shard_map/ppermute | solution.py:43
  766.4 30.1 %collective-permute-start.68 = (bf16[2,48,2048]{2,1,0:T(8,128)(2,1)S(1)}, bf16[2,48,2048]{2,1,0:T(8,128)(2,1)S(1)}, u32[]{:S(2)}, u32[]{:S(2)}) collective-permute-start(bf16[2,48,2048]{2,1,0:T(8,128)(2,1)S(1)} %get-tuple-element.483), channel_id=1, source_target_pairs={{0,8},{1,9},{2,10},{3,11},{4,12},{5,13},{6,14},{7,15},{8,0},{9,1},... | collective-permute-start | bytes 1179656 | tf_op jit(solution)/shard_map/ppermute | solution.py:43
  773.3 35.3 %collective-permute-start.77 = (bf16[2,2,40,2048]{3,2,1,0:T(8,128)(2,1)}, bf16[2,2,40,2048]{3,2,1,0:T(8,128)(2,1)}, u32[]{:S(2)}, u32[]{:S(2)}) collective-permute-start(bf16[2,2,40,2048]{3,2,1,0:T(8,128)(2,1)} %bitcast.235), channel_id=1, source_target_pairs={{0,2},{1,3},{2,0},{3,1},{4,6},{5,7},{6,4},{7,5},{8,10},{9,11},{10,... | collective-permute-start | bytes 1966088 | tf_op jit(solution)/shard_map/ppermute | solution.py:43
  799.5 28.4 %collective-permute-start.75 = (bf16[2,2,48,2048]{3,2,1,0:T(8,128)(2,1)}, bf16[2,2,48,2048]{3,2,1,0:T(8,128)(2,1)}, u32[]{:S(2)}, u32[]{:S(2)}) collective-permute-start(bf16[2,2,48,2048]{3,2,1,0:T(8,128)(2,1)} %bitcast.233), channel_id=1, source_target_pairs={{0,4},{1,5},{2,6},{3,7},{4,0},{5,1},{6,2},{7,3},{8,12},{9,13},{10,... | collective-permute-start | bytes 2359304 | tf_op jit(solution)/shard_map/ppermute | solution.py:43
  804.5 42.3 %all-to-all-start.5 = ((bf16[32,64,384]{2,1,0:T(8,128)(2,1)}), bf16[32,64,384]{2,1,0:T(8,128)(2,1)S(1)}, u32[]{:S(2)}, u32[]{:S(2)}) async-start(bf16[32,64,384]{2,1,0:T(8,128)(2,1)} %bitcast.586), calls=%async_computation.5 | async-start | bytes 3145728 | tf_op jit(solution)/shard_map/all_to_all | solution.py:920
  857.8 16.0 %collective-permute-start.88 = (bf16[64,2048]{1,0:T(8,128)(2,1)S(1)}, bf16[64,2048]{1,0:T(8,128)(2,1)S(1)}, u32[]{:S(2)}, u32[]{:S(2)}) collective-permute-start(bf16[64,2048]{1,0:T(8,128)(2,1)S(1)} %get-tuple-element.505), channel_id=1, source_target_pairs={{0,0},{1,1},{16,2},{17,3},{2,4},{3,5},{18,6},{19,7},{4,8},{5,9},{2... | collective-permute-start | bytes 786440 | tf_op jit(solution)/shard_map/ppermute | solution.py:43
  858.5 33.8 %collective-permute-start.89 = (bf16[64,2048]{1,0:T(8,128)(2,1)S(1)}, bf16[64,2048]{1,0:T(8,128)(2,1)S(1)}, u32[]{:S(2)}, u32[]{:S(2)}) collective-permute-start(bf16[64,2048]{1,0:T(8,128)(2,1)S(1)} %get-tuple-element.506), channel_id=1, source_target_pairs={{16,0},{17,1},{0,2},{1,3},{18,4},{19,5},{2,6},{3,7},{20,8},{21,9},... | collective-permute-start | bytes 786440 | tf_op jit(solution)/shard_map/ppermute | solution.py:43
  862.9 49.8 %collective-permute-start.71 = (bf16[128,2048]{1,0:T(8,128)(2,1)}, bf16[128,2048]{1,0:T(8,128)(2,1)}, u32[]{:S(2)}, u32[]{:S(2)}) collective-permute-start(bf16[128,2048]{1,0:T(8,128)(2,1)} %slice_bitcast_fusion.12), channel_id=1, source_target_pairs={{0,16},{1,17},{2,18},{3,19},{4,20},{5,21},{6,22},{7,23},{8,24},{9,... | collective-permute-start | bytes 1572872 | tf_op jit(solution)/shard_map/ppermute | solution.py:43
  871.7 34.5 %collective-permute-start.86 = (bf16[2,4,8,2048]{3,2,1,0:T(8,128)(2,1)S(1)}, bf16[2,4,8,2048]{3,2,1,0:T(8,128)(2,1)S(1)}, u32[]{:S(2)}, u32[]{:S(2)}) collective-permute-start(bf16[2,4,8,2048]{3,2,1,0:T(8,128)(2,1)S(1)} %get-tuple-element.514), channel_id=1, source_target_pairs={{0,16},{1,17},{2,18},{3,19},{4,20},{5,21},{6,22},{7,23},{8,24},{9,... | collective-permute-start | bytes 786440 | tf_op jit(solution)/shard_map/ppermute | solution.py:43
  (196 other events, 1341.2 us)
Sparse Core Ops, SparseCore 0:
  136.1 158.4 all-gather.2
